TPU v7x, 32 devices: a whole 2x2x4 slice. The times are simulated.
32 devices in a mesh: dp: 4 (over x, core), fsdp: 8 (over z, y).
Axes of the slice: x: 2, y: 2, z: 4, core: 2. Of those that a mesh axis runs over, the one named last changes fastest.
Arguments:
- tokens_in: bfloat16 [2, 64, 384, 768], P(None, 'dp', 'fsdp'), may hold values from -6 to 6
- cotangent: bfloat16 [2, 64, 384, 768], P(None, 'dp', 'fsdp'), may hold values from -6 to 6
- lengths: int32 [2, 64], replicated, may hold values from 1 to 5, as said below
- bin_deal: int32 [2, 4, 16], replicated, may hold values from 0 to 15, as said below
- random_blocks: int32 [2, 64, 6, 3], replicated, may hold values from 0 to 5
- weight_qkv: bfloat16 [2, 768, 2304], P(None, ('dp', 'fsdp')), may hold values from -0.21875 to 0.21875
- bias_query: bfloat16 [2, 768], P(None, ('dp', 'fsdp')), may hold values from -2 to 2
- bias_value: bfloat16 [2, 768], P(None, ('dp', 'fsdp')), may hold values from -2 to 2
- weight_out: bfloat16 [2, 768, 768], P(None, ('dp', 'fsdp')), may hold values from -0.625 to 0.625
- bias_out: bfloat16 [2, 768], P(None, ('dp', 'fsdp')), may hold values from -2 to 2
- gain_attn: bfloat16 [2, 768], P(None, ('dp', 'fsdp')), may hold values from 0.5 to 1.5
- beta_attn: bfloat16 [2, 768], P(None, ('dp', 'fsdp')), may hold values from -2 to 2
- weight_up: bfloat16 [2, 768, 3072], P(None, ('dp', 'fsdp')), may hold values from -0.21875 to 0.21875
- bias_up: bfloat16 [2, 3072], P(None, ('dp', 'fsdp')), may hold values from -2 to 2
- weight_down: bfloat16 [2, 3072, 768], P(None, ('dp', 'fsdp')), may hold values from -0.109375 to 0.109375
- bias_down: bfloat16 [2, 768], P(None, ('dp', 'fsdp')), may hold values from -2 to 2
- gain_ffn: bfloat16 [2, 768], P(None, ('dp', 'fsdp')), may hold values from 0.5 to 1.5
- beta_ffn: bfloat16 [2, 768], P(None, ('dp', 'fsdp')), may hold values from -2 to 2
Outputs:
- output: bfloat16 [2, 64, 384, 768], P(None, 'dp', 'fsdp')
- input_grad: bfloat16 [2, 64, 384, 768], P(None, 'dp', 'fsdp')
- grad_weight_qkv: float32 [2, 768, 2304], P(None, ('dp', 'fsdp'))
- grad_bias_query: float32 [2, 768], P(None, ('dp', 'fsdp'))
- grad_bias_value: float32 [2, 768], P(None, ('dp', 'fsdp'))
- grad_weight_out: float32 [2, 768, 768], P(None, ('dp', 'fsdp'))
- grad_bias_out: float32 [2, 768], P(None, ('dp', 'fsdp'))
- grad_gain_attn: float32 [2, 768], P(None, ('dp', 'fsdp'))
- grad_beta_attn: float32 [2, 768], P(None, ('dp', 'fsdp'))
- grad_weight_up: float32 [2, 768, 3072], P(None, ('dp', 'fsdp'))
- grad_bias_up: float32 [2, 3072], P(None, ('dp', 'fsdp'))
- grad_weight_down: float32 [2, 3072, 768], P(None, ('dp', 'fsdp'))
- grad_bias_down: float32 [2, 768], P(None, ('dp', 'fsdp'))
- grad_gain_ffn: float32 [2, 768], P(None, ('dp', 'fsdp'))
- grad_beta_ffn: float32 [2, 768], P(None, ('dp', 'fsdp'))
Inputs may be any that keep to these rules, and one draw needn't show every extreme that they name: lengths are counted in blocks of 64 positions; the two sequences dealt to one bin have 6 blocks or fewer together, and in every group of every micro-batch some bin holds exactly 6. For each micro-batch m and group g, bin_deal[m, g] names each of 0 to 15 once.
All inputs are finite; a program needn't handle non-finite values.
Results may differ from a plain program's by a relative error of at most 0.02.
Values may be sent and summed in bfloat16 or wider, within the bound.
A program may use at most 320 MiB of HBM per device.

v0:
```python
import jax
import jax.numpy as jnp
from jax import lax
from jax.sharding import PartitionSpec as P

HEADS = 12
BLOCK = 64
NBLK = 6
LAYERS = 2


epsilon = 1e-06


def bin_mask(first_blocks, second_blocks, random_pair):
    block_ids = jnp.arange(NBLK)
    later_seg = block_ids >= first_blocks
    rel_block = jnp.where(later_seg, block_ids - first_blocks, block_ids)
    seg_len = jnp.where(later_seg, second_blocks, first_blocks)
    live_block = block_ids < first_blocks + second_blocks
    rand_rows = jnp.where(
        later_seg[:, None],
        jnp.take(random_pair[1], rel_block, axis=0),
        jnp.take(random_pair[0], rel_block, axis=0),
    )
    picked = jnp.remainder(rand_rows, seg_len[:, None])
    row_rel = rel_block[:, None]
    col_rel = rel_block[None, :]
    row_len = seg_len[:, None]
    nearby = jnp.abs(row_rel - col_rel) <= 1
    global_hit = (
        (col_rel == 0) | (col_rel == row_len - 1) | (row_rel == 0) | (row_rel == row_len - 1)
    )
    random_hit = jnp.any(picked[:, :, None] == rel_block[None, None, :], axis=1)
    same_seg = (
        (later_seg[:, None] == later_seg[None, :]) & live_block[:, None] & live_block[None, :]
    )
    allowed = (nearby | global_hit | random_hit) & same_seg
    return jnp.repeat(jnp.repeat(allowed, BLOCK, axis=0), BLOCK, axis=1)


def layer_norm(residual):
    center = residual - jnp.mean(residual, axis=-1, keepdims=True)
    inv_std = lax.rsqrt(jnp.mean(center * center, axis=-1, keepdims=True) + epsilon)
    return (center * inv_std, inv_std)


def norm_back(grad_out, normed, inv_std, gain):
    scaled = grad_out * gain
    return inv_std * (
        scaled
        - jnp.mean(scaled, axis=-1, keepdims=True)
        - normed * jnp.mean(scaled * normed, axis=-1, keepdims=True)
    )


def gelu_tanh(values_in):
    return jax.nn.gelu(values_in, approximate=True)


def as_float(vector):
    return vector.astype(jnp.float32)


def layer_forward(hidden, params, layer_at, allowed):
    (
        weight_qkv,
        bias_query,
        bias_value,
        weight_out,
        bias_out,
        gain_attn,
        beta_attn,
        weight_up,
        bias_up,
        weight_down,
        bias_down,
        gain_ffn,
        beta_ffn,
    ) = params
    seq_len, model_width = hidden.shape
    head_dim = model_width // HEADS
    score_scale = head_dim ** (-0.5)
    act_in = hidden.astype(jnp.bfloat16)
    qkv_raw = jnp.dot(act_in, weight_qkv[layer_at], preferred_element_type=jnp.float32)
    queries = (
        (qkv_raw[:, :model_width] + as_float(bias_query[layer_at]))
        .astype(jnp.bfloat16)
        .reshape(seq_len, HEADS, head_dim)
    )
    key_rows = (
        qkv_raw[:, model_width : 2 * model_width]
        .astype(jnp.bfloat16)
        .reshape(seq_len, HEADS, head_dim)
    )
    value_rows = (
        (qkv_raw[:, 2 * model_width :] + as_float(bias_value[layer_at]))
        .astype(jnp.bfloat16)
        .reshape(seq_len, HEADS, head_dim)
    )
    scores = (
        jnp.einsum("qhd,khd->hqk", queries, key_rows, preferred_element_type=jnp.float32)
        * score_scale
    )
    scores = jnp.where(allowed[None], scores, -1000000000.0)
    top_score = jnp.max(scores, axis=-1, keepdims=True)
    exp_scores = jnp.exp(scores - top_score)
    exp_total = jnp.sum(exp_scores, axis=-1, keepdims=True)
    soft_weights = exp_scores / exp_total
    log_total = top_score + jnp.log(exp_total)
    mixed_rows = jnp.einsum(
        "hqk,khd->qhd",
        soft_weights.astype(jnp.bfloat16),
        value_rows,
        preferred_element_type=jnp.float32,
    )
    context = mixed_rows.reshape(seq_len, model_width).astype(jnp.bfloat16)
    attn_out = jnp.dot(
        context, weight_out[layer_at], preferred_element_type=jnp.float32
    ) + as_float(bias_out[layer_at])
    normed_a, inv_a = layer_norm(hidden + attn_out)
    middle = normed_a * as_float(gain_attn[layer_at]) + as_float(beta_attn[layer_at])
    act_mid = middle.astype(jnp.bfloat16)
    up_pre = jnp.dot(act_mid, weight_up[layer_at], preferred_element_type=jnp.float32) + as_float(
        bias_up[layer_at]
    )
    act_up = gelu_tanh(up_pre).astype(jnp.bfloat16)
    down_out = jnp.dot(
        act_up, weight_down[layer_at], preferred_element_type=jnp.float32
    ) + as_float(bias_down[layer_at])
    normed_f, inv_f = layer_norm(middle + down_out)
    result = normed_f * as_float(gain_ffn[layer_at]) + as_float(beta_ffn[layer_at])
    stored = (
        act_in,
        queries,
        key_rows,
        value_rows,
        log_total,
        context,
        normed_a,
        inv_a,
        act_mid,
        up_pre,
        act_up,
        normed_f,
        inv_f,
    )
    return (result, stored)


def layer_backward(grad_out, stored, params, layer_at, allowed):
    (
        act_in,
        queries,
        key_rows,
        value_rows,
        log_total,
        context,
        normed_a,
        inv_a,
        act_mid,
        up_pre,
        act_up,
        normed_f,
        inv_f,
    ) = stored
    (
        weight_qkv,
        bias_query,
        bias_value,
        weight_out,
        bias_out,
        gain_attn,
        beta_attn,
        weight_up,
        bias_up,
        weight_down,
        bias_down,
        gain_ffn,
        beta_ffn,
    ) = params
    seq_len, model_width = context.shape
    head_dim = model_width // HEADS
    score_scale = head_dim ** (-0.5)
    grad_gain_ffn = jnp.sum(grad_out * normed_f, axis=0)
    grad_beta_ffn = jnp.sum(grad_out, axis=0)
    grad_resid_f = norm_back(grad_out, normed_f, inv_f, as_float(gain_ffn[layer_at]))
    grad_bias_down = jnp.sum(grad_resid_f, axis=0)
    down_low = grad_resid_f.astype(jnp.bfloat16)
    grad_weight_down = jnp.einsum("sf,sd->fd", act_up, down_low, preferred_element_type=jnp.float32)
    grad_act = jnp.einsum(
        "sd,fd->sf", down_low, weight_down[layer_at], preferred_element_type=jnp.float32
    )
    unused, gelu_pull = jax.vjp(gelu_tanh, up_pre)
    grad_up = gelu_pull(grad_act)[0]
    grad_bias_up = jnp.sum(grad_up, axis=0)
    up_low = grad_up.astype(jnp.bfloat16)
    grad_weight_up = jnp.einsum("sd,sf->df", act_mid, up_low, preferred_element_type=jnp.float32)
    grad_middle = grad_resid_f + jnp.einsum(
        "sf,df->sd", up_low, weight_up[layer_at], preferred_element_type=jnp.float32
    )
    grad_gain_attn = jnp.sum(grad_middle * normed_a, axis=0)
    grad_beta_attn = jnp.sum(grad_middle, axis=0)
    grad_resid_a = norm_back(grad_middle, normed_a, inv_a, as_float(gain_attn[layer_at]))
    grad_bias_out = jnp.sum(grad_resid_a, axis=0)
    attn_low = grad_resid_a.astype(jnp.bfloat16)
    grad_weight_out = jnp.einsum("so,sd->od", context, attn_low, preferred_element_type=jnp.float32)
    grad_context = jnp.einsum(
        "sd,od->so", attn_low, weight_out[layer_at], preferred_element_type=jnp.float32
    )
    grad_context = grad_context.astype(jnp.bfloat16).reshape(seq_len, HEADS, head_dim)
    scores = (
        jnp.einsum("qhd,khd->hqk", queries, key_rows, preferred_element_type=jnp.float32)
        * score_scale
    )
    scores = jnp.where(allowed[None], scores, -1000000000.0)
    soft_weights = jnp.exp(scores - log_total)
    grad_soft = jnp.einsum(
        "qhd,khd->hqk", grad_context, value_rows, preferred_element_type=jnp.float32
    )
    grad_values = jnp.einsum(
        "hqk,qhd->khd",
        soft_weights.astype(jnp.bfloat16),
        grad_context,
        preferred_element_type=jnp.float32,
    )
    inner_sum = jnp.sum(grad_soft * soft_weights, axis=-1, keepdims=True)
    grad_scores = (soft_weights * (grad_soft - inner_sum)).astype(jnp.bfloat16)
    grad_queries = (
        jnp.einsum("hqk,khd->qhd", grad_scores, key_rows, preferred_element_type=jnp.float32)
        * score_scale
    )
    grad_keys = (
        jnp.einsum("hqk,qhd->khd", grad_scores, queries, preferred_element_type=jnp.float32)
        * score_scale
    )
    grad_queries = grad_queries.reshape(seq_len, model_width)
    grad_keys = grad_keys.reshape(seq_len, model_width)
    grad_values = grad_values.reshape(seq_len, model_width)
    grad_bias_query = jnp.sum(grad_queries, axis=0)
    grad_bias_value = jnp.sum(grad_values, axis=0)
    grad_qkv = jnp.concatenate([grad_queries, grad_keys, grad_values], axis=1).astype(jnp.bfloat16)
    grad_weight_qkv = jnp.einsum("sd,se->de", act_in, grad_qkv, preferred_element_type=jnp.float32)
    grad_input = grad_resid_a + jnp.einsum(
        "se,de->sd", grad_qkv, weight_qkv[layer_at], preferred_element_type=jnp.float32
    )
    layer_grads_out = (
        grad_weight_qkv,
        grad_bias_query,
        grad_bias_value,
        grad_weight_out,
        grad_bias_out,
        grad_gain_attn,
        grad_beta_attn,
        grad_weight_up,
        grad_bias_up,
        grad_weight_down,
        grad_bias_down,
        grad_gain_ffn,
        grad_beta_ffn,
    )
    return (grad_input, layer_grads_out)


def unpack_bin(bin_rows, first_len, second_len, positions, bin_len):
    first_slot = jnp.where((positions < first_len)[:, None], bin_rows, 0)
    later_index = jnp.minimum(positions + first_len, bin_len - 1)
    second_slot = jnp.where(
        (positions < second_len)[:, None], jnp.take(bin_rows, later_index, axis=0), 0
    )
    return jnp.stack([first_slot, second_slot])


def per_device(
    tokens_in,
    cotangent,
    lengths,
    bin_deal,
    random_blocks,
    weight_qkv,
    bias_query,
    bias_value,
    weight_out,
    bias_out,
    gain_attn,
    beta_attn,
    weight_up,
    bias_up,
    weight_down,
    bias_down,
    gain_ffn,
    beta_ffn,
):
    members = lax.axis_size("fsdp")
    member = lax.axis_index("fsdp")
    group_at = lax.axis_index("dp")
    slot_count = 2 * members
    slot_ids = jnp.arange(slot_count)
    deal_here = lax.dynamic_index_in_dim(bin_deal, group_at, 1, keepdims=False)
    slot_hits = (deal_here[:, :, None] == slot_ids[None, None, :]).astype(jnp.int32)
    source_of = jnp.sum(slot_hits * slot_ids[None, :, None], axis=1)
    lengths_here = lax.dynamic_slice_in_dim(lengths, group_at * slot_count, slot_count, 1)
    bin_lengths = jnp.take_along_axis(lengths_here, source_of, axis=1)
    random_here = lax.dynamic_slice_in_dim(random_blocks, group_at * slot_count, slot_count, 1)
    batch_count, unused_slots, rows_dev, model_width = tokens_in.shape
    bin_len = rows_dev * members
    order_index = source_of[:, :, None, None]
    sent_x = jnp.take_along_axis(tokens_in, order_index, axis=1).reshape(
        batch_count, members, 2, rows_dev, model_width
    )
    sent_grad = jnp.take_along_axis(cotangent, order_index, axis=1).reshape(
        batch_count, members, 2, rows_dev, model_width
    )
    arrived_x, arrived_grad = (
        lax.all_to_all(sent_x, "fsdp", split_axis=1, concat_axis=3, tiled=True),
        lax.all_to_all(sent_grad, "fsdp", split_axis=1, concat_axis=3, tiled=True),
    )
    positions = jnp.arange(bin_len)
    totals = None
    out_slots = []
    grad_slots = []
    for batch_at in range(batch_count):
        params = (
            lax.all_gather(weight_qkv, ("dp", "fsdp"), axis=1, tiled=True),
            lax.all_gather(bias_query, ("dp", "fsdp"), axis=1, tiled=True),
            lax.all_gather(bias_value, ("dp", "fsdp"), axis=1, tiled=True),
            lax.all_gather(weight_out, ("dp", "fsdp"), axis=1, tiled=True),
            lax.all_gather(bias_out, ("dp", "fsdp"), axis=1, tiled=True),
            lax.all_gather(gain_attn, ("dp", "fsdp"), axis=1, tiled=True),
            lax.all_gather(beta_attn, ("dp", "fsdp"), axis=1, tiled=True),
            lax.all_gather(weight_up, ("dp", "fsdp"), axis=1, tiled=True),
            lax.all_gather(bias_up, ("dp", "fsdp"), axis=1, tiled=True),
            lax.all_gather(weight_down, ("dp", "fsdp"), axis=1, tiled=True),
            lax.all_gather(bias_down, ("dp", "fsdp"), axis=1, tiled=True),
            lax.all_gather(gain_ffn, ("dp", "fsdp"), axis=1, tiled=True),
            lax.all_gather(beta_ffn, ("dp", "fsdp"), axis=1, tiled=True),
        )
        slot_pair = lax.dynamic_slice_in_dim(bin_lengths[batch_at], 2 * member, 2)
        first_blocks = slot_pair[0]
        second_blocks = slot_pair[1]
        random_pair = lax.dynamic_slice_in_dim(random_here[batch_at], 2 * member, 2, 0)
        allowed = bin_mask(first_blocks, second_blocks, random_pair)
        first_len = first_blocks * BLOCK
        second_len = second_blocks * BLOCK
        live_mask = positions < first_len + second_len
        row_source = jnp.where(positions < first_len, positions, bin_len + positions - first_len)
        row_source = jnp.where(live_mask, row_source, 0)
        live_rows = live_mask.astype(jnp.float32)[:, None]
        both_x = arrived_x[batch_at, 0].reshape(2 * bin_len, model_width)
        both_grad = arrived_grad[batch_at, 0].reshape(2 * bin_len, model_width)
        hidden = jnp.take(both_x, row_source, axis=0).astype(jnp.float32) * live_rows
        kept_all = []
        for layer_at in range(LAYERS):
            hidden, stored = layer_forward(hidden, params, layer_at, allowed)
            kept_all.append(stored)
        out_bin = (hidden * live_rows).astype(jnp.bfloat16)
        out_slots.append(unpack_bin(out_bin, first_len, second_len, positions, bin_len))
        grad_hidden = jnp.take(both_grad, row_source, axis=0).astype(jnp.float32) * live_rows
        layer_grads = [None] * LAYERS
        for layer_at in reversed(range(LAYERS)):
            grad_hidden, layer_grads[layer_at] = layer_backward(
                grad_hidden, kept_all[layer_at], params, layer_at, allowed
            )
        grad_bin = grad_hidden.astype(jnp.bfloat16)
        grad_slots.append(unpack_bin(grad_bin, first_len, second_len, positions, bin_len))
        stacked = tuple(
            (
                jnp.stack([layer_grads[layer_at][member_at] for layer_at in range(LAYERS)])
                for member_at in range(13)
            )
        )
        if totals is None:
            totals = tuple(stacked)
        else:
            totals = tuple((earlier + later for earlier, later in zip(totals, stacked)))
    back_out = jnp.stack(out_slots)[:, None]
    back_grad = jnp.stack(grad_slots)[:, None]
    returned_out, returned_grad = (
        lax.all_to_all(back_out, "fsdp", split_axis=3, concat_axis=1, tiled=True),
        lax.all_to_all(back_grad, "fsdp", split_axis=3, concat_axis=1, tiled=True),
    )
    flat_out = returned_out.reshape(batch_count, slot_count, rows_dev, model_width)
    flat_grad = returned_grad.reshape(batch_count, slot_count, rows_dev, model_width)
    deal_index = deal_here[:, :, None, None]
    output = jnp.take_along_axis(flat_out, deal_index, axis=1)
    input_grad = jnp.take_along_axis(flat_grad, deal_index, axis=1)
    summed = (
        lax.psum_scatter(totals[0], ("dp", "fsdp"), scatter_dimension=1, tiled=True),
        lax.psum_scatter(totals[1], ("dp", "fsdp"), scatter_dimension=1, tiled=True),
        lax.psum_scatter(totals[2], ("dp", "fsdp"), scatter_dimension=1, tiled=True),
        lax.psum_scatter(totals[3], ("dp", "fsdp"), scatter_dimension=1, tiled=True),
        lax.psum_scatter(totals[4], ("dp", "fsdp"), scatter_dimension=1, tiled=True),
        lax.psum_scatter(totals[5], ("dp", "fsdp"), scatter_dimension=1, tiled=True),
        lax.psum_scatter(totals[6], ("dp", "fsdp"), scatter_dimension=1, tiled=True),
        lax.psum_scatter(totals[7], ("dp", "fsdp"), scatter_dimension=1, tiled=True),
        lax.psum_scatter(totals[8], ("dp", "fsdp"), scatter_dimension=1, tiled=True),
        lax.psum_scatter(totals[9], ("dp", "fsdp"), scatter_dimension=1, tiled=True),
        lax.psum_scatter(totals[10], ("dp", "fsdp"), scatter_dimension=1, tiled=True),
        lax.psum_scatter(totals[11], ("dp", "fsdp"), scatter_dimension=1, tiled=True),
        lax.psum_scatter(totals[12], ("dp", "fsdp"), scatter_dimension=1, tiled=True),
    )
    return (output, input_grad) + tuple(summed)


def solution(mesh):
    placed = (
        P(None, "dp", "fsdp", None),
        P(None, "dp", "fsdp", None),
        P(),
        P(),
        P(),
        P(None, ("dp", "fsdp"), None),
        P(None, ("dp", "fsdp")),
        P(None, ("dp", "fsdp")),
        P(None, ("dp", "fsdp"), None),
        P(None, ("dp", "fsdp")),
        P(None, ("dp", "fsdp")),
        P(None, ("dp", "fsdp")),
        P(None, ("dp", "fsdp"), None),
        P(None, ("dp", "fsdp")),
        P(None, ("dp", "fsdp"), None),
        P(None, ("dp", "fsdp")),
        P(None, ("dp", "fsdp")),
        P(None, ("dp", "fsdp")),
    )
    return jax.shard_map(
        per_device,
        mesh=mesh,
        in_specs=placed,
        out_specs=(
            P(None, "dp", "fsdp", None),
            P(None, "dp", "fsdp", None),
            P(None, ("dp", "fsdp"), None),
            P(None, ("dp", "fsdp")),
            P(None, ("dp", "fsdp")),
            P(None, ("dp", "fsdp"), None),
            P(None, ("dp", "fsdp")),
            P(None, ("dp", "fsdp")),
            P(None, ("dp", "fsdp")),
            P(None, ("dp", "fsdp"), None),
            P(None, ("dp", "fsdp")),
            P(None, ("dp", "fsdp"), None),
            P(None, ("dp", "fsdp")),
            P(None, ("dp", "fsdp")),
            P(None, ("dp", "fsdp")),
        ),
        check_vma=False,
    )
```

profile of v0, /device:TPU:0, one launch (start us, length us, event | category | flops | bytes accessed | tf_op | source)
XLA Modules:
  0.0 1869.7 jit_solution(17434660651088488173)
XLA Ops:
  22.7 7.5 all-to-all-start
  37.6 112.7 %all-gather.2 = bf16[32,24,2]{1,2,0:T(2,128)(2,1)S(1)} all-gather(bf16[1,24,2]{1,2,0:T(2,128)(2,1)S(1)} %bitcast.577), channel_id=1, replica_groups=mesh['dp'=4,'fsdp'=8] {'dp','fsdp'}, dimensions={0}, use_global_device_ids=true | all-gather | bytes 3168 | tf_op jit(solution)/shard_map/all_gather | solution.py:328
  150.5 64.4 %all-gather.1 = bf16[32,24,2]{1,2,0:T(2,128)(2,1)S(1)} all-gather(bf16[1,24,2]{1,2,0:T(2,128)(2,1)S(1)} %bitcast.578), channel_id=1, replica_groups=mesh['dp'=4,'fsdp'=8] {'dp','fsdp'}, dimensions={0}, use_global_device_ids=true | all-gather | bytes 3168 | tf_op jit(solution)/shard_map/all_gather | solution.py:325
  215.0 65.9 %all-gather = bf16[32,24,2]{1,2,0:T(2,128)(2,1)S(1)} all-gather(bf16[1,24,2]{1,2,0:T(2,128)(2,1)S(1)} %bitcast.579), channel_id=1, replica_groups=mesh['dp'=4,'fsdp'=8] {'dp','fsdp'}, dimensions={0}, use_global_device_ids=true | all-gather | bytes 3168 | tf_op jit(solution)/shard_map/all_gather | solution.py:326
  303.1 131.9 %all-gather.4 = bf16[32,24,2]{1,2,0:T(2,128)(2,1)S(1)} all-gather(bf16[1,24,2]{1,2,0:T(2,128)(2,1)S(1)} %bitcast.580), channel_id=1, replica_groups=mesh['dp'=4,'fsdp'=8] {'dp','fsdp'}, dimensions={0}, use_global_device_ids=true | all-gather | bytes 3168 | tf_op jit(solution)/shard_map/all_gather | solution.py:330
  435.1 63.4 %all-gather.3 = bf16[32,24,2]{1,2,0:T(2,128)(2,1)S(1)} all-gather(bf16[1,24,2]{1,2,0:T(2,128)(2,1)S(1)} %bitcast.581), channel_id=1, replica_groups=mesh['dp'=4,'fsdp'=8] {'dp','fsdp'}, dimensions={0}, use_global_device_ids=true | all-gather | bytes 3168 | tf_op jit(solution)/shard_map/all_gather | solution.py:329
  498.7 65.6 %all-gather.6 = bf16[32,24,2]{1,2,0:T(2,128)(2,1)S(1)} all-gather(bf16[1,24,2]{1,2,0:T(2,128)(2,1)S(1)} %bitcast.582), channel_id=1, replica_groups=mesh['dp'=4,'fsdp'=8] {'dp','fsdp'}, dimensions={0}, use_global_device_ids=true | all-gather | bytes 3168 | tf_op jit(solution)/shard_map/all_gather | solution.py:334
  564.4 63.4 %all-gather.5 = bf16[32,96,2]{1,2,0:T(2,128)(2,1)S(1)} all-gather(bf16[1,96,2]{1,2,0:T(2,128)(2,1)S(1)} %bitcast.583), channel_id=1, replica_groups=mesh['dp'=4,'fsdp'=8] {'dp','fsdp'}, dimensions={0}, use_global_device_ids=true | all-gather | bytes 12672 | tf_op jit(solution)/shard_map/all_gather | solution.py:332
  627.9 65.6 %all-gather.8 = bf16[32,24,2]{1,2,0:T(2,128)(2,1)S(1)} all-gather(bf16[1,24,2]{1,2,0:T(2,128)(2,1)S(1)} %bitcast.584), channel_id=1, replica_groups=mesh['dp'=4,'fsdp'=8] {'dp','fsdp'}, dimensions={0}, use_global_device_ids=true | all-gather | bytes 3168 | tf_op jit(solution)/shard_map/all_gather | solution.py:336
  693.7 63.4 %all-gather.7 = bf16[32,24,2]{1,2,0:T(2,128)(2,1)S(1)} all-gather(bf16[1,24,2]{1,2,0:T(2,128)(2,1)S(1)} %bitcast.585), channel_id=1, replica_groups=mesh['dp'=4,'fsdp'=8] {'dp','fsdp'}, dimensions={0}, use_global_device_ids=true | all-gather | bytes 3168 | tf_op jit(solution)/shard_map/all_gather | solution.py:335
  819.1 6.9 fusion.247
  878.0 7.1 fusion.253
  887.4 7.3 fusion.254
  898.8 7.7 fusion.256
  918.8 7.3 multiply_reduce_fusion.3
  971.3 7.7 fusion.255
  1009.3 7.6 multiply_reduce_fusion
  1084.4 11.4 maximum_add_fusion
  1117.9 11.6 maximum_add_fusion.1
  1169.0 63.2 %all-to-all-done.3 = bf16[2,1,2,384,768]{4,2,0,1,3:T(2,128)(2,1)S(1)} async-done(((bf16[2,1,2,384,768]{4,2,0,1,3:T(2,128)(2,1)}), bf16[2,1,2,384,768]{4,2,0,1,3:T(2,128)(2,1)S(1)}, u32[]{:S(2)}, u32[]{:S(2)}) %all-to-all-start.3) | async-done | bytes 2359328 | tf_op jit(solution)/shard_map/all_to_all | solution.py:380
  1238.0 75.6 %all-reduce.8 = (f32[2,768]{1,0:T(2,128)S(1)}, f32[2,768]{1,0:T(2,128)S(1)}, f32[2,768]{1,0:T(2,128)S(1)}, f32[2,768]{1,0:T(2,128)S(1)}, f32[2,768]{1,0:T(2,128)...) all-reduce(f32[2,768]{1,0:T(2,128)S(1)} %maximum_add_fusion.5, ...), channel_id=3, replica_groups=mesh['dp'=4,'fsdp'=8] {'dp','fsdp'}, use_global_device_ids=true, to_apply=%region_52.58.clone | all-reduce | flops 12288 | bytes 98304
  1335.8 104.9 %reduce-scatter.16.cloned.1.call-done = f32[2,24,2304]{2,1,0:T(8,128)} async-done(((f32[2,768,2304]{2,1,0:T(8,128)}), f32[2,24,2304]{2,1,0:T(8,128)}) %reduce-scatter.16.cloned.1.call-update) | async-done | bytes 442384 | tf_op jit(solution)/shard_map/reduce_scatter | solution.py:388
  1440.7 210.9 %reduce-scatter.20.cloned.1.call-done = f32[2,24,3072]{2,1,0:T(8,128)} async-done(((f32[2,768,3072]{2,1,0:T(8,128)}), f32[2,24,3072]{2,1,0:T(8,128)}) %reduce-scatter.20.cloned.1.call-update) | async-done | bytes 589840 | tf_op jit(solution)/shard_map/reduce_scatter | solution.py:395
  1651.6 211.3 %reduce-scatter.22.cloned.1.call-done = f32[2,96,768]{2,1,0:T(8,128)} async-done(((f32[2,3072,768]{2,1,0:T(8,128)}), f32[2,96,768]{2,1,0:T(8,128)}) %reduce-scatter.22.cloned.1.call-update) | async-done | bytes 589840 | tf_op jit(solution)/shard_map/reduce_scatter | solution.py:397
  (1023 shorter events, 401.4 us)
Async XLA Ops:
  7.2 776.5 %all-gather.14.cloned.1.call-start = ((), (), s32[]{:S(2)}) async-start(), calls=%async_computation.9 | async-start | bytes 7299072 | tf_op jit(solution)/shard_map/all_gather | solution.py:324
  7.9 793.0 %all-gather.16.cloned.1.call-start = ((), (), s32[]{:S(2)}) async-start(), calls=%async_computation.10 | async-start | bytes 2433024 | tf_op jit(solution)/shard_map/all_gather | solution.py:327
  8.7 803.8 %all-gather.18.cloned.1.call-start = ((), (), s32[]{:S(2)}) async-start(), calls=%async_computation.11 | async-start | bytes 9732096 | tf_op jit(solution)/shard_map/all_gather | solution.py:331
  9.4 809.6 %all-gather.20.cloned.1.call-start = ((), (), s32[]{:S(2)}) async-start(), calls=%async_computation.12 | async-start | bytes 9732096 | tf_op jit(solution)/shard_map/all_gather | solution.py:333
  22.6 127.8 %copy-start.276 = (bf16[2,24]{1,0:T(2,128)(2,1)S(1)}, bf16[2,24]{1,0:T(2,128)(2,1)}, u32[]{:S(2)}) copy-start(bf16[2,24]{1,0:T(2,128)(2,1)} %param.34) | copy-start | bytes 292
  22.6 192.4 %copy-start.277 = (bf16[2,24]{1,0:T(2,128)(2,1)S(1)}, bf16[2,24]{1,0:T(2,128)(2,1)}, u32[]{:S(2)}) copy-start(bf16[2,24]{1,0:T(2,128)(2,1)} %param.35) | copy-start | bytes 292
  22.6 258.4 %copy-start.156 = (s32[2,64,6,3]{1,0,3,2:T(2,128)S(1)}, s32[2,64,6,3]{1,0,3,2:T(2,128)}, u32[]{:S(2)}) copy-start(s32[2,64,6,3]{1,0,3,2:T(2,128)} %param.32) | copy-start | bytes 27652
  22.7 271.3 %all-to-all-start = ((bf16[2,8,2,48,768]{4,3,2,0,1:T(8,128)(2,1)}), bf16[2,8,2,48,768]{4,3,2,0,1:T(8,128)(2,1)S(1)}, u32[]{:S(2)}, u32[]{:S(2)}) async-start(bf16[2,8,2,48,768]{4,3,2,0,1:T(8,128)(2,1)} %copy.262), calls=%async_computation | async-start | bytes 4718592 | tf_op jit(solution)/shard_map/all_to_all | solution.py:315
  293.9 141.3 %copy-start.279 = (bf16[2,24]{1,0:T(2,128)(2,1)S(1)}, bf16[2,24]{1,0:T(2,128)(2,1)}, u32[]{:S(2)}) copy-start(bf16[2,24]{1,0:T(2,128)(2,1)} %param.38) | copy-start | bytes 292
  293.9 204.8 %copy-start.280 = (bf16[2,24]{1,0:T(2,128)(2,1)S(1)}, bf16[2,24]{1,0:T(2,128)(2,1)}, u32[]{:S(2)}) copy-start(bf16[2,24]{1,0:T(2,128)(2,1)} %param.43) | copy-start | bytes 292
  293.9 270.5 %copy-start.281 = (bf16[2,96]{1,0:T(2,128)(2,1)S(1)}, bf16[2,96]{1,0:T(2,128)(2,1)}, u32[]{:S(2)}) copy-start(bf16[2,96]{1,0:T(2,128)(2,1)} %param.41) | copy-start | bytes 1156
  293.9 334.0 %copy-start.282 = (bf16[2,24]{1,0:T(2,128)(2,1)S(1)}, bf16[2,24]{1,0:T(2,128)(2,1)}, u32[]{:S(2)}) copy-start(bf16[2,24]{1,0:T(2,128)(2,1)} %param.45) | copy-start | bytes 292
  293.9 399.8 %copy-start.283 = (bf16[2,24]{1,0:T(2,128)(2,1)S(1)}, bf16[2,24]{1,0:T(2,128)(2,1)}, u32[]{:S(2)}) copy-start(bf16[2,24]{1,0:T(2,128)(2,1)} %param.44) | copy-start | bytes 292
  293.9 474.5 %all-to-all-start.2 = ((bf16[2,8,2,48,768]{4,3,2,0,1:T(8,128)(2,1)}), bf16[2,8,2,48,768]{4,3,2,0,1:T(8,128)(2,1)}, u32[]{:S(2)}, u32[]{:S(2)}) async-start(bf16[2,8,2,48,768]{4,3,2,0,1:T(8,128)(2,1)} %copy.305), calls=%async_computation.2 | async-start | bytes 4718592 | tf_op jit(solution)/shard_map/all_to_all | solution.py:316
  298.5 1020.2 %reduce-scatter.24.cloned.1.call-start = ((), (), s32[]{:S(2)}) async-start(), calls=%async_computation.17 | async-start | bytes 1622016
  1009.2 326.6 %reduce-scatter.18.cloned.1.call-start = ((), (), s32[]{:S(2)}) async-start(), calls=%async_computation.14 | async-start | bytes 4866048 | tf_op jit(solution)/shard_map/reduce_scatter | solution.py:391
  1023.9 416.8 %reduce-scatter.16.cloned.1.call-start = ((), (), s32[]{:S(2)}) async-start(), calls=%async_computation.13 | async-start | bytes 14598144 | tf_op jit(solution)/shard_map/reduce_scatter | solution.py:388
  1067.3 584.3 %reduce-scatter.20.cloned.1.call-start = ((), (), s32[]{:S(2)}) async-start(), calls=%async_computation.15 | async-start | bytes 19464192 | tf_op jit(solution)/shard_map/reduce_scatter | solution.py:395
  1095.8 767.1 %reduce-scatter.22.cloned.1.call-start = ((), (), s32[]{:S(2)}) async-start(), calls=%async_computation.16 | async-start | bytes 19464192 | tf_op jit(solution)/shard_map/reduce_scatter | solution.py:397
  1159.6 72.5 %all-to-all-start.3 = ((bf16[2,1,2,384,768]{4,2,0,1,3:T(2,128)(2,1)}), bf16[2,1,2,384,768]{4,2,0,1,3:T(2,128)(2,1)S(1)}, u32[]{:S(2)}, u32[]{:S(2)}) async-start(bf16[2,1,2,384,768]{4,2,0,1,3:T(2,128)(2,1)} %copy.324), calls=%async_computation.3 | async-start | bytes 4718592 | tf_op jit(solution)/shard_map/all_to_all | solution.py:380
  1169.0 68.8 %copy-start.230 = (f32[768]{0:T(1024)S(1)}, f32[768]{0:T(1024)}, u32[]{:S(2)}) copy-start(f32[768]{0:T(1024)} %get-tuple-element.152) | copy-start | bytes 9220
  1169.0 68.8 %copy-start.260 = (f32[768]{0:T(1024)S(1)}, f32[768]{0:T(1024)}, u32[]{:S(2)}) copy-start(f32[768]{0:T(1024)} %get-tuple-element.144) | copy-start | bytes 9220
  1232.2 88.5 %all-to-all-start.1 = ((bf16[2,1,2,384,768]{4,2,0,1,3:T(2,128)(2,1)}), bf16[2,1,2,384,768]{4,2,0,1,3:T(2,128)(2,1)}, u32[]{:S(2)}, u32[]{:S(2)}) async-start(bf16[2,1,2,384,768]{4,2,0,1,3:T(2,128)(2,1)} %copy.302), calls=%async_computation.1 | async-start | bytes 4718592 | tf_op jit(solution)/shard_map/all_to_all | solution.py:379
  1330.3 532.7 %copy-start.1 = (bf16[2,16,48,768]{3,2,1,0:T(8,128)(2,1)S(1)}, bf16[2,16,48,768]{3,2,1,0:T(8,128)(2,1)}, u32[]{:S(2)}) copy-start(bf16[2,16,48,768]{3,2,1,0:T(8,128)(2,1)} %param.29) | copy-start | bytes 7077892
  (314 other events, 3646.3 us)
Sparse Core Ops, SparseCore 0:
  10.9 106.3 all-gather.13
  120.1 55.6 all-gather.15
  178.7 80.4 all-gather.17
  261.9 119.4 all-gather.19
  1009.3 96.3 reduce-scatter.23
  1111.6 145.9 reduce-scatter.17
  1264.2 176.4 reduce-scatter.15
  1447.7 203.8 reduce-scatter.19
  1658.6 204.3 reduce-scatter.21
where the time goes:
time: 1880 us; the launch traced here: 1870 us
  blocking collectives  772 us (41%)
  waiting for transfers between devices  593 us (32%)
  matrix products  238 us (13%)
  local copies, waits for them, and re-layouts  111 us (6%)
  other arithmetic  110 us (6%)
  between operations  23.8 us (1%)
  starting transfers between devices  21.4 us (1%)
    reduce_scatter x1, waiting for transfers between devices, per_device(): lax.psum_scatter(totals[9], ('dp', 'fsdp'), scatter_dimension=1, tiled=True)  211 us
    reduce_scatter x1, waiting for transfers between devices, per_device(): lax.psum_scatter(totals[7], ('dp', 'fsdp'), scatter_dimension=1, tiled=True)  211 us
    all_gather x1, blocking collectives, per_device(): lax.all_gather(beta_attn, ('dp', 'fsdp'), axis=1, tiled=True)  132 us
    all_gather x1, blocking collectives, per_device(): lax.all_gather(bias_out, ('dp', 'fsdp'), axis=1, tiled=True)  113 us
    reduce_scatter x1, waiting for transfers between devices, per_device(): lax.psum_scatter(totals[0], ('dp', 'fsdp'), scatter_dimension=1, tiled=True)  105 us
    unnamed x1, blocking collectives  75.6 us
    all_gather x1, blocking collectives, per_device(): lax.all_gather(bias_value, ('dp', 'fsdp'), axis=1, tiled=True)  65.9 us
    all_gather x1, blocking collectives, per_device(): lax.all_gather(bias_down, ('dp', 'fsdp'), axis=1, tiled=True)  65.6 us
  transfers between devices with their start and end apart: 13, of which 4 were waited for; matrix products, arithmetic and copies ran while one was open for 14% of the time, Pallas kernels for 0%

commit v1 on v0

v1 whole, which is shorter than its diff:
```python
import jax
import jax.numpy as jnp
from jax import lax
from jax.experimental import pallas as pl
from jax.experimental.pallas import tpu as pltpu
from jax.sharding import PartitionSpec as P

HEADS = 12
BLOCK = 64
NBLK = 6
LAYERS = 2
CORES = 2
AXES = ("dp", "fsdp")
NEG = -1000000000.0
HEAD_DIM = 64


epsilon = 1e-06


def split_fsdp(count):
    inner = 1
    while (2 * inner) ** 2 <= count:
        inner *= 2
    return (count // inner, inner)


class Grid:
    def __init__(self, dp_count, fsdp_count):
        outer, inner = split_fsdp(fsdp_count)
        self.sizes = (dp_count // CORES, CORES, outer, inner)
        dp_at, fsdp_at = lax.axis_index("dp"), lax.axis_index("fsdp")
        self.at = (dp_at // CORES, dp_at % CORES, fsdp_at // inner, fsdp_at % inner)

        self.count = dp_count * fsdp_count

    def index(self, place):
        total = 0
        for size, at in zip(self.sizes, place):
            total = total * size + at
        return total

    def send(self, array, axis, offset):
        pairs = []
        sizes = self.sizes
        for flat in range(sizes[0] * sizes[1] * sizes[2] * sizes[3]):
            place, rest = [], flat
            for size in reversed(sizes):
                place.insert(0, rest % size)
                rest //= size
            place[axis] = (place[axis] + offset) % sizes[axis]
            pairs.append((flat, self.index(place)))
        return lax.ppermute(array, AXES, pairs)


ALL = slice(None)
HBM = pl.BlockSpec(memory_space=pl.ANY)


class Links:
    def __init__(self, sizes, send_sem, recv_sem):
        outer, inner = sizes[2:]
        dp_at, fsdp_at = lax.axis_index("dp"), lax.axis_index("fsdp")
        self.sizes = sizes
        self.at = (dp_at // CORES, dp_at % CORES, fsdp_at // inner, fsdp_at % inner)
        self.send_sem, self.recv_sem = send_sem, recv_sem
        self.used = 0

    def device(self, place):
        return (place[0] * CORES + place[1], place[2] * self.sizes[3] + place[3])

    def along(self, axis, offset):
        place = list(self.at)
        place[axis] = (place[axis] + offset) % self.sizes[axis]
        return self.device(place)

    def start(self, source, target, device):
        copy = pltpu.make_async_remote_copy(
            src_ref=source,
            dst_ref=target,
            send_sem=self.send_sem.at[self.used],
            recv_sem=self.recv_sem.at[self.used],
            device_id=device,
            device_id_type=pl.DeviceIdType.MESH,
        )
        self.used += 1
        copy.start()
        return copy

    def start_here(self, source, target):
        copy = pltpu.make_async_copy(source, target, self.recv_sem.at[self.used])
        self.used += 1
        copy.start()
        return copy

    def greet(self, devices):
        barrier = pltpu.get_barrier_semaphore()
        for device in devices:
            pl.semaphore_signal(barrier, inc=1, device_id=device, device_id_type=pl.DeviceIdType.MESH)
        pl.semaphore_wait(barrier, len(devices))

    def partners(self):
        found = [self.along(axis, k) for axis in (0, 1) for k in range(1, self.sizes[axis])]
        count = self.sizes[2] * self.sizes[3]
        return found + [self.member(k) for k in range(1, count)]

    def member(self, offset):
        count = self.sizes[2] * self.sizes[3]
        flat = self.at[2] * self.sizes[3] + self.at[3]
        return (self.at[0] * CORES + self.at[1], (flat + offset) % count)


class Gather:
    def __init__(self, links, source, target, order):
        self.links, self.source, self.target, self.order = links, source, target, order
        self.sent = []
        self.across = []

    def begin(self):
        links = self.links
        spot = self.target(*links.at)
        self.own = links.start_here(self.source, spot)
        self.column = [
            links.start(self.source, spot, links.along(2, k)) for k in range(1, links.sizes[2])
        ]

    def hand_over(self, spot):
        self.across.append(self.links.start(spot, spot, self.links.along(1, 1)))

    def first(self):
        links = self.links
        x, c, o, i = links.at
        self.own.wait()
        for copy in self.column:
            copy.wait_recv()
        spot = self.target(x, c, ALL, i)
        axis = self.order[0]
        self.line = [
            links.start(spot, spot, links.along(axis, k)) for k in range(1, links.sizes[axis])
        ]
        self.hand_over(spot)

    def second(self):
        links = self.links
        x, c, o, i = links.at
        for copy in self.line:
            copy.wait_recv()
        first, second = self.order
        spot = self.target(ALL, c, ALL, i) if first == 0 else self.target(x, c, ALL, ALL)
        self.sheet = [
            links.start(spot, spot, links.along(second, k)) for k in range(1, links.sizes[second])
        ]
        for k in range(1, links.sizes[first]):
            near = (links.at[first] - k) % links.sizes[first]
            self.hand_over(
                self.target(near, c, ALL, i) if first == 0 else self.target(x, c, ALL, near)
            )

    def third(self):
        links = self.links
        c = links.at[1]
        second = self.order[1]
        for k, copy in enumerate(self.sheet, 1):
            copy.wait_recv()
            near = (links.at[second] - k) % links.sizes[second]
            self.hand_over(
                self.target(near, c, ALL, ALL) if second == 0 else self.target(ALL, c, ALL, near)
            )

    def end(self):
        for copy in self.across:
            copy.wait()
        for copy in self.column + self.line + self.sheet:
            copy.wait_send()


def deal_out(links, source, target):
    count = links.sizes[2] * links.sizes[3]
    me = links.at[2] * links.sizes[3] + links.at[3]
    spot = target.at[:, :, me]
    copies = [links.start_here(source.at[:, me], spot)]
    for k in range(1, count):
        copies.append(links.start(source.at[:, (me + k) % count], spot, links.member(k)))
    return copies


def deal_back(links, source, target):
    count = links.sizes[2] * links.sizes[3]
    me = links.at[2] * links.sizes[3] + links.at[3]
    spot = target.at[:, me]
    copies = [links.start_here(source.at[:, :, me], spot)]
    for k in range(1, count):
        copies.append(links.start(source.at[:, :, (me + k) % count], spot, links.member(k)))
    return copies


def gathers_of(links, layer_at, square, down, small, all_square, all_down, all_small):
    def of_square(start, order):
        blocks = slice(start, start + 2)
        return Gather(
            links,
            square.at[layer_at, blocks],
            lambda *place: all_square.at[(layer_at, blocks) + place],
            order,
        )

    def of_down(start, order):
        blocks = slice(start, start + 2)
        return Gather(
            links,
            down.at[layer_at, blocks],
            lambda *place: all_down.at[(layer_at,) + place + (blocks,)],
            order,
        )

    tiny = Gather(
        links, small.at[layer_at], lambda *place: all_small.at[(layer_at,) + place], (0, 3)
    )
    return [
        [tiny, of_square(0, (0, 3)), of_square(2, (3, 0))],
        [of_square(4, (0, 3)), of_square(6, (3, 0))],
        [of_down(0, (0, 3)), of_down(2, (3, 0))],
    ]


def bring_kernel(sizes, *refs):
    sent_x, sent_grad, square, down, small = refs[:5]
    got_x, got_grad, all_square, all_down, all_small = refs[5:10]
    links = Links(sizes, *refs[10:])
    links.greet(links.partners())
    groups = []
    for layer_at in range(LAYERS):
        groups += gathers_of(
            links, layer_at, square, down, small, all_square, all_down, all_small
        )
    for at, group in enumerate(groups):
        for item in group:
            item.begin()
        if at == 2:
            moved = deal_out(links, sent_x, got_x)
    moved += deal_out(links, sent_grad, got_grad)
    for at in range(len(groups) + 1):
        if at > 0:
            for item in groups[at - 1]:
                item.second()
        if at < len(groups):
            for item in groups[at]:
                item.first()
        if at > 1:
            for item in groups[at - 2]:
                item.third()
    for item in groups[-1]:
        item.third()
    for group in groups:
        for item in group:
            item.end()
    for copy in moved:
        copy.wait()


def bring(sizes, sent_x, sent_grad, square, down, small):
    low = jnp.bfloat16
    batch, members, two, rows, width = sent_x.shape
    r = square.shape[2]
    got = jax.ShapeDtypeStruct((batch, two, members, rows, width), low)
    outs = [
        got,
        got,
        jax.ShapeDtypeStruct((LAYERS, square.shape[1]) + sizes + (r, width), low),
        jax.ShapeDtypeStruct((LAYERS,) + sizes + (down.shape[1], r, width), low),
        jax.ShapeDtypeStruct((LAYERS,) + sizes + (8, width), low),
    ]
    per_item = 1 + sum(n - 1 for n in sizes) + 4 + sizes[0] + sizes[3]
    count = 7 * LAYERS * per_item + 2 * members
    return pl.pallas_call(
        lambda *refs: bring_kernel(sizes, *refs),
        out_shape=outs,
        in_specs=[HBM] * 5,
        out_specs=[HBM] * 5,
        scratch_shapes=[pltpu.SemaphoreType.DMA((count,)), pltpu.SemaphoreType.DMA((count,))],
        compiler_params=pltpu.CompilerParams(collective_id=0, has_side_effects=True),
        name="bring",
    )(sent_x, sent_grad, square, down, small)


def pick(array, at, axis):
    return lax.dynamic_index_in_dim(array, at, axis, keepdims=False)


def gather_rows(grid, rows):
    count, width = rows.shape
    half = width // 2
    xs, cs, outs, ins = grid.sizes
    x, c, o, i = grid.at
    column = jnp.zeros((outs, count, width), rows.dtype)
    for step in range(outs):
        piece = rows if step == 0 else grid.send(rows, 2, step)
        column = lax.dynamic_update_slice(column, piece[None], ((o - step) % outs, 0, 0))
    pieces = {}
    for side, (first, second) in enumerate(((0, 3), (3, 0))):
        start = column[:, :, side * half : (side + 1) * half]
        line = [start] + [grid.send(start, first, k) for k in range(1, grid.sizes[first])]
        for far, piece in enumerate(line):
            for near in range(grid.sizes[second]):
                moved = piece if near == 0 else grid.send(piece, second, near)
                kx, ki = (far, near) if first == 0 else (near, far)
                pieces[side, kx, ki, 0] = moved
    for (side, kx, ki, unused), piece in list(pieces.items()):
        pieces[side, kx, ki, 1] = grid.send(piece, 1, 1)
    whole = jnp.zeros((xs, cs, outs, ins, count, width), rows.dtype)
    for (side, kx, ki, kc), piece in pieces.items():
        place = ((x - kx) % xs, (c - kc) % cs, 0, (i - ki) % ins, 0, side * half)
        whole = lax.dynamic_update_slice(whole, piece[None, None, :, None], place)
    return whole


def scatter_rows(grid, whole):
    width = whole.shape[-1]
    half = width // 2
    low = whole.dtype
    x, c, o, i = grid.at
    here = pick(whole, c, 1).astype(jnp.float32)
    there = grid.send(pick(whole, 1 - c, 1), 1, 1).astype(jnp.float32)
    both = (here + there).astype(low)
    sides = []
    for side, order in enumerate(((3, 0), (0, 3))):
        part = both[..., side * half : (side + 1) * half]
        left = [0, 2, 3]
        for axis in order + (2,):
            at = left.index(axis)
            left.remove(axis)
            mine = grid.at[axis]
            size = grid.sizes[axis]
            total = pick(part, mine, at).astype(jnp.float32)
            for k in range(1, size):
                total = total + grid.send(pick(part, (mine + k) % size, at), axis, k).astype(jnp.float32)
            part = total if axis == 2 else total.astype(low)
        sides.append(part)
    return jnp.concatenate(sides, axis=-1)


def bin_mask(first_blocks, second_blocks, random_pair):
    block_ids = jnp.arange(NBLK)
    later_seg = block_ids >= first_blocks
    rel_block = jnp.where(later_seg, block_ids - first_blocks, block_ids)
    seg_len = jnp.where(later_seg, second_blocks, first_blocks)
    live_block = block_ids < first_blocks + second_blocks
    rand_rows = jnp.where(
        later_seg[:, None],
        jnp.take(random_pair[1], rel_block, axis=0),
        jnp.take(random_pair[0], rel_block, axis=0),
    )
    picked = jnp.remainder(rand_rows, seg_len[:, None])
    row_rel = rel_block[:, None]
    col_rel = rel_block[None, :]
    row_len = seg_len[:, None]
    nearby = jnp.abs(row_rel - col_rel) <= 1
    global_hit = (
        (col_rel == 0) | (col_rel == row_len - 1) | (row_rel == 0) | (row_rel == row_len - 1)
    )
    random_hit = jnp.any(picked[:, :, None] == rel_block[None, None, :], axis=1)
    same_seg = (
        (later_seg[:, None] == later_seg[None, :]) & live_block[:, None] & live_block[None, :]
    )
    allowed = (nearby | global_hit | random_hit) & same_seg
    return jnp.repeat(jnp.repeat(allowed, BLOCK, axis=0), BLOCK, axis=1)


def dot(left, right):
    return jnp.dot(left, right, preferred_element_type=jnp.float32)


def dot_back(left, right):
    return lax.dot_general(left, right, (((1,), (1,)), ((), ())), preferred_element_type=jnp.float32)


def dot_weight(left, right):
    return lax.dot_general(left, right, (((0,), (0,)), ((), ())), preferred_element_type=jnp.float32)


LOW = jnp.bfloat16
LANES = 128
BQ, BV, BO, GA, BA, BD, GF, BF, BU = range(9)


def layer_norm(residual):
    center = residual - jnp.mean(residual, axis=-1, keepdims=True)
    inv_std = lax.rsqrt(jnp.mean(center * center, axis=-1, keepdims=True) + epsilon)
    return (center * inv_std, inv_std)


def norm_back(grad_out, normed, inv_std, gain):
    scaled = grad_out * gain
    return inv_std * (
        scaled
        - jnp.mean(scaled, axis=-1, keepdims=True)
        - normed * jnp.mean(scaled * normed, axis=-1, keepdims=True)
    )


def gelu_parts(u):
    root = 0.7978845608028654
    t = jnp.tanh(root * (u + 0.044715 * (u * u * u)))
    half = 0.5 * (1.0 + t)
    slope = half + 0.5 * u * (1.0 - t * t) * (root * (1.0 + 3 * 0.044715 * (u * u)))
    return (u * half, slope)


def lanes_of(pair, head):
    return pair[:, head * HEAD_DIM : (head + 1) * HEAD_DIM]


def pair_at(pair, offset=0):
    return pl.ds(pl.multiple_of(offset + pair * 2 * HEAD_DIM, 2 * HEAD_DIM), 2 * HEAD_DIM)


def lane_ids(rows):
    return lax.broadcasted_iota(jnp.int32, (rows, LANES), 1)


def attn_fwd_kernel(x_ref, w_ref, v_ref, mask_ref, qkv_ref, ctx_ref, stat_ref, normed_ref):
    rows, width = x_ref.shape
    act = x_ref[...].astype(LOW)
    for j, bias in enumerate((BQ, None, BV)):
        out = dot(act, w_ref[0, j])
        if bias is not None:
            out = out + v_ref[0, bias : bias + 1, :]
        qkv_ref[:, j * width : (j + 1) * width] = out.astype(LOW)
    scale = HEAD_DIM ** (-0.5)
    lanes = lane_ids(rows)
    stat_ref[...] = jnp.zeros_like(stat_ref)

    def pair_step(pair, carry):
        q = qkv_ref[:, pair_at(pair)]
        k = qkv_ref[:, pair_at(pair, width)]
        v = qkv_ref[:, pair_at(pair, 2 * width)]
        mixed = []
        for head in range(2):
            s = dot_back(lanes_of(q, head), lanes_of(k, head)) * scale
            s = jnp.where(mask_ref[0] > 0, s, NEG)
            top = jnp.max(s, axis=-1, keepdims=True)
            e = jnp.exp(s - top)
            total = jnp.sum(e, axis=-1, keepdims=True)
            mixed.append(dot(e.astype(LOW), lanes_of(v, head)) / total)
            log_total = top + jnp.log(total)
            stat_ref[...] = jnp.where(lanes == 2 * pair + head, log_total, stat_ref[...])
        ctx_ref[:, pair_at(pair)] = jnp.concatenate(mixed, axis=1).astype(LOW)
        return carry

    lax.fori_loop(0, HEADS // 2, pair_step, 0)
    resid = x_ref[...].astype(jnp.float32) + dot(ctx_ref[...], w_ref[0, 3])
    normed, inv = layer_norm(resid + v_ref[0, BO : BO + 1, :])
    normed_ref[...] = normed
    stat_ref[...] = jnp.where(lanes == HEADS, inv, stat_ref[...])


def attn_fwd(x, square, vectors, mask, layer_at):
    rows, width = x.shape
    bins, block = mask.shape[:2]
    row = lambda n: pl.BlockSpec((block, n), lambda b: (b, 0))
    f32 = jnp.float32
    return pl.pallas_call(
        attn_fwd_kernel,
        grid=(bins,),
        in_specs=[
            row(width),
            pl.BlockSpec((1, 4, width, width), lambda b: (layer_at, 0, 0, 0)),
            pl.BlockSpec((1,) + vectors.shape[1:], lambda b: (layer_at, 0, 0)),
            pl.BlockSpec((1, block, block), lambda b: (b, 0, 0)),
        ],
        out_specs=[row(3 * width), row(width), row(LANES), row(width)],
        out_shape=[
            jax.ShapeDtypeStruct((rows, 3 * width), LOW),
            jax.ShapeDtypeStruct((rows, width), LOW),
            jax.ShapeDtypeStruct((rows, LANES), f32),
            jax.ShapeDtypeStruct((rows, width), f32),
        ],
        name="attn_fwd",
    )(x, square, vectors, mask)


def middle_of(normed_ref, v_ref):
    return normed_ref[...] * v_ref[0, GA : GA + 1, :] + v_ref[0, BA : BA + 1, :]


def bias_up_of(v_ref, at, count):
    picked = v_ref[0, BU : BU + 1, :]
    for j in range(1, count):
        picked = jnp.where(at == j, v_ref[0, BU + j : BU + j + 1, :], picked)
    return picked


def mlp_fwd_kernel(
    count, normed_ref, wu_ref, wd_ref, v_ref, up_ref, out_ref, low_ref, fnorm_ref, stat_ref, mid, acc
):
    at = pl.program_id(0)

    @pl.when(at == 0)
    def _():
        mid[...] = middle_of(normed_ref, v_ref).astype(LOW)
        acc[...] = jnp.zeros_like(acc)

    up = dot(mid[...], wu_ref[0, 0]) + bias_up_of(v_ref, at, count)
    up_ref[...] = up
    acc[...] += dot(gelu_parts(up)[0].astype(LOW), wd_ref[0])

    @pl.when(at == count - 1)
    def _():
        resid = middle_of(normed_ref, v_ref) + acc[...] + v_ref[0, BD : BD + 1, :]
        normed, inv = layer_norm(resid)
        fnorm_ref[...] = normed
        stat_ref[...] = jnp.broadcast_to(inv, stat_ref.shape)
        out = normed * v_ref[0, GF : GF + 1, :] + v_ref[0, BF : BF + 1, :]
        out_ref[...] = out
        low_ref[...] = out.astype(LOW)


def mlp_fwd(normed, square, down, vectors, layer_at):
    rows, width = normed.shape
    count = down.shape[1] // width
    whole = lambda n: pl.BlockSpec((rows, n), lambda j: (0, 0))
    f32 = jnp.float32
    return pl.pallas_call(
        lambda *refs: mlp_fwd_kernel(count, *refs),
        grid=(count,),
        in_specs=[
            whole(width),
            pl.BlockSpec((1, 1, width, width), lambda j: (layer_at, 4 + j, 0, 0)),
            pl.BlockSpec((1, width, width), lambda j: (layer_at, j, 0)),
            pl.BlockSpec((1,) + vectors.shape[1:], lambda j: (layer_at, 0, 0)),
        ],
        out_specs=[
            pl.BlockSpec((rows, width), lambda j: (0, j)),
            whole(width),
            whole(width),
            whole(width),
            whole(LANES),
        ],
        out_shape=[
            jax.ShapeDtypeStruct((rows, count * width), f32),
            jax.ShapeDtypeStruct((rows, width), f32),
            jax.ShapeDtypeStruct((rows, width), LOW),
            jax.ShapeDtypeStruct((rows, width), f32),
            jax.ShapeDtypeStruct((rows, LANES), f32),
        ],
        scratch_shapes=[pltpu.VMEM((rows, width), LOW), pltpu.VMEM((rows, width), f32)],
        name="mlp_fwd",
    )(normed, square, down, vectors)


def sum_rows(values):
    return jnp.sum(values, axis=0, keepdims=True)


def mlp_bwd_kernel(
    count,
    grad_ref,
    fnorm_ref,
    fstat_ref,
    normed_ref,
    stat_ref,
    up_ref,
    wu_ref,
    wd_ref,
    v_ref,
    dwu_ref,
    dwd_ref,
    grad_a_ref,
    vec_ref,
    mid,
    grad_f,
    low_f,
    acc,
):
    at = pl.program_id(0)

    @pl.when(at == 0)
    def _():
        grad_out, normed = grad_ref[...].astype(jnp.float32), fnorm_ref[...]
        vec_ref[...] = jnp.zeros_like(vec_ref)
        vec_ref[GF : GF + 1, :] = sum_rows(grad_out * normed)
        vec_ref[BF : BF + 1, :] = sum_rows(grad_out)
        grad = norm_back(grad_out, normed, fstat_ref[:, :1], v_ref[0, GF : GF + 1, :])
        vec_ref[BD : BD + 1, :] = sum_rows(grad)
        grad_f[...] = grad
        low_f[...] = grad.astype(LOW)
        mid[...] = middle_of(normed_ref, v_ref).astype(LOW)
        acc[...] = jnp.zeros_like(acc)

    act, slope = gelu_parts(up_ref[...])
    dwd_ref[...] = dot_weight(act.astype(LOW), low_f[...]).astype(LOW)
    grad_up = dot_back(low_f[...], wd_ref[0]) * slope
    vec_ref[pl.ds(BU + at, 1), :] = sum_rows(grad_up)
    low_up = grad_up.astype(LOW)
    dwu_ref[0] = dot_weight(mid[...], low_up).astype(LOW)
    acc[...] += dot_back(low_up, wu_ref[0, 0])

    @pl.when(at == count - 1)
    def _():
        grad_mid, normed = grad_f[...] + acc[...], normed_ref[...]
        vec_ref[GA : GA + 1, :] = sum_rows(grad_mid * normed)
        vec_ref[BA : BA + 1, :] = sum_rows(grad_mid)
        inv = stat_ref[:, HEADS : HEADS + 1]
        grad = norm_back(grad_mid, normed, inv, v_ref[0, GA : GA + 1, :])
        vec_ref[BO : BO + 1, :] = sum_rows(grad)
        grad_a_ref[...] = grad


def mlp_bwd(grad, fnorm, fstat, normed, stat, up, square, down, vectors, layer_at):
    rows, width = normed.shape
    count = down.shape[1] // width
    whole = lambda n: pl.BlockSpec((rows, n), lambda j: (0, 0))
    f32 = jnp.float32
    vec_rows = vectors.shape[1]
    return pl.pallas_call(
        lambda *refs: mlp_bwd_kernel(count, *refs),
        grid=(count,),
        in_specs=[
            whole(width),
            whole(width),
            whole(LANES),
            whole(width),
            whole(LANES),
            pl.BlockSpec((rows, width), lambda j: (0, j)),
            pl.BlockSpec((1, 1, width, width), lambda j: (layer_at, 4 + j, 0, 0)),
            pl.BlockSpec((1, width, width), lambda j: (layer_at, j, 0)),
            pl.BlockSpec((1, vec_rows, width), lambda j: (layer_at, 0, 0)),
        ],
        out_specs=[
            pl.BlockSpec((1, width, width), lambda j: (j, 0, 0)),
            pl.BlockSpec((width, width), lambda j: (j, 0)),
            whole(width),
            pl.BlockSpec((vec_rows, width), lambda j: (0, 0)),
        ],
        out_shape=[
            jax.ShapeDtypeStruct((count, width, width), LOW),
            jax.ShapeDtypeStruct((count * width, width), LOW),
            jax.ShapeDtypeStruct((rows, width), f32),
            jax.ShapeDtypeStruct((vec_rows, width), f32),
        ],
        scratch_shapes=[
            pltpu.VMEM((rows, width), LOW),
            pltpu.VMEM((rows, width), f32),
            pltpu.VMEM((rows, width), LOW),
            pltpu.VMEM((rows, width), f32),
        ],
        name="mlp_bwd",
    )(grad, fnorm, fstat, normed, stat, up, square, down, vectors)


def attn_bwd_kernel(
    grad_ref, qkv_ref, stat_ref, mask_ref, w_ref, vec_in, dqkv_ref, grad_in_ref, low_ref, vec_ref, gctx
):
    rows, width = grad_ref.shape

    @pl.when(pl.program_id(0) == 0)
    def _():
        vec_ref[...] = vec_in[...]

    low_ref[...] = grad_ref[...].astype(LOW)
    gctx[...] = dot_back(low_ref[...], w_ref[0, 3]).astype(LOW)
    scale = HEAD_DIM ** (-0.5)
    lanes = lane_ids(rows)

    def pair_step(pair, carry):
        q = qkv_ref[:, pair_at(pair)]
        k = qkv_ref[:, pair_at(pair, width)]
        v = qkv_ref[:, pair_at(pair, 2 * width)]
        g = gctx[:, pair_at(pair)]
        grads = [[], [], []]
        for head in range(2):
            qh, kh, vh, gh = (lanes_of(t, head) for t in (q, k, v, g))
            log_total = jnp.sum(
                jnp.where(lanes == 2 * pair + head, stat_ref[...], 0.0), axis=-1, keepdims=True
            )
            s = dot_back(qh, kh) * scale
            s = jnp.where(mask_ref[0] > 0, s, NEG)
            p = jnp.exp(s - log_total)
            grad_p = dot_back(gh, vh)
            inner = jnp.sum(grad_p * p, axis=-1, keepdims=True)
            low_s = (p * (grad_p - inner)).astype(LOW)
            grads[0].append(dot(low_s, kh) * scale)
            grads[1].append(dot_weight(low_s, qh) * scale)
            grads[2].append(dot_weight(p.astype(LOW), gh))
        for j, row in ((0, BQ), (1, None), (2, BV)):
            both = jnp.concatenate(grads[j], axis=1)
            dqkv_ref[:, pair_at(pair, j * width)] = both.astype(LOW)
            if row is not None:
                vec_ref[row : row + 1, pair_at(pair)] += sum_rows(both)
        return carry

    lax.fori_loop(0, HEADS // 2, pair_step, 0)
    total = grad_ref[...]
    for j in range(3):
        total = total + dot_back(dqkv_ref[:, j * width : (j + 1) * width], w_ref[0, j])
    grad_in_ref[...] = total


def attn_bwd(grad_a, qkv, stat, mask, square, vec, layer_at):
    rows, width = grad_a.shape
    bins, block = mask.shape[:2]
    row = lambda n: pl.BlockSpec((block, n), lambda b: (b, 0))
    fixed = pl.BlockSpec(vec.shape, lambda b: (0, 0))
    f32 = jnp.float32
    return pl.pallas_call(
        attn_bwd_kernel,
        grid=(bins,),
        in_specs=[
            row(width),
            row(3 * width),
            row(LANES),
            pl.BlockSpec((1, block, block), lambda b: (b, 0, 0)),
            pl.BlockSpec((1, 4, width, width), lambda b: (layer_at, 0, 0, 0)),
            fixed,
        ],
        out_specs=[row(3 * width), row(width), row(width), fixed],
        out_shape=[
            jax.ShapeDtypeStruct((rows, 3 * width), LOW),
            jax.ShapeDtypeStruct((rows, width), f32),
            jax.ShapeDtypeStruct((rows, width), LOW),
            jax.ShapeDtypeStruct(vec.shape, f32),
        ],
        scratch_shapes=[pltpu.VMEM((block, width), LOW)],
        name="attn_bwd",
    )(grad_a, qkv, stat, mask, square, vec)


def attn_dw_kernel(act_ref, dqkv_ref, ctx_ref, low_ref, out_ref):
    at = pl.program_id(0)

    @pl.when(at < 3)
    def _():
        out_ref[0] = dot_weight(act_ref[...].astype(LOW), dqkv_ref[...]).astype(LOW)

    @pl.when(at == 3)
    def _():
        out_ref[0] = dot_weight(ctx_ref[...], low_ref[...]).astype(LOW)


def attn_dw(act, dqkv, ctx, low):
    rows, width = act.shape
    whole = pl.BlockSpec((rows, width), lambda j: (0, 0))
    return pl.pallas_call(
        attn_dw_kernel,
        grid=(4,),
        in_specs=[
            whole,
            pl.BlockSpec((rows, width), lambda j: (0, jnp.minimum(j, 2))),
            whole,
            whole,
        ],
        out_specs=pl.BlockSpec((1, width, width), lambda j: (j, 0, 0)),
        out_shape=jax.ShapeDtypeStruct((4, width, width), LOW),
        name="attn_dw",
    )(act, dqkv, ctx, low)


SMALL = ("bq", "bv", "bo", "ga", "ba", "bd", "gf", "bf", "bu")


def pack_attn(p, layer_at):
    wq = p["wqkv"][layer_at]
    rows, width = p["wo"][layer_at].shape
    small = jnp.concatenate([p[name][layer_at] for name in SMALL])
    pad = 8 * width - small.shape[0]
    small = jnp.pad(small, (0, pad)).reshape(8, width)
    parts = [wq[:, j * width : (j + 1) * width] for j in range(3)] + [p["wo"][layer_at], small]
    return jnp.concatenate(parts, axis=0)


def pack_mlp(p, layer_at):
    width = p["wd"].shape[-1]
    wu = p["wu"][layer_at]
    count = wu.shape[1] // width
    parts = [wu[:, j * width : (j + 1) * width] for j in range(count)] + [p["wd"][layer_at]]
    return jnp.concatenate(parts, axis=0)


def small_rows(p, layer_at, width):
    small = jnp.concatenate([p[name][layer_at] for name in SMALL])
    return jnp.pad(small, (0, 8 * width - small.shape[0])).reshape(8, width)


def vectors_of(all_small, rows):
    layers, width = all_small.shape[0], all_small.shape[-1]
    flat = all_small.reshape(layers, -1, 8 * width).astype(jnp.float32)
    even = flat[:, :, : 8 * rows].reshape(layers, -1, 8, rows).transpose(0, 2, 1, 3)
    up = flat[:, :, 8 * rows : 12 * rows]
    return jnp.concatenate([even.reshape(layers, 8, width), up.reshape(layers, 4, width)], axis=1)


def small_of(vec, rows):
    even = vec[:BU].reshape(BU, -1, rows).transpose(1, 0, 2).reshape(-1, BU * rows)
    return jnp.concatenate([even, vec[BU:].reshape(even.shape[0], -1)], axis=1)


def forward(hidden, act_in, w, mask, layer_at):
    square, down, vectors = w
    qkv, ctx, stat, normed = attn_fwd(hidden, square, vectors, mask, layer_at)
    up, out, out_low, fnorm, fstat = mlp_fwd(normed, square, down, vectors, layer_at)
    return out, out_low, (act_in, qkv, ctx, stat, normed, up, fnorm, fstat)


def backward(grad, kept, w, mask, layer_at):
    square, down, vectors = w
    act_in, qkv, ctx, stat, normed, up, fnorm, fstat = kept
    dwu, dwd, grad_a, vec = mlp_bwd(
        grad, fnorm, fstat, normed, stat, up, square, down, vectors, layer_at
    )
    dqkv, grad_in, low_a, vec = attn_bwd(grad_a, qkv, stat, mask, square, vec, layer_at)
    return grad_in, (attn_dw(act_in, dqkv, ctx, low_a), dwu, dwd, vec)


def whole_attn(grid, square, vec, rows):
    width = square.shape[-1]
    shape = grid.sizes
    small = small_of(vec, rows)
    small = jnp.pad(small, ((0, 0), (0, 8 * width - small.shape[1])))
    parts = [square[j].reshape(shape + (rows, width)) for j in range(4)]
    parts.append(small.astype(LOW).reshape(shape + (8, width)))
    return jnp.concatenate(parts, axis=-2)


def whole_mlp(grid, dwu, dwd, rows):
    width = dwd.shape[-1]
    shape = grid.sizes
    parts = [dwu[j].reshape(shape + (rows, width)) for j in range(dwu.shape[0])]
    parts.append(dwd.reshape(shape + (-1, width)))
    return jnp.concatenate(parts, axis=-2)


def shift_down(rows, amount):
    doubled = jnp.concatenate([jnp.zeros_like(rows), rows], axis=0)
    return lax.dynamic_slice_in_dim(doubled, rows.shape[0] - amount, rows.shape[0], 0)


def shift_up(rows, amount):
    doubled = jnp.concatenate([rows, jnp.zeros_like(rows)], axis=0)
    return lax.dynamic_slice_in_dim(doubled, amount, rows.shape[0], 0)


def pack_bin(slots, first_len, second_len):
    positions = jnp.arange(slots.shape[1])[:, None]
    later = shift_down(jnp.where(positions < second_len, slots[1], 0), first_len)
    return jnp.where(positions < first_len, slots[0], later)


def unpack_bin(rows, first_len, second_len):
    positions = jnp.arange(rows.shape[0])[:, None]
    first = jnp.where(positions < first_len, rows, 0)
    second = jnp.where(positions < second_len, shift_up(rows, first_len), 0)
    return jnp.stack([first, second])


def per_device(tokens_in, cotangent, lengths, bin_deal, random_blocks, *weights):
    names = ("wqkv", "bq", "bv", "wo", "bo", "ga", "ba", "wu", "bu", "wd", "bd", "gf", "bf")
    p = dict(zip(names, weights))
    rows = p["wo"].shape[1]
    members = lax.axis_size("fsdp")
    member = lax.axis_index("fsdp")
    group_at = lax.axis_index("dp")
    grid = Grid(lax.axis_size("dp"), members)
    slot_count = 2 * members
    slot_ids = jnp.arange(slot_count)
    deal_here = lax.dynamic_index_in_dim(bin_deal, group_at, 1, keepdims=False)
    slot_hits = (deal_here[:, :, None] == slot_ids[None, None, :]).astype(jnp.int32)
    source_of = jnp.sum(slot_hits * slot_ids[None, :, None], axis=1)
    lengths_here = lax.dynamic_slice_in_dim(lengths, group_at * slot_count, slot_count, 1)
    bin_lengths = jnp.take_along_axis(lengths_here, source_of, axis=1)
    random_here = lax.dynamic_slice_in_dim(random_blocks, group_at * slot_count, slot_count, 1)
    batch_count, unused_slots, rows_dev, width = tokens_in.shape
    bin_len = rows_dev * members
    order_index = source_of[:, :, None, None]

    def dealt(array):
        sent = jnp.take_along_axis(array, order_index, axis=1)
        return sent.reshape(batch_count, members, 2, rows_dev, width)

    blocks = lambda w: w.reshape(LAYERS, rows, -1, width).transpose(0, 2, 1, 3)
    square = jnp.concatenate([blocks(p["wqkv"]), blocks(p["wo"]), blocks(p["wu"])], axis=1)
    down = p["wd"].reshape(LAYERS, -1, rows, width)
    small = jnp.stack([small_rows(p, layer_at, width) for layer_at in range(LAYERS)])
    got_x, got_grad, *gathered = bring(
        grid.sizes, dealt(tokens_in), dealt(cotangent), square, down, small
    )
    arrived_x = got_x.reshape(batch_count, 2, bin_len, width)
    arrived_grad = got_grad.reshape(batch_count, 2, bin_len, width)
    square, down, small = gathered
    side = rows * grid.count
    w = (
        square.reshape(LAYERS, -1, side, width),
        down.reshape(LAYERS, -1, width),
        vectors_of(small, rows),
    )
    slot_pair = lax.dynamic_slice_in_dim(bin_lengths, 2 * member, 2, 1)
    random_pair = lax.dynamic_slice_in_dim(random_here, 2 * member, 2, 1)
    allowed = jax.vmap(bin_mask)(slot_pair[:, 0], slot_pair[:, 1], random_pair)
    first_len = slot_pair[:, 0] * BLOCK
    second_len = slot_pair[:, 1] * BLOCK

    def packed(slots):
        bins = [pack_bin(slots[m], first_len[m], second_len[m]) for m in range(batch_count)]
        return jnp.concatenate(bins, axis=0)

    def given_back(bins):
        bins = bins.reshape(batch_count, bin_len, width)
        slots = [unpack_bin(bins[m], first_len[m], second_len[m]) for m in range(batch_count)]
        sent = jnp.stack(slots)[:, None]
        back = lax.all_to_all(sent, "fsdp", split_axis=3, concat_axis=1, tiled=True)
        back = back.reshape(batch_count, slot_count, rows_dev, width)
        return jnp.take_along_axis(back, deal_here[:, :, None, None], axis=1)

    mask = allowed.astype(jnp.float32)
    hidden = act_in = packed(arrived_x)
    kept = []
    for layer_at in range(LAYERS):
        hidden, act_in, stored = forward(hidden, act_in, w, mask, layer_at)
        kept.append(stored)
    output = given_back(act_in)
    grad = packed(arrived_grad)
    sums = [None] * LAYERS
    for layer_at in reversed(range(LAYERS)):
        grad, (dws, dwu, dwd, vec) = backward(grad, kept[layer_at], w, mask, layer_at)
        sums[layer_at] = (
            scatter_rows(grid, whole_attn(grid, dws, vec, rows)),
            scatter_rows(grid, whole_mlp(grid, dwu, dwd, rows)),
        )
    input_grad = given_back(grad.astype(jnp.bfloat16))
    out = {name: [] for name in names}
    for attn, mlp in sums:
        blocks = [attn[j * rows : (j + 1) * rows] for j in range(4)]
        out["wqkv"].append(jnp.concatenate(blocks[:3], axis=1))
        out["wo"].append(blocks[3])
        small = attn[4 * rows :].reshape(-1)
        at = 0
        for name in SMALL:
            count = rows * (4 if name == "bu" else 1)
            out[name].append(small[at : at + count])
            at += count
        half = mlp.shape[0] // 2
        ups = [mlp[j * rows : (j + 1) * rows] for j in range(half // rows)]
        out["wu"].append(jnp.concatenate(ups, axis=1))
        out["wd"].append(mlp[half:])
    return (output, input_grad) + tuple(jnp.stack(out[name]) for name in names)


def solution(mesh):
    tokens = P(None, "dp", "fsdp", None)
    matrix = P(None, AXES, None)
    vector = P(None, AXES)
    weights = (matrix, vector, vector, matrix, vector, vector, vector)
    weights += (matrix, vector, matrix, vector, vector, vector)
    return jax.shard_map(
        per_device,
        mesh=mesh,
        in_specs=(tokens, tokens, P(), P(), P()) + weights,
        out_specs=(tokens, tokens) + weights,
        check_vma=False,
    )
```

time: 1880 us -> 854 us (0.45)
  blocking collectives: 772 us -> 0 us
  Pallas kernels: 0 us -> 435 us
  waiting for transfers between devices: 593 us -> 161 us
  matrix products: 238 us -> 0 us
  starting transfers between devices: 21.4 us -> 83.1 us
  other arithmetic: 110 us -> 58.8 us
    all_gather x9 -> x0, blocking collectives: 696 us -> none  [the longest x1 132 us: per_device(): lax.all_gather(beta_attn, ('dp', 'fsdp'), axis=1, tiled=True)]
    reduce_scatter x4 -> x0, waiting for transfers between devices: 527 us -> none  [the longest x1 211 us: per_device(): lax.psum_scatter(totals[9], ('dp', 'fsdp'), scatter_dimension=1, tiled=True)]
    pallas_call x0 -> x11, Pallas kernels: none -> 435 us  [the longest x1 223 us: bring(): pl.pallas_call(lambda *refs: bring_kernel(sizes, *refs), out_shape=outs,...]
    dot_general x72 -> x0, matrix products: 238 us -> none  [the longest x4 29.5 us: layer_backward(): jnp.einsum('sd,fd->sf', down_low, weight_down[layer_at], preferred_elemen...]
    ppermute x0 -> x44, waiting for transfers between devices: none -> 161 us  [send(): return lax.ppermute(array, AXES, pairs)]
    unnamed x1 -> x0, blocking collectives: 75.6 us -> none
    ppermute x0 -> x44, starting transfers between devices: none -> 75 us  [send(): return lax.ppermute(array, AXES, pairs)]
    all_to_all x4 -> x2, waiting for transfers between devices: 63.2 us -> 0.01 us  [given_back(): back = lax.all_to_all(sent, 'fsdp', split_axis=3, concat_axis=1, tiled=True)]
  transfers between devices with their start and end apart: 13 -> 46, of which waited for: 4 -> 17; matrix products, arithmetic and copies ran while one was open for 14% -> 12% of each run, Pallas kernels for 0% -> 1%
where the time goes in v1:
time: 854 us; the launch traced here: 849 us
  Pallas kernels  435 us (51%)
  waiting for transfers between devices  161 us (19%)
  local copies, waits for them, and re-layouts  102 us (12%)
  starting transfers between devices  83.1 us (10%)
  other arithmetic  58.8 us (7%)
  between operations  8.94 us (1%)
    pallas_call x1, Pallas kernels, bring(): pl.pallas_call(lambda *refs: bring_kernel(sizes, *refs), out_shape=outs,...  223 us
    ppermute x44, waiting for transfers between devices, send(): return lax.ppermute(array, AXES, pairs)  161 us
    ppermute x44, starting transfers between devices, send(): return lax.ppermute(array, AXES, pairs)  75 us
    pallas_call x2, Pallas kernels, mlp_bwd(): pl.pallas_call(lambda *refs: mlp_bwd_kernel(count, *refs), grid=(count,),...  60.9 us
    pallas_call x2, Pallas kernels, attn_bwd(): pl.pallas_call(attn_bwd_kernel, grid=(bins,), in_specs=[row(width), row(3...  58 us
    pallas_call x2, Pallas kernels, attn_fwd(): pl.pallas_call(attn_fwd_kernel, grid=(bins,), in_specs=[row(width), pl.Bl...  42.2 us
    pallas_call x2, Pallas kernels, mlp_fwd(): pl.pallas_call(lambda *refs: mlp_fwd_kernel(count, *refs), grid=(count,),...  33.5 us
    unnamed x111, local copies, waits for them, and re-layouts  25.3 us
  transfers between devices with their start and end apart: 46, of which 17 were waited for; matrix products, arithmetic and copies ran while one was open for 12% of the time, Pallas kernels for 1%

profile of v1, /device:TPU:0, one launch (start us, length us, event | category | flops | bytes accessed | tf_op | source)
XLA Modules:
  0.0 849.4 jit_solution(13754438021577905325)
XLA Ops:
  22.3 223.4 %bring.1 = (bf16[2,2,8,48,768]{4,3,2,1,0:T(8,128)(2,1)}, bf16[2,2,8,48,768]{4,3,2,1,0:T(8,128)(2,1)}, bf16[2,8,2,2,4,2,24,768]{7,6,5,4,3,2,1,0:T(8,128)(2,1)}, b...) custom-call(bf16[2,8,2,48,768]{4,3,2,1,0:T(8,128)(2,1)} %bitcast.445, ...), custom_call_target="tpu_custom_call" | custom-call | tf_op jit(solution)/shard_map/bring/pallas_call | solution.py:275
  263.3 20.9 %attn_fwd.2 = (bf16[768,2304]{1,0:T(8,128)(2,1)}, bf16[768,768]{1,0:T(8,128)(2,1)}, f32[768,128]{1,0:T(8,128)}, f32[768,768]{1,0:T(8,128)}) custom-call(bf16[768,768]{1,0:T(8,128)(2,1)} %pad_maximum_fusion.x_ref.act_ref, bf16[2,8,768,768]{3,2,1,0:T(8,128)(2,1)} %bitcast.422, f32[2,12,768]{2,1,0:T(8,128)} %copy-done.6, f32[2,384,384]{2,1,0:T(8,128)} %copy.242.mask_ref), custom_call_target="tpu_custom_call" | custom-call | tf_op jit(solution)/shard_map/attn_fwd/pallas_call | solution.py:462
  284.2 16.8 %mlp_fwd.2 = (f32[768,3072]{1,0:T(8,128)}, f32[768,768]{1,0:T(8,128)}, bf16[768,768]{1,0:T(8,128)(2,1)}, f32[768,768]{1,0:T(8,128)}, f32[768,128]{1,0:T(8,128)}) custom-call(f32[768,768]{1,0:T(8,128)} %get-tuple-element.58.refs_0_.refs_3_, bf16[2,8,768,768]{3,2,1,0:T(8,128)(2,1)} %bitcast.423, bf16[2,3072,768]{2,1,0:T(8,128)(2,1)} %bitcast.430, ...), custom_call_target="tpu_custom_call" | custom-call | tf_op jit(solution)/shard_map/mlp_fwd/pallas_call | solution.py:523
  301.0 21.3 %attn_fwd.3 = (bf16[768,2304]{1,0:T(8,128)(2,1)}, bf16[768,768]{1,0:T(8,128)(2,1)}, f32[768,128]{1,0:T(8,128)}, f32[768,768]{1,0:T(8,128)}) custom-call(f32[768,768]{1,0:T(8,128)} %get-tuple-element.60.x_ref, bf16[2,8,768,768]{3,2,1,0:T(8,128)(2,1)} %bitcast.424, f32[2,12,768]{2,1,0:T(8,128)} %copy-done.6, f32[2,384,384]{2,1,0:T(8,128)} %copy.242.mask_ref), custom_call_target="tpu_custom_call" | custom-call | tf_op jit(solution)/shard_map/attn_fwd/pallas_call | solution.py:462
  322.3 16.8 %mlp_fwd.3 = (f32[768,3072]{1,0:T(8,128)}, f32[768,768]{1,0:T(8,128)}, bf16[768,768]{1,0:T(8,128)(2,1)}, f32[768,768]{1,0:T(8,128)}, f32[768,128]{1,0:T(8,128)}) custom-call(f32[768,768]{1,0:T(8,128)} %get-tuple-element.61.refs_0_.refs_3_, bf16[2,8,768,768]{3,2,1,0:T(8,128)(2,1)} %bitcast.425, bf16[2,3072,768]{2,1,0:T(8,128)(2,1)} %bitcast.431, ...), custom_call_target="tpu_custom_call" | custom-call | tf_op jit(solution)/shard_map/mlp_fwd/pallas_call | solution.py:523
  340.1 30.4 %mlp_bwd.2 = (bf16[4,768,768]{2,1,0:T(8,128)(2,1)}, bf16[3072,768]{1,0:T(8,128)(2,1)}, f32[768,768]{1,0:T(8,128)}, f32[12,768]{1,0:T(8,128)}) custom-call(bf16[768,768]{1,0:T(8,128)(2,1)} %pad_maximum_fusion.1.refs_0_, f32[768,768]{1,0:T(8,128)} %get-tuple-element.64.refs_1_, f32[768,128]{1,0:T(8,128)} %get-tuple-element.65.refs_2_, ...), custom_call_target="tpu_custom_call" | custom-call | tf_op jit(solution)/shard_map/mlp_bwd/pallas_call | solution.py:615
  370.5 29.0 %attn_bwd.2 = (bf16[768,2304]{1,0:T(8,128)(2,1)}, f32[768,768]{1,0:T(8,128)}, bf16[768,768]{1,0:T(8,128)(2,1)}, f32[12,768]{1,0:T(8,128)}) custom-call(f32[768,768]{1,0:T(8,128)} %get-tuple-element.68.grad_ref, bf16[768,2304]{1,0:T(8,128)(2,1)} %get-tuple-element.69.qkv_ref, f32[768,128]{1,0:T(8,128)} %get-tuple-element.66.refs_4_.stat_ref, ...), custom_call_target="tpu_custom_call" | custom-call | tf_op jit(solution)/shard_map/attn_bwd/pallas_call | solution.py:705
  399.5 30.5 %mlp_bwd.3 = (bf16[4,768,768]{2,1,0:T(8,128)(2,1)}, bf16[3072,768]{1,0:T(8,128)(2,1)}, f32[768,768]{1,0:T(8,128)}, f32[12,768]{1,0:T(8,128)}) custom-call(f32[768,768]{1,0:T(8,128)} %get-tuple-element.71.refs_0_, f32[768,768]{1,0:T(8,128)} %get-tuple-element.72.refs_1_, f32[768,128]{1,0:T(8,128)} %get-tuple-element.73.refs_2_, ...), custom_call_target="tpu_custom_call" | custom-call | tf_op jit(solution)/shard_map/mlp_bwd/pallas_call | solution.py:615
  430.0 29.0 %attn_bwd.3 = (bf16[768,2304]{1,0:T(8,128)(2,1)}, f32[768,768]{1,0:T(8,128)}, bf16[768,768]{1,0:T(8,128)(2,1)}, f32[12,768]{1,0:T(8,128)}) custom-call(f32[768,768]{1,0:T(8,128)} %get-tuple-element.76.grad_ref, bf16[768,2304]{1,0:T(8,128)(2,1)} %get-tuple-element.77.qkv_ref, f32[768,128]{1,0:T(8,128)} %get-tuple-element.74.refs_4_.stat_ref, ...), custom_call_target="tpu_custom_call" | custom-call | tf_op jit(solution)/shard_map/attn_bwd/pallas_call | solution.py:705
  461.1 8.7 %attn_dw.2 = bf16[4,768,768]{2,1,0:T(8,128)(2,1)} custom-call(bf16[768,768]{1,0:T(8,128)(2,1)} %pad_maximum_fusion.x_ref.act_ref, bf16[768,2304]{1,0:T(8,128)(2,1)} %get-tuple-element.80.dqkv_ref, bf16[768,768]{1,0:T(8,128)(2,1)} %get-tuple-element.81.ctx_ref, bf16[768,768]{1,0:T(8,128)(2,1)} %get-tuple-element.82.low_ref), custom_call_target="tpu_custom_call" | custom-call | tf_op jit(solution)/shard_map/attn_dw/pallas_call | solution.py:743
  484.7 8.5 %attn_dw.3 = bf16[4,768,768]{2,1,0:T(8,128)(2,1)} custom-call(bf16[768,768]{1,0:T(8,128)(2,1)} %get-tuple-element.84.act_ref, bf16[768,2304]{1,0:T(8,128)(2,1)} %get-tuple-element.85.dqkv_ref, bf16[768,768]{1,0:T(8,128)(2,1)} %get-tuple-element.86.ctx_ref, bf16[768,768]{1,0:T(8,128)(2,1)} %get-tuple-element.87.low_ref), custom_call_target="tpu_custom_call" | custom-call | tf_op jit(solution)/shard_map/attn_dw/pallas_call | solution.py:743
  507.6 6.7 constant_dynamic-slice_fusion.4
  525.8 6.9 constant_dynamic-slice_fusion.2
  569.5 27.3 %collective-permute-done.1 = bf16[2,4,104,384]{3,2,1,0:T(8,128)(2,1)S(1)} collective-permute-done((bf16[2,4,104,384]{3,2,1,0:T(8,128)(2,1)S(1)}, bf16[2,4,104,384]{3,2,1,0:T(8,128)(2,1)S(1)}, u32[]{:S(2)}, u32[]{:S(2)}) %collective-permute-start.1) | collective-permute-done | bytes 639008 | tf_op jit(solution)/shard_map/ppermute | solution.py:53
  599.4 11.0 %collective-permute-done.12 = bf16[2,4,104,384]{3,2,1,0:T(8,128)(2,1)S(1)} collective-permute-done((bf16[2,4,104,384]{3,2,1,0:T(8,128)(2,1)S(1)}, bf16[2,4,104,384]{3,2,1,0:T(8,128)(2,1)S(1)}, u32[]{:S(2)}, u32[]{:S(2)}) %collective-permute-start.12) | collective-permute-done | bytes 639008 | tf_op jit(solution)/shard_map/ppermute | solution.py:53
  614.8 6.1 collective-permute-done.2
  628.4 5.2 collective-permute-start.5
  652.5 33.0 %collective-permute-done.14 = bf16[104,384]{1,0:T(8,128)(2,1)S(1)} collective-permute-done((bf16[104,384]{1,0:T(8,128)(2,1)}, bf16[104,384]{1,0:T(8,128)(2,1)S(1)}, u32[]{:S(2)}, u32[]{:S(2)}) %collective-permute-start.14) | collective-permute-done | bytes 79904 | tf_op jit(solution)/shard_map/ppermute | solution.py:53
  685.4 13.2 %collective-permute-start.19 = (bf16[104,384]{1,0:T(8,128)(2,1)}, bf16[104,384]{1,0:T(8,128)(2,1)S(1)}, u32[]{:S(2)}, u32[]{:S(2)}) collective-permute-start(bf16[104,384]{1,0:T(8,128)(2,1)} %get-tuple-element.170), channel_id=1, source_target_pairs={{0,2},{1,3},{2,4},{3,5},{4,6},{5,7},{6,0},{7,1},{8,10},{9,11},{10,... | collective-permute-start | bytes 239624 | tf_op jit(solution)/shard_map/ppermute | solution.py:53
  725.7 5.3 fusion.1
  743.9 17.2 %collective-permute-done.23 = bf16[2,4,192,384]{3,2,1,0:T(8,128)(2,1)} collective-permute-done((bf16[2,4,192,384]{3,2,1,0:T(8,128)(2,1)S(1)}, bf16[2,4,192,384]{3,2,1,0:T(8,128)(2,1)}, u32[]{:S(2)}, u32[]{:S(2)}) %collective-permute-start.23) | collective-permute-done | bytes 1179680 | tf_op jit(solution)/shard_map/ppermute | solution.py:53
  765.0 21.2 %collective-permute-done.34 = bf16[2,4,192,384]{3,2,1,0:T(8,128)(2,1)S(1)} collective-permute-done((bf16[2,4,192,384]{3,2,1,0:T(8,128)(2,1)S(1)}, bf16[2,4,192,384]{3,2,1,0:T(8,128)(2,1)S(1)}, u32[]{:S(2)}, u32[]{:S(2)}) %collective-permute-start.34) | collective-permute-done | bytes 1179680 | tf_op jit(solution)/shard_map/ppermute | solution.py:53
  788.9 10.2 %collective-permute-done.24 = bf16[4,192,384]{2,1,0:T(8,128)(2,1)S(1)} collective-permute-done((bf16[4,192,384]{2,1,0:T(8,128)(2,1)S(1)}, bf16[4,192,384]{2,1,0:T(8,128)(2,1)S(1)}, u32[]{:S(2)}, u32[]{:S(2)}) %collective-permute-start.24) | collective-permute-done | bytes 589856 | tf_op jit(solution)/shard_map/ppermute | solution.py:53
  816.0 8.5 %collective-permute-start.37 = (bf16[192,384]{1,0:T(8,128)(2,1)S(1)}, bf16[192,384]{1,0:T(8,128)(2,1)S(1)}, u32[]{:S(2)}, u32[]{:S(2)}) collective-permute-start(bf16[192,384]{1,0:T(8,128)(2,1)S(1)} %get-tuple-element.152), channel_id=1, source_target_pairs={{0,4},{1,5},{2,6},{3,7},{4,0},{5,1},{6,2},{7,3},{8,12},{9,13},{10,... | collective-permute-start | bytes 442376 | tf_op jit(solution)/shard_map/ppermute | solution.py:53
  (406 shorter events, 233.3 us)
Async XLA Ops:
  483.8 75.9 %collective-permute-start = (bf16[2,4,2,104,768]{4,3,1,2,0:T(8,128)(2,1)}, bf16[2,4,2,104,768]{4,3,1,2,0:T(8,128)(2,1)}, u32[]{:S(2)}, u32[]{:S(2)}) collective-permute-start(bf16[2,4,2,104,768]{4,3,1,2,0:T(8,128)(2,1)} %bitcast.417), channel_id=1, source_target_pairs={{0,8},{1,9},{2,10},{3,11},{4,12},{5,13},{6,14},{7,15},{8,0},{9,1},... | collective-permute-start | bytes 7667720 | tf_op jit(solution)/shard_map/ppermute | solution.py:53
  499.8 65.9 %collective-permute-start.11 = (bf16[2,4,2,104,768]{4,3,1,2,0:T(8,128)(2,1)}, bf16[2,4,2,104,768]{4,3,1,2,0:T(8,128)(2,1)}, u32[]{:S(2)}, u32[]{:S(2)}) collective-permute-start(bf16[2,4,2,104,768]{4,3,1,2,0:T(8,128)(2,1)} %bitcast.416), channel_id=1, source_target_pairs={{0,8},{1,9},{2,10},{3,11},{4,12},{5,13},{6,14},{7,15},{8,0},{9,1},... | collective-permute-start | bytes 7667720 | tf_op jit(solution)/shard_map/ppermute | solution.py:53
  517.0 208.7 %collective-permute-start.22 = (bf16[2,4,2,192,768]{4,3,1,2,0:T(8,128)(2,1)}, bf16[2,4,2,192,768]{4,3,1,2,0:T(8,128)(2,1)}, u32[]{:S(2)}, u32[]{:S(2)}) collective-permute-start(bf16[2,4,2,192,768]{4,3,1,2,0:T(8,128)(2,1)} %bitcast.415), channel_id=1, source_target_pairs={{0,8},{1,9},{2,10},{3,11},{4,12},{5,13},{6,14},{7,15},{8,0},{9,1},... | collective-permute-start | bytes 14155784 | tf_op jit(solution)/shard_map/ppermute | solution.py:53
  535.2 197.7 %collective-permute-start.33 = (bf16[2,4,2,192,768]{4,3,1,2,0:T(8,128)(2,1)}, bf16[2,4,2,192,768]{4,3,1,2,0:T(8,128)(2,1)}, u32[]{:S(2)}, u32[]{:S(2)}) collective-permute-start(bf16[2,4,2,192,768]{4,3,1,2,0:T(8,128)(2,1)} %bitcast.414), channel_id=1, source_target_pairs={{0,8},{1,9},{2,10},{3,11},{4,12},{5,13},{6,14},{7,15},{8,0},{9,1},... | collective-permute-start | bytes 14155784 | tf_op jit(solution)/shard_map/ppermute | solution.py:53
  550.3 87.6 %all-to-all-start = ((bf16[2,1,2,384,768]{4,2,0,1,3:T(2,128)(2,1)}), bf16[2,1,2,384,768]{4,2,0,1,3:T(2,128)(2,1)S(1)}, u32[]{:S(2)}, u32[]{:S(2)}) async-start(bf16[2,1,2,384,768]{4,2,0,1,3:T(2,128)(2,1)} %copy.244), calls=%async_computation | async-start | bytes 4718592 | tf_op jit(solution)/shard_map/all_to_all | solution.py:909
  563.1 33.7 %collective-permute-start.1 = (bf16[2,4,104,384]{3,2,1,0:T(8,128)(2,1)S(1)}, bf16[2,4,104,384]{3,2,1,0:T(8,128)(2,1)S(1)}, u32[]{:S(2)}, u32[]{:S(2)}) collective-permute-start(bf16[2,4,104,384]{3,2,1,0:T(8,128)(2,1)S(1)} %dynamic-slice_bitcast_fusion.7), channel_id=1, source_target_pairs={{0,1},{1,0},{2,3},{3,2},{4,5},{5,4},{6,7},{7,6},{8,9},{9,8},{10,11... | collective-permute-start | bytes 1916936 | tf_op jit(solution)/shard_map/ppermute | solution.py:53
  565.0 32.6 %collective-permute-start.6 = (bf16[4,2,104,384]{3,2,0,1:T(8,128)(2,1)S(1)}, bf16[4,2,104,384]{3,2,0,1:T(8,128)(2,1)S(1)}, u32[]{:S(2)}, u32[]{:S(2)}) collective-permute-start(bf16[4,2,104,384]{3,2,0,1:T(8,128)(2,1)S(1)} %dynamic-slice_bitcast_fusion.6), channel_id=1, source_target_pairs={{0,16},{1,17},{2,18},{3,19},{4,20},{5,21},{6,22},{7,23},{8,24},{9,... | collective-permute-start | bytes 1916936 | tf_op jit(solution)/shard_map/ppermute | solution.py:53
  568.5 42.0 %collective-permute-start.12 = (bf16[2,4,104,384]{3,2,1,0:T(8,128)(2,1)S(1)}, bf16[2,4,104,384]{3,2,1,0:T(8,128)(2,1)S(1)}, u32[]{:S(2)}, u32[]{:S(2)}) collective-permute-start(bf16[2,4,104,384]{3,2,1,0:T(8,128)(2,1)S(1)} %dynamic-slice_bitcast_fusion.5), channel_id=1, source_target_pairs={{0,1},{1,0},{2,3},{3,2},{4,5},{5,4},{6,7},{7,6},{8,9},{9,8},{10,11... | collective-permute-start | bytes 1916936 | tf_op jit(solution)/shard_map/ppermute | solution.py:53
  597.6 23.3 %collective-permute-start.2 = (bf16[4,104,384]{2,1,0:T(8,128)(2,1)S(1)}, bf16[4,104,384]{2,1,0:T(8,128)(2,1)S(1)}, u32[]{:S(2)}, u32[]{:S(2)}) collective-permute-start(bf16[4,104,384]{2,1,0:T(8,128)(2,1)S(1)} %dynamic-slice_bitcast_fusion.15), channel_id=1, source_target_pairs={{0,16},{1,17},{2,18},{3,19},{4,20},{5,21},{6,22},{7,23},{8,24},{9,... | collective-permute-start | bytes 958472 | tf_op jit(solution)/shard_map/ppermute | solution.py:53
  637.9 78.3 %all-to-all-start.1 = ((bf16[2,1,2,384,768]{4,2,0,1,3:T(2,128)(2,1)}), bf16[2,1,2,384,768]{4,2,0,1,3:T(2,128)(2,1)}, u32[]{:S(2)}, u32[]{:S(2)}) async-start(bf16[2,1,2,384,768]{4,2,0,1,3:T(2,128)(2,1)} %copy.249), calls=%async_computation.1 | async-start | bytes 4718592 | tf_op jit(solution)/shard_map/all_to_all | solution.py:909
  642.3 43.1 %collective-permute-start.14 = (bf16[104,384]{1,0:T(8,128)(2,1)}, bf16[104,384]{1,0:T(8,128)(2,1)S(1)}, u32[]{:S(2)}, u32[]{:S(2)}) collective-permute-start(bf16[104,384]{1,0:T(8,128)(2,1)} %get-tuple-element.173), channel_id=1, source_target_pairs={{0,2},{1,3},{2,4},{3,5},{4,6},{5,7},{6,0},{7,1},{8,10},{9,11},{10,... | collective-permute-start | bytes 239624 | tf_op jit(solution)/shard_map/ppermute | solution.py:53
  645.3 57.9 %collective-permute-start.15 = (bf16[104,384]{1,0:T(8,128)(2,1)}, bf16[104,384]{1,0:T(8,128)(2,1)S(1)}, u32[]{:S(2)}, u32[]{:S(2)}) collective-permute-start(bf16[104,384]{1,0:T(8,128)(2,1)} %get-tuple-element.175), channel_id=1, source_target_pairs={{0,4},{1,5},{2,6},{3,7},{4,0},{5,1},{6,2},{7,3},{8,12},{9,13},{10,... | collective-permute-start | bytes 239624 | tf_op jit(solution)/shard_map/ppermute | solution.py:53
  647.1 56.0 %collective-permute-start.16 = (bf16[104,384]{1,0:T(8,128)(2,1)}, bf16[104,384]{1,0:T(8,128)(2,1)S(1)}, u32[]{:S(2)}, u32[]{:S(2)}) collective-permute-start(bf16[104,384]{1,0:T(8,128)(2,1)} %get-tuple-element.174), channel_id=1, source_target_pairs={{0,6},{1,7},{2,0},{3,1},{4,2},{5,3},{6,4},{7,5},{8,14},{9,15},{10,... | collective-permute-start | bytes 239624 | tf_op jit(solution)/shard_map/ppermute | solution.py:53
  732.0 29.0 %collective-permute-start.23 = (bf16[2,4,192,384]{3,2,1,0:T(8,128)(2,1)S(1)}, bf16[2,4,192,384]{3,2,1,0:T(8,128)(2,1)}, u32[]{:S(2)}, u32[]{:S(2)}) collective-permute-start(bf16[2,4,192,384]{3,2,1,0:T(8,128)(2,1)S(1)} %dynamic-slice_bitcast_fusion.3), channel_id=1, source_target_pairs={{0,1},{1,0},{2,3},{3,2},{4,5},{5,4},{6,7},{7,6},{8,9},{9,8},{10,11... | collective-permute-start | bytes 3538952 | tf_op jit(solution)/shard_map/ppermute | solution.py:53
  732.3 31.0 %collective-permute-start.28 = (bf16[4,2,192,384]{3,2,0,1:T(8,128)(2,1)S(1)}, bf16[4,2,192,384]{3,2,0,1:T(8,128)(2,1)}, u32[]{:S(2)}, u32[]{:S(2)}) collective-permute-start(bf16[4,2,192,384]{3,2,0,1:T(8,128)(2,1)S(1)} %dynamic-slice_bitcast_fusion.2), channel_id=1, source_target_pairs={{0,16},{1,17},{2,18},{3,19},{4,20},{5,21},{6,22},{7,23},{8,24},{9,... | collective-permute-start | bytes 3538952 | tf_op jit(solution)/shard_map/ppermute | solution.py:53
  737.5 48.8 %collective-permute-start.34 = (bf16[2,4,192,384]{3,2,1,0:T(8,128)(2,1)S(1)}, bf16[2,4,192,384]{3,2,1,0:T(8,128)(2,1)S(1)}, u32[]{:S(2)}, u32[]{:S(2)}) collective-permute-start(bf16[2,4,192,384]{3,2,1,0:T(8,128)(2,1)S(1)} %dynamic-slice_bitcast_fusion.1), channel_id=1, source_target_pairs={{0,1},{1,0},{2,3},{3,2},{4,5},{5,4},{6,7},{7,6},{8,9},{9,8},{10,11... | collective-permute-start | bytes 3538952 | tf_op jit(solution)/shard_map/ppermute | solution.py:53
  742.3 44.9 %collective-permute-start.39 = (bf16[4,2,192,384]{3,2,0,1:T(8,128)(2,1)S(1)}, bf16[4,2,192,384]{3,2,0,1:T(8,128)(2,1)S(1)}, u32[]{:S(2)}, u32[]{:S(2)}) collective-permute-start(bf16[4,2,192,384]{3,2,0,1:T(8,128)(2,1)S(1)} %dynamic-slice_bitcast_fusion), channel_id=1, source_target_pairs={{0,16},{1,17},{2,18},{3,19},{4,20},{5,21},{6,22},{7,23},{8,24},{9,... | collective-permute-start | bytes 3538952 | tf_op jit(solution)/shard_map/ppermute | solution.py:53
  762.7 36.4 %collective-permute-start.24 = (bf16[4,192,384]{2,1,0:T(8,128)(2,1)S(1)}, bf16[4,192,384]{2,1,0:T(8,128)(2,1)S(1)}, u32[]{:S(2)}, u32[]{:S(2)}) collective-permute-start(bf16[4,192,384]{2,1,0:T(8,128)(2,1)S(1)} %dynamic-slice_bitcast_fusion.11), channel_id=1, source_target_pairs={{0,16},{1,17},{2,18},{3,19},{4,20},{5,21},{6,22},{7,23},{8,24},{9,... | collective-permute-start | bytes 1769480 | tf_op jit(solution)/shard_map/ppermute | solution.py:53
  765.0 37.4 %collective-permute-start.29 = (bf16[4,192,384]{2,1,0:T(8,128)(2,1)S(1)}, bf16[4,192,384]{2,1,0:T(8,128)(2,1)S(1)}, u32[]{:S(2)}, u32[]{:S(2)}) collective-permute-start(bf16[4,192,384]{2,1,0:T(8,128)(2,1)S(1)} %dynamic-slice_bitcast_fusion.10), channel_id=1, source_target_pairs={{0,1},{1,0},{2,3},{3,2},{4,5},{5,4},{6,7},{7,6},{8,9},{9,8},{10,11... | collective-permute-start | bytes 1769480 | tf_op jit(solution)/shard_map/ppermute | solution.py:53
  786.6 20.1 %collective-permute-start.35 = (bf16[4,192,384]{2,1,0:T(8,128)(2,1)S(1)}, bf16[4,192,384]{2,1,0:T(8,128)(2,1)S(1)}, u32[]{:S(2)}, u32[]{:S(2)}) collective-permute-start(bf16[4,192,384]{2,1,0:T(8,128)(2,1)S(1)} %dynamic-slice_bitcast_fusion.9), channel_id=1, source_target_pairs={{0,16},{1,17},{2,18},{3,19},{4,20},{5,21},{6,22},{7,23},{8,24},{9,... | collective-permute-start | bytes 1769480 | tf_op jit(solution)/shard_map/ppermute | solution.py:53
  787.6 21.3 %collective-permute-start.40 = (bf16[4,192,384]{2,1,0:T(8,128)(2,1)S(1)}, bf16[4,192,384]{2,1,0:T(8,128)(2,1)S(1)}, u32[]{:S(2)}, u32[]{:S(2)}) collective-permute-start(bf16[4,192,384]{2,1,0:T(8,128)(2,1)S(1)} %dynamic-slice_bitcast_fusion.8), channel_id=1, source_target_pairs={{0,1},{1,0},{2,3},{3,2},{4,5},{5,4},{6,7},{7,6},{8,9},{9,8},{10,11... | collective-permute-start | bytes 1769480 | tf_op jit(solution)/shard_map/ppermute | solution.py:53
  808.9 24.1 %collective-permute-start.31 = (bf16[192,384]{1,0:T(8,128)(2,1)S(1)}, bf16[192,384]{1,0:T(8,128)(2,1)S(1)}, u32[]{:S(2)}, u32[]{:S(2)}) collective-permute-start(bf16[192,384]{1,0:T(8,128)(2,1)S(1)} %get-tuple-element.149), channel_id=1, source_target_pairs={{0,4},{1,5},{2,6},{3,7},{4,0},{5,1},{6,2},{7,3},{8,12},{9,13},{10,... | collective-permute-start | bytes 442376 | tf_op jit(solution)/shard_map/ppermute | solution.py:53
  811.6 21.4 %collective-permute-start.32 = (bf16[192,384]{1,0:T(8,128)(2,1)S(1)}, bf16[192,384]{1,0:T(8,128)(2,1)S(1)}, u32[]{:S(2)}, u32[]{:S(2)}) collective-permute-start(bf16[192,384]{1,0:T(8,128)(2,1)S(1)} %get-tuple-element.148), channel_id=1, source_target_pairs={{0,6},{1,7},{2,0},{3,1},{4,2},{5,3},{6,4},{7,5},{8,14},{9,15},{10,... | collective-permute-start | bytes 442376 | tf_op jit(solution)/shard_map/ppermute | solution.py:53
  816.0 26.5 %collective-permute-start.37 = (bf16[192,384]{1,0:T(8,128)(2,1)S(1)}, bf16[192,384]{1,0:T(8,128)(2,1)S(1)}, u32[]{:S(2)}, u32[]{:S(2)}) collective-permute-start(bf16[192,384]{1,0:T(8,128)(2,1)S(1)} %get-tuple-element.152), channel_id=1, source_target_pairs={{0,4},{1,5},{2,6},{3,7},{4,0},{5,1},{6,2},{7,3},{8,12},{9,13},{10,... | collective-permute-start | bytes 442376 | tf_op jit(solution)/shard_map/ppermute | solution.py:53
  (66 other events, 443.8 us)

commit v2 on v1

--- a/solution.py
+++ b/solution.py
@@ -13,6 +13,7 @@
 AXES = ("dp", "fsdp")
 NEG = -1000000000.0
 HEAD_DIM = 64
+VMEM_BYTES = 67043328
 
 
 epsilon = 1e-06
@@ -33,24 +34,6 @@
         self.at = (dp_at // CORES, dp_at % CORES, fsdp_at // inner, fsdp_at % inner)
 
         self.count = dp_count * fsdp_count
-
-    def index(self, place):
-        total = 0
-        for size, at in zip(self.sizes, place):
-            total = total * size + at
-        return total
-
-    def send(self, array, axis, offset):
-        pairs = []
-        sizes = self.sizes
-        for flat in range(sizes[0] * sizes[1] * sizes[2] * sizes[3]):
-            place, rest = [], flat
-            for size in reversed(sizes):
-                place.insert(0, rest % size)
-                rest //= size
-            place[axis] = (place[axis] + offset) % sizes[axis]
-            pairs.append((flat, self.index(place)))
-        return lax.ppermute(array, AXES, pairs)
 
 
 ALL = slice(None)
@@ -224,33 +207,29 @@
 
 
 def bring_kernel(sizes, *refs):
-    sent_x, sent_grad, square, down, small = refs[:5]
-    got_x, got_grad, all_square, all_down, all_small = refs[5:10]
-    links = Links(sizes, *refs[10:])
+    sent_x, square, down, small = refs[:4]
+    got_x, all_square, all_down, all_small = refs[4:8]
+    links = Links(sizes, *refs[8:])
     links.greet(links.partners())
     groups = []
     for layer_at in range(LAYERS):
         groups += gathers_of(
             links, layer_at, square, down, small, all_square, all_down, all_small
         )
-    for at, group in enumerate(groups):
+    for group in groups:
         for item in group:
             item.begin()
-        if at == 2:
-            moved = deal_out(links, sent_x, got_x)
-    moved += deal_out(links, sent_grad, got_grad)
-    for at in range(len(groups) + 1):
-        if at > 0:
-            for item in groups[at - 1]:
-                item.second()
+    moved = deal_out(links, sent_x, got_x)
+    for at in range(len(groups) + 2):
         if at < len(groups):
             for item in groups[at]:
                 item.first()
+        if 0 < at <= len(groups):
+            for item in groups[at - 1]:
+                item.second()
         if at > 1:
             for item in groups[at - 2]:
                 item.third()
-    for item in groups[-1]:
-        item.third()
     for group in groups:
         for item in group:
             item.end()
@@ -258,85 +237,277 @@
         copy.wait()
 
 
-def bring(sizes, sent_x, sent_grad, square, down, small):
+def bring(sizes, sent_x, square, down, small):
     low = jnp.bfloat16
     batch, members, two, rows, width = sent_x.shape
     r = square.shape[2]
     got = jax.ShapeDtypeStruct((batch, two, members, rows, width), low)
     outs = [
         got,
-        got,
         jax.ShapeDtypeStruct((LAYERS, square.shape[1]) + sizes + (r, width), low),
         jax.ShapeDtypeStruct((LAYERS,) + sizes + (down.shape[1], r, width), low),
         jax.ShapeDtypeStruct((LAYERS,) + sizes + (8, width), low),
     ]
     per_item = 1 + sum(n - 1 for n in sizes) + 4 + sizes[0] + sizes[3]
-    count = 7 * LAYERS * per_item + 2 * members
+    count = 7 * LAYERS * per_item + members
     return pl.pallas_call(
         lambda *refs: bring_kernel(sizes, *refs),
         out_shape=outs,
-        in_specs=[HBM] * 5,
-        out_specs=[HBM] * 5,
+        in_specs=[HBM] * 4,
+        out_specs=[HBM] * 4,
         scratch_shapes=[pltpu.SemaphoreType.DMA((count,)), pltpu.SemaphoreType.DMA((count,))],
         compiler_params=pltpu.CompilerParams(collective_id=0, has_side_effects=True),
         name="bring",
-    )(sent_x, sent_grad, square, down, small)
-
-
-def pick(array, at, axis):
-    return lax.dynamic_index_in_dim(array, at, axis, keepdims=False)
-
-
-def gather_rows(grid, rows):
-    count, width = rows.shape
-    half = width // 2
-    xs, cs, outs, ins = grid.sizes
-    x, c, o, i = grid.at
-    column = jnp.zeros((outs, count, width), rows.dtype)
-    for step in range(outs):
-        piece = rows if step == 0 else grid.send(rows, 2, step)
-        column = lax.dynamic_update_slice(column, piece[None], ((o - step) % outs, 0, 0))
-    pieces = {}
-    for side, (first, second) in enumerate(((0, 3), (3, 0))):
-        start = column[:, :, side * half : (side + 1) * half]
-        line = [start] + [grid.send(start, first, k) for k in range(1, grid.sizes[first])]
-        for far, piece in enumerate(line):
-            for near in range(grid.sizes[second]):
-                moved = piece if near == 0 else grid.send(piece, second, near)
-                kx, ki = (far, near) if first == 0 else (near, far)
-                pieces[side, kx, ki, 0] = moved
-    for (side, kx, ki, unused), piece in list(pieces.items()):
-        pieces[side, kx, ki, 1] = grid.send(piece, 1, 1)
-    whole = jnp.zeros((xs, cs, outs, ins, count, width), rows.dtype)
-    for (side, kx, ki, kc), piece in pieces.items():
-        place = ((x - kx) % xs, (c - kc) % cs, 0, (i - ki) % ins, 0, side * half)
-        whole = lax.dynamic_update_slice(whole, piece[None, None, :, None], place)
-    return whole
-
-
-def scatter_rows(grid, whole):
-    width = whole.shape[-1]
-    half = width // 2
-    low = whole.dtype
-    x, c, o, i = grid.at
-    here = pick(whole, c, 1).astype(jnp.float32)
-    there = grid.send(pick(whole, 1 - c, 1), 1, 1).astype(jnp.float32)
-    both = (here + there).astype(low)
-    sides = []
-    for side, order in enumerate(((3, 0), (0, 3))):
-        part = both[..., side * half : (side + 1) * half]
-        left = [0, 2, 3]
-        for axis in order + (2,):
-            at = left.index(axis)
-            left.remove(axis)
-            mine = grid.at[axis]
-            size = grid.sizes[axis]
-            total = pick(part, mine, at).astype(jnp.float32)
-            for k in range(1, size):
-                total = total + grid.send(pick(part, (mine + k) % size, at), axis, k).astype(jnp.float32)
-            part = total if axis == 2 else total.astype(low)
-        sides.append(part)
-    return jnp.concatenate(sides, axis=-1)
+    )(sent_x, square, down, small)
+
+
+def each(dims, body):
+    total = 1
+    for n in dims:
+        total *= n
+
+    def step(flat, carry):
+        at = []
+        for n in reversed(dims):
+            at.insert(0, flat % n)
+            flat = flat // n
+        body(tuple(at))
+        return carry
+
+    lax.fori_loop(0, total, step, 0)
+
+
+def wide(ref, at):
+    return ref[at].astype(jnp.float32)
+
+
+class Sum:
+    def __init__(self, links, source, order, lead, bufs, out_ref):
+        self.links, self.source, self.order, self.lead = links, source, order, lead
+        self.mine, self.theirs, self.first, self.half, self.second, self.quarter, self.last, self.out = bufs
+        self.out_ref = out_ref
+        self.sent = []
+
+    def send(self, source, target, axis, offset):
+        copy = self.links.start(source, target, self.links.along(axis, offset))
+        self.sent.append(copy)
+        return copy
+
+    def begin(self):
+        c = self.links.at[1]
+        self.here = self.links.start_here(self.source(c), self.mine)
+        self.there = self.send(self.source(1 - c), self.theirs, 1, 1)
+
+    def at(self, *place):
+        return (ALL,) * self.lead + place
+
+    def spread(self, ref, axes, axis, into):
+        size, me = self.links.sizes[axis], self.links.at[axis]
+        found = []
+        for k in range(1, size):
+            place = [ALL] * len(axes)
+            place[axes.index(axis)] = (me + k) % size
+            found.append(self.send(ref.at[self.at(*place)], into.at[k - 1], axis, k))
+        return found
+
+    def fold(self, ref, axes, axis, arrived, into):
+        size, me = self.links.sizes[axis], self.links.at[axis]
+        spot = axes.index(axis) + self.lead
+
+        def add(at):
+            total = wide(ref, at[:spot] + (me,) + at[spot:])
+            for k in range(size - 1):
+                total = total + wide(arrived, (k,) + at)
+            into[at] = total.astype(into.dtype)
+
+        each(into.shape[:-2], add)
+
+    def stage_one(self):
+        self.here.wait()
+        self.there.wait_recv()
+
+        def add(at):
+            self.mine[at] = (wide(self.mine, at) + wide(self.theirs, at)).astype(LOW)
+
+        each(self.mine.shape[:-2], add)
+        self.moving = self.spread(self.mine, (0, 2, 3), self.order[0], self.first)
+
+    def stage_two(self):
+        for copy in self.moving:
+            copy.wait_recv()
+        self.fold(self.mine, (0, 2, 3), self.order[0], self.first, self.half)
+        axes = (2, 3) if self.order[0] == 0 else (0, 2)
+        self.moving = self.spread(self.half, axes, self.order[1], self.second)
+
+    def stage_three(self):
+        for copy in self.moving:
+            copy.wait_recv()
+        axes = (2, 3) if self.order[0] == 0 else (0, 2)
+        self.fold(self.half, axes, self.order[1], self.second, self.quarter)
+        self.moving = self.spread(self.quarter, (2,), 2, self.last)
+
+    def stage_four(self):
+        for copy in self.moving:
+            copy.wait_recv()
+        self.fold(self.quarter, (2,), 2, self.last, self.out)
+        self.result = self.links.start_here(self.out, self.out_ref)
+
+    def end(self):
+        self.result.wait()
+        for copy in self.sent:
+            copy.wait_send()
+
+
+class Whole:
+    def __init__(self, links, source, bufs, out_ref):
+        self.links, self.source, self.out_ref = links, source, out_ref
+        self.held, self.arrived = bufs[:5], bufs[5:]
+        self.sent = []
+
+    def begin(self):
+        self.here = self.links.start_here(self.source, self.held[0])
+
+    def send(self, at, axis):
+        self.moving = [
+            self.links.start(
+                self.held[at], self.arrived[at].at[k - 1], self.links.along(axis, k)
+            )
+            for k in range(1, self.links.sizes[axis])
+        ]
+        self.sent += self.moving
+
+    def fold(self, at):
+        for copy in self.moving:
+            copy.wait_recv()
+        total = self.held[at][...]
+        for k in range(self.arrived[at].shape[0]):
+            total = total + self.arrived[at][k]
+        self.held[at + 1][...] = total
+
+    def stage_one(self):
+        self.here.wait()
+        self.send(0, 1)
+
+    def stage_two(self):
+        self.fold(0)
+        self.send(1, 0)
+
+    def stage_three(self):
+        self.fold(1)
+        self.send(2, 3)
+
+    def stage_four(self):
+        self.fold(2)
+        self.send(3, 2)
+
+    def end(self):
+        self.fold(3)
+        result = self.links.start_here(self.held[4], self.out_ref)
+        result.wait()
+        for copy in self.sent:
+            copy.wait_send()
+
+
+def whole_buffers(sizes, shape):
+    f32 = jnp.float32
+    arrived = [pltpu.VMEM((sizes[axis] - 1,) + shape, f32) for axis in (1, 0, 3, 2)]
+    return [pltpu.VMEM(shape, f32)] * 5 + arrived
+
+
+def sum_buffers(sizes, order, lead, tail):
+    x, c, o, i = sizes
+    whole = lead + (x, o, i) + tail
+    half = lead + ((x, o) if order[0] == 3 else (o, i)) + tail
+    quarter = lead + (o,) + tail
+    low = [
+        whole,
+        whole,
+        (sizes[order[0]] - 1,) + half,
+        half,
+        (sizes[order[1]] - 1,) + quarter,
+        quarter,
+        (o - 1,) + lead + tail,
+    ]
+    return [pltpu.VMEM(shape, LOW) for shape in low] + [pltpu.VMEM(lead + tail, jnp.float32)]
+
+
+def home_kernel(sizes, layouts, *refs):
+    inputs, refs = refs[: 3 * LAYERS], refs[3 * LAYERS :]
+    vec, sent, g_square, g_down, g_vec, back = refs[:6]
+    links = Links(sizes, *refs[6:8])
+    whole = Whole(links, vec, refs[8:17], g_vec)
+    refs = refs[17:]
+    links.greet(links.partners())
+    sums = []
+    for layer_at, kind, start, order, lead, tail in layouts:
+        dws, dwu, dwd = inputs[3 * layer_at : 3 * layer_at + 3]
+        bufs, refs = refs[:8], refs[8:]
+        blocks = slice(start, start + 2)
+        if kind == "down":
+            source = lambda core, blocks=blocks, dwd=dwd: dwd.at[:, core, :, :, blocks]
+            out = g_down.at[layer_at, blocks]
+        else:
+            array = dws if kind == "attn" else dwu
+            source = lambda core, blocks=blocks, array=array: array.at[blocks, :, core]
+            out = g_square.at[layer_at, blocks if kind == "attn" else slice(start + 4, start + 6)]
+        sums.append(Sum(links, source, order, len(lead), bufs, out))
+    groups = [sums[at : at + 2] for at in range(0, len(sums), 2)]
+    groups[0].append(whole)
+    sums.append(whole)
+    for group in groups:
+        for item in group:
+            item.begin()
+    moved = deal_back(links, sent, back)
+    stages = ("stage_one", "stage_two", "stage_three", "stage_four")
+    for turn in range(len(groups) + len(stages) - 1):
+        for depth in range(len(stages)):
+            if 0 <= turn - depth < len(groups):
+                for item in groups[turn - depth]:
+                    getattr(item, stages[depth])()
+    for item in sums:
+        item.end()
+    for copy in moved:
+        copy.wait()
+
+
+def take_home(sizes, grads, vec, sent):
+    r, width = grads[0][0].shape[-2:]
+    tail = (r, width)
+    y_first, x_first = (3, 0), (0, 3)
+    layouts = []
+    for layer_at in reversed(range(LAYERS)):
+        for kind in ("down", "up", "attn"):
+            lead, piece = ((), (2,) + tail) if kind == "down" else ((2,), tail)
+            layouts += [
+                (layer_at, kind, 0, y_first, lead, piece),
+                (layer_at, kind, 2, x_first, lead, piece),
+            ]
+    members = sizes[2] * sizes[3]
+    f32 = jnp.float32
+    batch, two, count, rows = sent.shape[:4]
+    outs = [
+        jax.ShapeDtypeStruct((LAYERS, 8, r, width), f32),
+        jax.ShapeDtypeStruct((LAYERS, 4, r, width), f32),
+        jax.ShapeDtypeStruct(vec.shape, f32),
+        jax.ShapeDtypeStruct((batch, count, two, rows, width), LOW),
+    ]
+    args = [array for group in grads for array in group] + [vec, sent]
+    scratch = whole_buffers(sizes, vec.shape)
+    for layer_at, kind, start, order, lead, piece in layouts:
+        scratch += sum_buffers(sizes, order, lead, piece)
+    count = (len(layouts) + 1) * (3 + sum(n - 1 for n in sizes)) + members
+    sems = [pltpu.SemaphoreType.DMA((count,)), pltpu.SemaphoreType.DMA((count,))]
+    return pl.pallas_call(
+        lambda *refs: home_kernel(sizes, layouts, *refs),
+        out_shape=outs,
+        in_specs=[HBM] * len(args),
+        out_specs=[HBM] * len(outs),
+        scratch_shapes=sems + scratch,
+        compiler_params=pltpu.CompilerParams(
+            collective_id=1, has_side_effects=True, vmem_limit_bytes=VMEM_BYTES
+        ),
+        name="take_home",
+    )(*args)
 
 
 def bin_mask(first_blocks, second_blocks, random_pair):
@@ -758,24 +929,6 @@
 SMALL = ("bq", "bv", "bo", "ga", "ba", "bd", "gf", "bf", "bu")
 
 
-def pack_attn(p, layer_at):
-    wq = p["wqkv"][layer_at]
-    rows, width = p["wo"][layer_at].shape
-    small = jnp.concatenate([p[name][layer_at] for name in SMALL])
-    pad = 8 * width - small.shape[0]
-    small = jnp.pad(small, (0, pad)).reshape(8, width)
-    parts = [wq[:, j * width : (j + 1) * width] for j in range(3)] + [p["wo"][layer_at], small]
-    return jnp.concatenate(parts, axis=0)
-
-
-def pack_mlp(p, layer_at):
-    width = p["wd"].shape[-1]
-    wu = p["wu"][layer_at]
-    count = wu.shape[1] // width
-    parts = [wu[:, j * width : (j + 1) * width] for j in range(count)] + [p["wd"][layer_at]]
-    return jnp.concatenate(parts, axis=0)
-
-
 def small_rows(p, layer_at, width):
     small = jnp.concatenate([p[name][layer_at] for name in SMALL])
     return jnp.pad(small, (0, 8 * width - small.shape[0])).reshape(8, width)
@@ -787,11 +940,6 @@
     even = flat[:, :, : 8 * rows].reshape(layers, -1, 8, rows).transpose(0, 2, 1, 3)
     up = flat[:, :, 8 * rows : 12 * rows]
     return jnp.concatenate([even.reshape(layers, 8, width), up.reshape(layers, 4, width)], axis=1)
-
-
-def small_of(vec, rows):
-    even = vec[:BU].reshape(BU, -1, rows).transpose(1, 0, 2).reshape(-1, BU * rows)
-    return jnp.concatenate([even, vec[BU:].reshape(even.shape[0], -1)], axis=1)
 
 
 def forward(hidden, act_in, w, mask, layer_at):
@@ -811,22 +959,11 @@
     return grad_in, (attn_dw(act_in, dqkv, ctx, low_a), dwu, dwd, vec)
 
 
-def whole_attn(grid, square, vec, rows):
-    width = square.shape[-1]
-    shape = grid.sizes
-    small = small_of(vec, rows)
-    small = jnp.pad(small, ((0, 0), (0, 8 * width - small.shape[1])))
-    parts = [square[j].reshape(shape + (rows, width)) for j in range(4)]
-    parts.append(small.astype(LOW).reshape(shape + (8, width)))
-    return jnp.concatenate(parts, axis=-2)
-
-
-def whole_mlp(grid, dwu, dwd, rows):
+def to_send(sizes, grads, rows):
+    dws, dwu, dwd = grads
     width = dwd.shape[-1]
-    shape = grid.sizes
-    parts = [dwu[j].reshape(shape + (rows, width)) for j in range(dwu.shape[0])]
-    parts.append(dwd.reshape(shape + (-1, width)))
-    return jnp.concatenate(parts, axis=-2)
+    split = lambda t: t.reshape((4,) + sizes + (rows, width))
+    return split(dws), split(dwu), dwd.reshape(sizes + (4, rows, width))
 
 
 def shift_down(rows, amount):
@@ -880,11 +1017,13 @@
     square = jnp.concatenate([blocks(p["wqkv"]), blocks(p["wo"]), blocks(p["wu"])], axis=1)
     down = p["wd"].reshape(LAYERS, -1, rows, width)
     small = jnp.stack([small_rows(p, layer_at, width) for layer_at in range(LAYERS)])
-    got_x, got_grad, *gathered = bring(
-        grid.sizes, dealt(tokens_in), dealt(cotangent), square, down, small
-    )
+    sent_grad = dealt(cotangent)
+    got_x, *gathered = bring(grid.sizes, dealt(tokens_in), square, down, small)
+    got_x, sent_grad = lax.optimization_barrier((got_x, sent_grad))
     arrived_x = got_x.reshape(batch_count, 2, bin_len, width)
-    arrived_grad = got_grad.reshape(batch_count, 2, bin_len, width)
+    arrived_grad = lax.all_to_all(
+        sent_grad, "fsdp", split_axis=1, concat_axis=3, tiled=True
+    )[:, 0]
     square, down, small = gathered
     side = rows * grid.count
     w = (
@@ -902,11 +1041,12 @@
         bins = [pack_bin(slots[m], first_len[m], second_len[m]) for m in range(batch_count)]
         return jnp.concatenate(bins, axis=0)
 
-    def given_back(bins):
+    def to_slots(bins):
         bins = bins.reshape(batch_count, bin_len, width)
         slots = [unpack_bin(bins[m], first_len[m], second_len[m]) for m in range(batch_count)]
-        sent = jnp.stack(slots)[:, None]
-        back = lax.all_to_all(sent, "fsdp", split_axis=3, concat_axis=1, tiled=True)
+        return jnp.stack(slots)
+
+    def in_order(back):
         back = back.reshape(batch_count, slot_count, rows_dev, width)
         return jnp.take_along_axis(back, deal_here[:, :, None, None], axis=1)
 
@@ -916,32 +1056,31 @@
     for layer_at in range(LAYERS):
         hidden, act_in, stored = forward(hidden, act_in, w, mask, layer_at)
         kept.append(stored)
-    output = given_back(act_in)
+    sent = to_slots(act_in)[:, None]
+    back = lax.all_to_all(sent, "fsdp", split_axis=3, concat_axis=1, tiled=True)
+    output = in_order(back)
+    arrived_grad, act_in = lax.optimization_barrier((arrived_grad, act_in))
     grad = packed(arrived_grad)
-    sums = [None] * LAYERS
+    sums, vecs = [None] * LAYERS, [None] * LAYERS
     for layer_at in reversed(range(LAYERS)):
-        grad, (dws, dwu, dwd, vec) = backward(grad, kept[layer_at], w, mask, layer_at)
-        sums[layer_at] = (
-            scatter_rows(grid, whole_attn(grid, dws, vec, rows)),
-            scatter_rows(grid, whole_mlp(grid, dwu, dwd, rows)),
-        )
-    input_grad = given_back(grad.astype(jnp.bfloat16))
-    out = {name: [] for name in names}
-    for attn, mlp in sums:
-        blocks = [attn[j * rows : (j + 1) * rows] for j in range(4)]
-        out["wqkv"].append(jnp.concatenate(blocks[:3], axis=1))
-        out["wo"].append(blocks[3])
-        small = attn[4 * rows :].reshape(-1)
-        at = 0
-        for name in SMALL:
-            count = rows * (4 if name == "bu" else 1)
-            out[name].append(small[at : at + count])
-            at += count
-        half = mlp.shape[0] // 2
-        ups = [mlp[j * rows : (j + 1) * rows] for j in range(half // rows)]
-        out["wu"].append(jnp.concatenate(ups, axis=1))
-        out["wd"].append(mlp[half:])
-    return (output, input_grad) + tuple(jnp.stack(out[name]) for name in names)
+        grad, (*grads, vecs[layer_at]) = backward(grad, kept[layer_at], w, mask, layer_at)
+        sums[layer_at] = to_send(grid.sizes, grads, rows)
+    sent = to_slots(grad.astype(LOW)).reshape(batch_count, 2, members, rows_dev, width)
+    g_square, g_down, g_vec, back = take_home(grid.sizes, sums, jnp.stack(vecs), sent)
+    input_grad = in_order(back)
+    beside = lambda blocks: blocks.transpose(0, 2, 1, 3).reshape(LAYERS, rows, -1)
+    out = {
+        "wqkv": beside(g_square[:, :3]),
+        "wo": g_square[:, 3],
+        "wu": beside(g_square[:, 4:]),
+        "wd": g_down.reshape(LAYERS, -1, width),
+    }
+    place = group_at * members + member
+    for at, name in enumerate(SMALL):
+        values = g_vec[:, at:].reshape(LAYERS, -1) if name == "bu" else g_vec[:, at]
+        count = rows * (values.shape[1] // width)
+        out[name] = lax.dynamic_slice_in_dim(values, place * count, count, 1)
+    return (output, input_grad) + tuple(out[name] for name in names)
 
 
 def solution(mesh):

time: 854 us -> 674 us (0.79)
  waiting for transfers between devices: 161 us -> 0.01 us
  Pallas kernels: 435 us -> 569 us
  starting transfers between devices: 83.1 us -> 14.4 us
  local copies, waits for them, and re-layouts: 102 us -> 52.9 us
  other arithmetic: 58.8 us -> 25.3 us
    pallas_call x0 -> x1, Pallas kernels: none -> 176 us  [take_home(): pl.pallas_call(lambda *refs: home_kernel(sizes, layouts, *refs), out_shap...]
    ppermute x44 -> x0, waiting for transfers between devices: 161 us -> none  [send(): return lax.ppermute(array, AXES, pairs)]
    ppermute x44 -> x0, starting transfers between devices: 75 us -> none  [send(): return lax.ppermute(array, AXES, pairs)]
    pallas_call x1, Pallas kernels: 223 us -> 182 us  [bring(): pl.pallas_call(lambda *refs: bring_kernel(sizes, *refs), out_shape=outs,...]
    unnamed x111 -> x36, local copies, waits for them, and re-layouts: 25.3 us -> 4.1 us
    convert_element_type x21 -> x1, other arithmetic: 21.9 us -> 1.88 us  [per_device(): grad.astype(LOW)]
    dynamic_slice x4 -> x9, local copies, waits for them, and re-layouts: 19.7 us -> 5.72 us  [per_device(): out[name] = lax.dynamic_slice_in_dim(values, place * count, count, 1)]
  transfers between devices with their start and end apart: 46 -> 2, of which waited for: 17 -> 0; matrix products, arithmetic and copies ran while one was open for 12% -> 6% of each run, Pallas kernels for 1% -> 40%
where the time goes in v2:
time: 674 us; the launch traced here: 670 us
  Pallas kernels  569 us (84%)
  local copies, waits for them, and re-layouts  52.9 us (8%)
  other arithmetic  25.3 us (4%)
  starting transfers between devices  14.4 us (2%)
  between operations  7.79 us (1%)
    pallas_call x1, Pallas kernels, bring(): pl.pallas_call(lambda *refs: bring_kernel(sizes, *refs), out_shape=outs,...  182 us
    pallas_call x1, Pallas kernels, take_home(): pl.pallas_call(lambda *refs: home_kernel(sizes, layouts, *refs), out_shap...  176 us
    pallas_call x2, Pallas kernels, mlp_bwd(): pl.pallas_call(lambda *refs: mlp_bwd_kernel(count, *refs), grid=(count,),...  61.1 us
    pallas_call x2, Pallas kernels, attn_bwd(): pl.pallas_call(attn_bwd_kernel, grid=(bins,), in_specs=[row(width), row(3...  58 us
    pallas_call x2, Pallas kernels, attn_fwd(): pl.pallas_call(attn_fwd_kernel, grid=(bins,), in_specs=[row(width), pl.Bl...  42.2 us
    pallas_call x2, Pallas kernels, mlp_fwd(): pl.pallas_call(lambda *refs: mlp_fwd_kernel(count, *refs), grid=(count,),...  33.5 us
    pallas_call x2, Pallas kernels, attn_dw(): pl.pallas_call(attn_dw_kernel, grid=(4,), in_specs=[whole, pl.BlockSpec((...  17.1 us
  transfers between devices with their start and end apart: 2, of which 0 were waited for; matrix products, arithmetic and copies ran while one was open for 6% of the time, Pallas kernels for 40%

profile of v2, /device:TPU:0, one launch (start us, length us, event | category | flops | bytes accessed | tf_op | source)
XLA Modules:
  0.0 669.8 jit_solution(8175758878489380625)
XLA Ops:
  8.0 3.9 gather_fusion.2
  12.0 2.1 gather_fusion.1
  15.6 4.3 broadcast_select_fusion.2
  19.8 181.7 %bring.1 = (bf16[2,2,8,48,768]{4,3,2,1,0:T(8,128)(2,1)}, bf16[2,8,2,2,4,2,24,768]{7,6,5,4,3,2,1,0:T(8,128)(2,1)}, bf16[2,2,2,4,2,4,24,768]{7,6,5,4,3,2,1,0:T(8,128)(2,1)}, bf16[2,2,2,4,2,8,768]{6,5,4,3,2,1,0:T(8,128)(2,1)}) custom-call(bf16[2,8,2,48,768]{4,3,2,1,0:T(8,128)(2,1)} %bitcast.205, bf16[2,8,24,768]{3,2,1,0:T(8,128)(2,1)} %pad_maximum_fusion.2.refs_1_, ...), custom_call_target="tpu_custom_call" | custom-call | tf_op jit(solution)/shard_map/bring/pallas_call | solution.py:253
  203.1 8.3 %all-to-all-start.1 = ((bf16[2,8,2,48,768]{4,3,2,0,1:T(8,128)(2,1)}), bf16[2,8,2,48,768]{4,3,2,0,1:T(8,128)(2,1)S(1)}, u32[]{:S(2)}, u32[]{:S(2)}) async-start(bf16[2,8,2,48,768]{4,3,2,0,1:T(8,128)(2,1)} %copy.149), calls=%async_computation.1 | async-start | bytes 4718592 | tf_op jit(solution)/shard_map/all_to_all | solution.py:1024
  232.9 1.8 fusion.19
  236.7 20.9 %attn_fwd.2 = (bf16[768,2304]{1,0:T(8,128)(2,1)}, bf16[768,768]{1,0:T(8,128)(2,1)}, f32[768,128]{1,0:T(8,128)}, f32[768,768]{1,0:T(8,128)}) custom-call(bf16[768,768]{1,0:T(8,128)(2,1)} %pad_maximum_fusion.x_ref.act_ref, bf16[2,8,768,768]{3,2,1,0:T(8,128)(2,1)} %bitcast.181, f32[2,12,768]{2,1,0:T(8,128)} %copy-done, f32[2,384,384]{2,1,0:T(8,128)} %copy.144.mask_ref), custom_call_target="tpu_custom_call" | custom-call | tf_op jit(solution)/shard_map/attn_fwd/pallas_call | solution.py:633
  257.6 16.8 %mlp_fwd.2 = (f32[768,3072]{1,0:T(8,128)}, f32[768,768]{1,0:T(8,128)}, bf16[768,768]{1,0:T(8,128)(2,1)}, f32[768,768]{1,0:T(8,128)}, f32[768,128]{1,0:T(8,128)}) custom-call(f32[768,768]{1,0:T(8,128)} %get-tuple-element.65.refs_0_.refs_3_, bf16[2,8,768,768]{3,2,1,0:T(8,128)(2,1)} %bitcast.182, bf16[2,3072,768]{2,1,0:T(8,128)(2,1)} %bitcast.189, ...), custom_call_target="tpu_custom_call" | custom-call | tf_op jit(solution)/shard_map/mlp_fwd/pallas_call | solution.py:694
  274.3 21.3 %attn_fwd.3 = (bf16[768,2304]{1,0:T(8,128)(2,1)}, bf16[768,768]{1,0:T(8,128)(2,1)}, f32[768,128]{1,0:T(8,128)}, f32[768,768]{1,0:T(8,128)}) custom-call(f32[768,768]{1,0:T(8,128)} %get-tuple-element.67.x_ref, bf16[2,8,768,768]{3,2,1,0:T(8,128)(2,1)} %bitcast.183, f32[2,12,768]{2,1,0:T(8,128)} %copy-done, f32[2,384,384]{2,1,0:T(8,128)} %copy.144.mask_ref), custom_call_target="tpu_custom_call" | custom-call | tf_op jit(solution)/shard_map/attn_fwd/pallas_call | solution.py:633
  295.6 16.8 %mlp_fwd.3 = (f32[768,3072]{1,0:T(8,128)}, f32[768,768]{1,0:T(8,128)}, bf16[768,768]{1,0:T(8,128)(2,1)}, f32[768,768]{1,0:T(8,128)}, f32[768,128]{1,0:T(8,128)}) custom-call(f32[768,768]{1,0:T(8,128)} %get-tuple-element.68.refs_0_.refs_3_, bf16[2,8,768,768]{3,2,1,0:T(8,128)(2,1)} %bitcast.184, bf16[2,3072,768]{2,1,0:T(8,128)(2,1)} %bitcast.190, ...), custom_call_target="tpu_custom_call" | custom-call | tf_op jit(solution)/shard_map/mlp_fwd/pallas_call | solution.py:694
  316.0 30.6 %mlp_bwd.2 = (bf16[4,768,768]{2,1,0:T(8,128)(2,1)}, bf16[3072,768]{1,0:T(8,128)(2,1)}, f32[768,768]{1,0:T(8,128)}, f32[12,768]{1,0:T(8,128)}) custom-call(bf16[768,768]{1,0:T(8,128)(2,1)} %pad_maximum_fusion.1.refs_0_, f32[768,768]{1,0:T(8,128)} %get-tuple-element.72.refs_1_, f32[768,128]{1,0:T(8,128)} %get-tuple-element.73.refs_2_, ...), custom_call_target="tpu_custom_call" | custom-call | tf_op jit(solution)/shard_map/mlp_bwd/pallas_call | solution.py:786
  346.6 29.0 %attn_bwd.2 = (bf16[768,2304]{1,0:T(8,128)(2,1)}, f32[768,768]{1,0:T(8,128)}, bf16[768,768]{1,0:T(8,128)(2,1)}, f32[12,768]{1,0:T(8,128)}) custom-call(f32[768,768]{1,0:T(8,128)} %get-tuple-element.76.grad_ref, bf16[768,2304]{1,0:T(8,128)(2,1)} %get-tuple-element.77.qkv_ref, f32[768,128]{1,0:T(8,128)} %get-tuple-element.74.refs_4_.stat_ref, ...), custom_call_target="tpu_custom_call" | custom-call | tf_op jit(solution)/shard_map/attn_bwd/pallas_call | solution.py:876
  375.6 30.5 %mlp_bwd.3 = (bf16[4,768,768]{2,1,0:T(8,128)(2,1)}, bf16[3072,768]{1,0:T(8,128)(2,1)}, f32[768,768]{1,0:T(8,128)}, f32[12,768]{1,0:T(8,128)}) custom-call(f32[768,768]{1,0:T(8,128)} %get-tuple-element.79.refs_0_, f32[768,768]{1,0:T(8,128)} %get-tuple-element.80.refs_1_, f32[768,128]{1,0:T(8,128)} %get-tuple-element.81.refs_2_, ...), custom_call_target="tpu_custom_call" | custom-call | tf_op jit(solution)/shard_map/mlp_bwd/pallas_call | solution.py:786
  406.1 29.0 %attn_bwd.3 = (bf16[768,2304]{1,0:T(8,128)(2,1)}, f32[768,768]{1,0:T(8,128)}, bf16[768,768]{1,0:T(8,128)(2,1)}, f32[12,768]{1,0:T(8,128)}) custom-call(f32[768,768]{1,0:T(8,128)} %get-tuple-element.84.grad_ref, bf16[768,2304]{1,0:T(8,128)(2,1)} %get-tuple-element.85.qkv_ref, f32[768,128]{1,0:T(8,128)} %get-tuple-element.82.refs_4_.stat_ref, ...), custom_call_target="tpu_custom_call" | custom-call | tf_op jit(solution)/shard_map/attn_bwd/pallas_call | solution.py:876
  435.1 1.9 convert_element_type.38
  439.3 3.8 copy.146
  443.2 6.0 all-to-all-start
  449.8 8.5 %attn_dw.2 = bf16[4,768,768]{2,1,0:T(8,128)(2,1)} custom-call(bf16[768,768]{1,0:T(8,128)(2,1)} %pad_maximum_fusion.x_ref.act_ref, bf16[768,2304]{1,0:T(8,128)(2,1)} %get-tuple-element.87.dqkv_ref, bf16[768,768]{1,0:T(8,128)(2,1)} %get-tuple-element.88.ctx_ref, bf16[768,768]{1,0:T(8,128)(2,1)} %get-tuple-element.89.low_ref), custom_call_target="tpu_custom_call" | custom-call | tf_op jit(solution)/shard_map/attn_dw/pallas_call | solution.py:914
  458.3 8.5 %attn_dw.3 = bf16[4,768,768]{2,1,0:T(8,128)(2,1)} custom-call(bf16[768,768]{1,0:T(8,128)(2,1)} %get-tuple-element.92.act_ref, bf16[768,2304]{1,0:T(8,128)(2,1)} %get-tuple-element.93.dqkv_ref, bf16[768,768]{1,0:T(8,128)(2,1)} %get-tuple-element.94.ctx_ref, bf16[768,768]{1,0:T(8,128)(2,1)} %get-tuple-element.95.low_ref), custom_call_target="tpu_custom_call" | custom-call | tf_op jit(solution)/shard_map/attn_dw/pallas_call | solution.py:914
  469.1 175.9 %take_home.1 = (f32[2,8,24,768]{3,2,1,0:T(8,128)}, f32[2,4,24,768]{3,2,1,0:T(8,128)}, f32[2,12,768]{2,1,0:T(8,128)}, bf16[2,8,2,48,768]{4,3,2,1,0:T(8,128)(2,1)}) custom-call(bf16[4,2,2,4,2,24,768]{6,5,4,3,2,1,0:T(8,128)(2,1)} %bitcast.193, bf16[4,2,2,4,2,24,768]{6,5,4,3,2,1,0:T(8,128)(2,1)} %bitcast.210, bf16[2,2,4,2,4,24,768]{6,5,4,3,2,1,0:T(8,128)(2,1)} %bitcast.211, ...), custom_call_target="tpu_custom_call" | custom-call | tf_op jit(solution)/shard_map/take_home/pallas_call | solution.py:500
  649.9 2.1 gather_fusion.6
  659.3 2.0 copy.147
  661.5 2.1 gather_fusion.5
  663.6 5.1 broadcast_select_fusion
  (139 shorter events, 49.1 us)
Async XLA Ops:
  8.0 3.9 copy-start.2
  12.0 2.7 copy-start.7
  203.1 8.5 %copy-start.13 = (s32[2,64]{1,0:T(2,128)S(1)}, s32[2,64]{1,0:T(2,128)}, u32[]{:S(2)}) copy-start(s32[2,64]{1,0:T(2,128)} %param.24) | copy-start | bytes 1540
  203.1 15.4 %copy-start.5 = (bf16[2,2,2,4,2,8,768]{6,5,4,3,2,1,0:T(8,128)(2,1)S(1)}, bf16[2,2,2,4,2,8,768]{6,5,4,3,2,1,0:T(8,128)(2,1)}, u32[]{:S(2)}) copy-start(bf16[2,2,2,4,2,8,768]{6,5,4,3,2,1,0:T(8,128)(2,1)} %get-tuple-element.64) | copy-start | bytes 2359300
  203.1 110.7 %all-to-all-start.1 = ((bf16[2,8,2,48,768]{4,3,2,0,1:T(8,128)(2,1)}), bf16[2,8,2,48,768]{4,3,2,0,1:T(8,128)(2,1)S(1)}, u32[]{:S(2)}, u32[]{:S(2)}) async-start(bf16[2,8,2,48,768]{4,3,2,0,1:T(8,128)(2,1)} %copy.149), calls=%async_computation.1 | async-start | bytes 4718592 | tf_op jit(solution)/shard_map/all_to_all | solution.py:1024
  211.4 11.7 %copy-start.8 = (s32[2,64,6,3]{1,0,3,2:T(2,128)S(1)}, s32[2,64,6,3]{1,0,3,2:T(2,128)}, u32[]{:S(2)}) copy-start(s32[2,64,6,3]{1,0,3,2:T(2,128)} %param.26) | copy-start | bytes 27652
  232.9 1.8 copy-start
  295.6 18.1 %copy-start.14 = (pred[768]{0:T(1024)(128)(4,1)S(1)}, pred[768]{0:T(1024)(128)(4,1)}, u32[]{:S(2)}) copy-start(pred[768]{0:T(1024)(128)(4,1)} %constant.114.clone.1) | copy-start | bytes 2308
  435.1 2.0 copy-start.1
  443.2 216.1 %all-to-all-start = ((bf16[2,1,2,384,768]{4,2,0,1,3:T(2,128)(2,1)}), bf16[2,1,2,384,768]{4,2,0,1,3:T(2,128)(2,1)}, u32[]{:S(2)}, u32[]{:S(2)}) async-start(bf16[2,1,2,384,768]{4,2,0,1,3:T(2,128)(2,1)} %copy.146), calls=%async_computation | async-start | bytes 4718592 | tf_op jit(solution)/shard_map/all_to_all | solution.py:1060
  458.3 8.6 %copy-start.10 = (f32[12,768]{1,0:T(8,128)S(1)}, f32[12,768]{1,0:T(8,128)}, u32[]{:S(2)}) copy-start(f32[12,768]{1,0:T(8,128)} %get-tuple-element.99) | copy-start | bytes 110596
  458.3 8.6 %copy-start.11 = (f32[12,768]{1,0:T(8,128)S(1)}, f32[12,768]{1,0:T(8,128)}, u32[]{:S(2)}) copy-start(f32[12,768]{1,0:T(8,128)} %get-tuple-element.98) | copy-start | bytes 110596
  645.1 4.8 copy-start.3
  645.1 4.8 copy-start.4
  649.9 2.1 copy-start.9
  661.5 2.1 copy-start.12
  663.6 5.1 copy-start.6

commit v3 on v2

--- a/solution.py
+++ b/solution.py
@@ -57,7 +57,7 @@
         place[axis] = (place[axis] + offset) % self.sizes[axis]
         return self.device(place)
 
-    def start(self, source, target, device):
+    def plan(self, source, target, device):
         copy = pltpu.make_async_remote_copy(
             src_ref=source,
             dst_ref=target,
@@ -67,12 +67,20 @@
             device_id_type=pl.DeviceIdType.MESH,
         )
         self.used += 1
+        return copy
+
+    def plan_here(self, source, target):
+        copy = pltpu.make_async_copy(source, target, self.recv_sem.at[self.used])
+        self.used += 1
+        return copy
+
+    def start(self, source, target, device):
+        copy = self.plan(source, target, device)
         copy.start()
         return copy
 
     def start_here(self, source, target):
-        copy = pltpu.make_async_copy(source, target, self.recv_sem.at[self.used])
-        self.used += 1
+        copy = self.plan_here(source, target)
         copy.start()
         return copy
 
@@ -86,6 +94,9 @@
         found = [self.along(axis, k) for axis in (0, 1) for k in range(1, self.sizes[axis])]
         count = self.sizes[2] * self.sizes[3]
         return found + [self.member(k) for k in range(1, count)]
+
+    def neighbours(self):
+        return [self.along(axis, k) for axis in range(4) for k in range(1, self.sizes[axis])]
 
     def member(self, offset):
         count = self.sizes[2] * self.sizes[3]
@@ -282,21 +293,40 @@
 
 
 class Sum:
-    def __init__(self, links, source, order, lead, bufs, out_ref):
-        self.links, self.source, self.order, self.lead = links, source, order, lead
-        self.mine, self.theirs, self.first, self.half, self.second, self.quarter, self.last, self.out = bufs
-        self.out_ref = out_ref
+    def __init__(self, links, source, order, lead, bufs, out_ref, leg="both"):
+        self.links, self.order, self.lead, self.leg = links, order, lead, leg
         self.sent = []
+        c = links.at[1]
+        late = (2, 3) if order[0] == 0 else (0, 2)
+        if leg == "late":
+            self.half = bufs[0]
+            self.opening = [links.plan_here(source, self.half)]
+        else:
+            self.mine, self.theirs, self.first, self.half = bufs[:4]
+            there = self.send(source(1 - c), self.theirs, 1, 1)
+            self.opening = [links.plan_here(source(c), self.mine), there]
+            self.moving_first = self.spread(self.mine, (0, 2, 3), order[0], self.first)
+        if leg == "early":
+            self.out = self.half
+            self.stages = [self.add_core, self.add_first, self.nothing, self.nothing]
+        else:
+            self.second, self.quarter, self.last, self.out = bufs[-4:]
+            self.moving_second = self.spread(self.half, late, order[1], self.second)
+            self.moving_last = self.spread(self.quarter, (2,), 2, self.last)
+            self.late = late
+            self.stages = [self.take_up, self.add_second, self.add_last, self.nothing]
+            if leg == "both":
+                self.stages = [self.add_core, self.add_first, self.add_second, self.add_last]
+        self.result = links.plan_here(self.out, out_ref)
 
     def send(self, source, target, axis, offset):
-        copy = self.links.start(source, target, self.links.along(axis, offset))
+        copy = self.links.plan(source, target, self.links.along(axis, offset))
         self.sent.append(copy)
         return copy
 
     def begin(self):
-        c = self.links.at[1]
-        self.here = self.links.start_here(self.source(c), self.mine)
-        self.there = self.send(self.source(1 - c), self.theirs, 1, 1)
+        for copy in self.opening:
+            copy.start()
 
     def at(self, *place):
         return (ALL,) * self.lead + place
@@ -322,35 +352,45 @@
 
         each(into.shape[:-2], add)
 
-    def stage_one(self):
-        self.here.wait()
-        self.there.wait_recv()
+    def nothing(self):
+        pass
+
+    def add_core(self):
+        here, there = self.opening
+        here.wait()
+        there.wait_recv()
 
         def add(at):
             self.mine[at] = (wide(self.mine, at) + wide(self.theirs, at)).astype(LOW)
 
         each(self.mine.shape[:-2], add)
-        self.moving = self.spread(self.mine, (0, 2, 3), self.order[0], self.first)
-
-    def stage_two(self):
-        for copy in self.moving:
+        for copy in self.moving_first:
+            copy.start()
+
+    def add_first(self):
+        for copy in self.moving_first:
             copy.wait_recv()
         self.fold(self.mine, (0, 2, 3), self.order[0], self.first, self.half)
-        axes = (2, 3) if self.order[0] == 0 else (0, 2)
-        self.moving = self.spread(self.half, axes, self.order[1], self.second)
-
-    def stage_three(self):
-        for copy in self.moving:
+        for copy in [self.result] if self.leg == "early" else self.moving_second:
+            copy.start()
+
+    def take_up(self):
+        self.opening[0].wait()
+        for copy in self.moving_second:
+            copy.start()
+
+    def add_second(self):
+        for copy in self.moving_second:
             copy.wait_recv()
-        axes = (2, 3) if self.order[0] == 0 else (0, 2)
-        self.fold(self.half, axes, self.order[1], self.second, self.quarter)
-        self.moving = self.spread(self.quarter, (2,), 2, self.last)
-
-    def stage_four(self):
-        for copy in self.moving:
+        self.fold(self.half, self.late, self.order[1], self.second, self.quarter)
+        for copy in self.moving_last:
+            copy.start()
+
+    def add_last(self):
+        for copy in self.moving_last:
             copy.wait_recv()
         self.fold(self.quarter, (2,), 2, self.last, self.out)
-        self.result = self.links.start_here(self.out, self.out_ref)
+        self.result.start()
 
     def end(self):
         self.result.wait()
@@ -363,6 +403,7 @@
         self.links, self.source, self.out_ref = links, source, out_ref
         self.held, self.arrived = bufs[:5], bufs[5:]
         self.sent = []
+        self.stages = [self.stage_one, self.stage_two, self.stage_three, self.stage_four]
 
     def begin(self):
         self.here = self.links.start_here(self.source, self.held[0])
@@ -414,91 +455,177 @@
     return [pltpu.VMEM(shape, f32)] * 5 + arrived
 
 
-def sum_buffers(sizes, order, lead, tail):
+Y_FIRST, X_FIRST = (3, 0), (0, 3)
+
+
+def pair_of(kind, r, width):
+    lead, tail = ((), (2, r, width)) if kind == "down" else ((2,), (r, width))
+    return [(Y_FIRST, 0, lead, tail), (X_FIRST, 2, lead, tail)]
+
+
+def half_shape(sizes, order, lead, tail):
+    x, c, o, i = sizes
+    return lead + ((x, o) if order[0] == 3 else (o, i)) + tail
+
+
+def sum_buffers(sizes, order, lead, tail, leg="both"):
     x, c, o, i = sizes
     whole = lead + (x, o, i) + tail
-    half = lead + ((x, o) if order[0] == 3 else (o, i)) + tail
+    half = half_shape(sizes, order, lead, tail)
     quarter = lead + (o,) + tail
-    low = [
-        whole,
-        whole,
-        (sizes[order[0]] - 1,) + half,
-        half,
-        (sizes[order[1]] - 1,) + quarter,
-        quarter,
-        (o - 1,) + lead + tail,
-    ]
-    return [pltpu.VMEM(shape, LOW) for shape in low] + [pltpu.VMEM(lead + tail, jnp.float32)]
-
-
-def home_kernel(sizes, layouts, *refs):
-    inputs, refs = refs[: 3 * LAYERS], refs[3 * LAYERS :]
-    vec, sent, g_square, g_down, g_vec, back = refs[:6]
-    links = Links(sizes, *refs[6:8])
-    whole = Whole(links, vec, refs[8:17], g_vec)
-    refs = refs[17:]
+    early = [whole, whole, (sizes[order[0]] - 1,) + half]
+    late = [(sizes[order[1]] - 1,) + quarter, quarter, (o - 1,) + lead + tail]
+    shapes = (early if leg != "late" else []) + [half] + (late if leg != "early" else [])
+    out = [pltpu.VMEM(lead + tail, jnp.float32)] if leg != "early" else []
+    return [pltpu.VMEM(shape, LOW) for shape in shapes] + out
+
+
+def sum_count(sizes):
+    return 3 + sum(n - 1 for n in sizes)
+
+
+def source_of_core(kind, array, start):
+    blocks = slice(start, start + 2)
+    if kind == "down":
+        return lambda core: array.at[:, core, :, :, blocks]
+    return lambda core: array.at[blocks, :, core]
+
+
+class Rider:
+    def __init__(self, sizes, r, width, legs, steps, number):
+        self.sizes, self.legs, self.steps, self.number = sizes, legs, steps, number
+        self.items = [(kind, leg, *item) for kind, leg in legs for item in pair_of(kind, r, width)]
+        self.outs, self.scratch, self.inputs = [], [], 0
+        for kind, leg in legs:
+            self.inputs += 2 if leg == "late" else 1
+            if leg == "late":
+                self.outs.append(jax.ShapeDtypeStruct((4, r, width), jnp.float32))
+            else:
+                for order, start, lead, tail in pair_of(kind, r, width):
+                    self.outs.append(
+                        jax.ShapeDtypeStruct(half_shape(sizes, order, lead, tail), LOW)
+                    )
+        count = len(self.items) * sum_count(sizes)
+        self.scratch = [pltpu.SemaphoreType.DMA((count,)), pltpu.SemaphoreType.DMA((count,))]
+        for kind, leg, order, start, lead, tail in self.items:
+            self.scratch += sum_buffers(sizes, order, lead, tail, leg)
+
+    def board(self, ins, outs, scratch):
+        self.links = Links(self.sizes, *scratch[:2])
+        scratch = list(scratch[2:])
+        ins, outs = list(ins), list(outs)
+        self.sums = {"early": [], "late": []}
+        for kind, leg in self.legs:
+            if leg == "early":
+                array = ins.pop(0)
+            else:
+                final = outs.pop(0)
+            for order, start, lead, tail in pair_of(kind, *scratch[0].shape[-2:]):
+                count = 4 if leg == "early" else 5
+                bufs = scratch[:count]
+                del scratch[:count]
+                if leg == "early":
+                    source, out = source_of_core(kind, array, start), outs.pop(0)
+                else:
+                    source, out = ins.pop(0), final.at[start : start + 2]
+                item = Sum(self.links, source, order, len(lead), bufs, out, leg)
+                self.sums[leg].append(item)
+
+    def begin(self):
+        self.links.greet(self.links.neighbours())
+        for item in self.sums["late"] + self.sums["early"]:
+            item.begin()
+
+    def stage(self, leg, at):
+        for item in self.sums[leg]:
+            item.stages[at]()
+
+    def end(self):
+        for item in self.sums["late"] + self.sums["early"]:
+            item.end()
+
+    def step(self, name):
+        if name == "begin":
+            self.begin()
+        elif name == "end":
+            self.end()
+        else:
+            leg, at = name
+            if self.sums[leg]:
+                self.stage(leg, at)
+
+    def params(self):
+        return pltpu.CompilerParams(
+            collective_id=self.number, has_side_effects=True, vmem_limit_bytes=VMEM_BYTES
+        )
+
+
+def home_kernel(sizes, legs, *refs):
+    inputs, refs = refs[: len(legs) + 1], refs[len(legs) + 1 :]
+    vec, sent, late_sum, g_square, g_down, g_vec, back = refs[:7]
+    links = Links(sizes, *refs[7:9])
+    whole = Whole(links, vec, refs[9:18], g_vec)
+    refs = list(refs[18:])
     links.greet(links.partners())
-    sums = []
-    for layer_at, kind, start, order, lead, tail in layouts:
-        dws, dwu, dwd = inputs[3 * layer_at : 3 * layer_at + 3]
-        bufs, refs = refs[:8], refs[8:]
-        blocks = slice(start, start + 2)
-        if kind == "down":
-            source = lambda core, blocks=blocks, dwd=dwd: dwd.at[:, core, :, :, blocks]
-            out = g_down.at[layer_at, blocks]
-        else:
-            array = dws if kind == "attn" else dwu
-            source = lambda core, blocks=blocks, array=array: array.at[blocks, :, core]
-            out = g_square.at[layer_at, blocks if kind == "attn" else slice(start + 4, start + 6)]
-        sums.append(Sum(links, source, order, len(lead), bufs, out))
-    groups = [sums[at : at + 2] for at in range(0, len(sums), 2)]
+    inputs = list(inputs)
+    groups = []
+    for kind, leg in legs:
+        if leg == "both":
+            array = inputs.pop(0)
+        group = []
+        for order, start, lead, tail in pair_of(kind, *refs[0].shape[-2:]):
+            count = 5 if leg == "late" else 8
+            bufs = refs[:count]
+            del refs[:count]
+            blocks = slice(start, start + 2)
+            if leg == "late":
+                source, out = inputs.pop(0), late_sum.at[blocks]
+            else:
+                source = source_of_core(kind, array, start)
+                out = g_down.at[blocks] if kind == "down" else None
+                if out is None:
+                    out = g_square.at[blocks if kind == "attn" else slice(start + 4, start + 6)]
+            group.append(Sum(links, source, order, len(lead), bufs, out, leg))
+        groups.append(group)
     groups[0].append(whole)
-    sums.append(whole)
-    for group in groups:
-        for item in group:
-            item.begin()
+    sums = [item for group in groups for item in group]
+    for item in sums:
+        item.begin()
     moved = deal_back(links, sent, back)
-    stages = ("stage_one", "stage_two", "stage_three", "stage_four")
-    for turn in range(len(groups) + len(stages) - 1):
-        for depth in range(len(stages)):
+    for turn in range(len(groups) + 3):
+        for depth in range(4):
             if 0 <= turn - depth < len(groups):
                 for item in groups[turn - depth]:
-                    getattr(item, stages[depth])()
+                    item.stages[depth]()
     for item in sums:
         item.end()
     for copy in moved:
         copy.wait()
 
 
-def take_home(sizes, grads, vec, sent):
-    r, width = grads[0][0].shape[-2:]
-    tail = (r, width)
-    y_first, x_first = (3, 0), (0, 3)
-    layouts = []
-    for layer_at in reversed(range(LAYERS)):
-        for kind in ("down", "up", "attn"):
-            lead, piece = ((), (2,) + tail) if kind == "down" else ((2,), tail)
-            layouts += [
-                (layer_at, kind, 0, y_first, lead, piece),
-                (layer_at, kind, 2, x_first, lead, piece),
-            ]
+def take_home(sizes, halves, grads, vec, sent):
+    dws, dwu, dwd = grads
+    r, width = dws.shape[-2:]
+    legs = [("attn", "late"), ("down", "both"), ("up", "both"), ("attn", "both")]
     members = sizes[2] * sizes[3]
     f32 = jnp.float32
     batch, two, count, rows = sent.shape[:4]
     outs = [
-        jax.ShapeDtypeStruct((LAYERS, 8, r, width), f32),
-        jax.ShapeDtypeStruct((LAYERS, 4, r, width), f32),
+        jax.ShapeDtypeStruct((4, r, width), f32),
+        jax.ShapeDtypeStruct((8, r, width), f32),
+        jax.ShapeDtypeStruct((4, r, width), f32),
         jax.ShapeDtypeStruct(vec.shape, f32),
         jax.ShapeDtypeStruct((batch, count, two, rows, width), LOW),
     ]
-    args = [array for group in grads for array in group] + [vec, sent]
+    args = [*halves, dwd, dwu, dws, vec, sent]
     scratch = whole_buffers(sizes, vec.shape)
-    for layer_at, kind, start, order, lead, piece in layouts:
-        scratch += sum_buffers(sizes, order, lead, piece)
-    count = (len(layouts) + 1) * (3 + sum(n - 1 for n in sizes)) + members
+    for kind, leg in legs:
+        for order, start, lead, tail in pair_of(kind, r, width):
+            scratch += sum_buffers(sizes, order, lead, tail, leg)
+    count = (2 * len(legs) + 1) * sum_count(sizes) + members
     sems = [pltpu.SemaphoreType.DMA((count,)), pltpu.SemaphoreType.DMA((count,))]
     return pl.pallas_call(
-        lambda *refs: home_kernel(sizes, layouts, *refs),
+        lambda *refs: home_kernel(sizes, legs, *refs),
         out_shape=outs,
         in_specs=[HBM] * len(args),
         out_specs=[HBM] * len(outs),
@@ -723,27 +850,66 @@
     return jnp.sum(values, axis=0, keepdims=True)
 
 
-def mlp_bwd_kernel(
-    count,
-    grad_ref,
-    fnorm_ref,
-    fstat_ref,
-    normed_ref,
-    stat_ref,
-    up_ref,
-    wu_ref,
-    wd_ref,
-    v_ref,
-    dwu_ref,
-    dwd_ref,
-    grad_a_ref,
-    vec_ref,
-    mid,
-    grad_f,
-    low_f,
-    acc,
-):
+def aboard(refs, rider, ins, outs):
+    if rider is None:
+        return refs, lambda here, part: None
+    rest = refs[ins + rider.inputs :]
+    middle, last = len(rider.outs), len(rider.scratch)
+    own = refs[:ins] + rest[:outs] + rest[outs + middle : len(rest) - last]
+    rider.board(refs[ins : ins + rider.inputs], rest[outs : outs + middle], rest[len(rest) - last :])
+
+    def ride(here, part):
+        for grid_at, due, name in rider.steps:
+            if due == part:
+
+                @pl.when(here(grid_at))
+                def _(name=name):
+                    rider.step(name)
+
+    return own, ride
+
+
+def carried(rider, in_specs, out_specs, out_shape, scratch):
+    if rider is not None:
+        in_specs = in_specs + [HBM] * rider.inputs
+        out_specs = out_specs + [HBM] * len(rider.outs)
+        out_shape = out_shape + rider.outs
+        scratch = scratch + rider.scratch
+    found = dict(
+        in_specs=in_specs, out_specs=out_specs, out_shape=out_shape, scratch_shapes=scratch
+    )
+    if rider is not None:
+        found["compiler_params"] = rider.params()
+    return found
+
+
+MLP_STEPS = [
+    (0, 0, "begin"),
+    (0, 1, ("late", 0)),
+    (0, 2, ("early", 0)),
+    (1, 1, ("late", 1)),
+    (3, 1, ("early", 1)),
+    (3, 2, ("late", 2)),
+    (3, 3, "end"),
+]
+ATTN_STEPS = [
+    (0, 0, "begin"),
+    (0, 2, ("late", 0)),
+    (0, 3, ("early", 0)),
+    (0, 6, ("late", 1)),
+    (1, 4, ("early", 1)),
+    (1, 7, ("late", 2)),
+    (1, 7, "end"),
+]
+
+
+def mlp_bwd_kernel(count, rider, *refs):
+    own, ride = aboard(refs, rider, 9, 4)
+    grad_ref, fnorm_ref, fstat_ref, normed_ref, stat_ref, up_ref, wu_ref, wd_ref, v_ref = own[:9]
+    dwu_ref, dwd_ref, grad_a_ref, vec_ref, mid, grad_f, low_f, acc = own[9:]
     at = pl.program_id(0)
+    here = lambda step: at == step
+    ride(here, 0)
 
     @pl.when(at == 0)
     def _():
@@ -760,11 +926,13 @@
 
     act, slope = gelu_parts(up_ref[...])
     dwd_ref[...] = dot_weight(act.astype(LOW), low_f[...]).astype(LOW)
+    ride(here, 1)
     grad_up = dot_back(low_f[...], wd_ref[0]) * slope
     vec_ref[pl.ds(BU + at, 1), :] = sum_rows(grad_up)
     low_up = grad_up.astype(LOW)
     dwu_ref[0] = dot_weight(mid[...], low_up).astype(LOW)
     acc[...] += dot_back(low_up, wu_ref[0, 0])
+    ride(here, 2)
 
     @pl.when(at == count - 1)
     def _():
@@ -776,53 +944,61 @@
         vec_ref[BO : BO + 1, :] = sum_rows(grad)
         grad_a_ref[...] = grad
 
-
-def mlp_bwd(grad, fnorm, fstat, normed, stat, up, square, down, vectors, layer_at):
+    ride(here, 3)
+
+
+def mlp_bwd(
+    grad, fnorm, fstat, normed, stat, up, square, down, vectors, layer_at, rider=None, load=()
+):
     rows, width = normed.shape
     count = down.shape[1] // width
     whole = lambda n: pl.BlockSpec((rows, n), lambda j: (0, 0))
     f32 = jnp.float32
     vec_rows = vectors.shape[1]
+    in_specs = [
+        whole(width),
+        whole(width),
+        whole(LANES),
+        whole(width),
+        whole(LANES),
+        pl.BlockSpec((rows, width), lambda j: (0, j)),
+        pl.BlockSpec((1, 1, width, width), lambda j: (layer_at, 4 + j, 0, 0)),
+        pl.BlockSpec((1, width, width), lambda j: (layer_at, j, 0)),
+        pl.BlockSpec((1, vec_rows, width), lambda j: (layer_at, 0, 0)),
+    ]
+    out_specs = [
+        pl.BlockSpec((1, width, width), lambda j: (j, 0, 0)),
+        pl.BlockSpec((width, width), lambda j: (j, 0)),
+        whole(width),
+        pl.BlockSpec((vec_rows, width), lambda j: (0, 0)),
+    ]
+    out_shape = [
+        jax.ShapeDtypeStruct((count, width, width), LOW),
+        jax.ShapeDtypeStruct((count * width, width), LOW),
+        jax.ShapeDtypeStruct((rows, width), f32),
+        jax.ShapeDtypeStruct((vec_rows, width), f32),
+    ]
+    scratch = [
+        pltpu.VMEM((rows, width), LOW),
+        pltpu.VMEM((rows, width), f32),
+        pltpu.VMEM((rows, width), LOW),
+        pltpu.VMEM((rows, width), f32),
+    ]
     return pl.pallas_call(
-        lambda *refs: mlp_bwd_kernel(count, *refs),
+        lambda *refs: mlp_bwd_kernel(count, rider, *refs),
         grid=(count,),
-        in_specs=[
-            whole(width),
-            whole(width),
-            whole(LANES),
-            whole(width),
-            whole(LANES),
-            pl.BlockSpec((rows, width), lambda j: (0, j)),
-            pl.BlockSpec((1, 1, width, width), lambda j: (layer_at, 4 + j, 0, 0)),
-            pl.BlockSpec((1, width, width), lambda j: (layer_at, j, 0)),
-            pl.BlockSpec((1, vec_rows, width), lambda j: (layer_at, 0, 0)),
-        ],
-        out_specs=[
-            pl.BlockSpec((1, width, width), lambda j: (j, 0, 0)),
-            pl.BlockSpec((width, width), lambda j: (j, 0)),
-            whole(width),
-            pl.BlockSpec((vec_rows, width), lambda j: (0, 0)),
-        ],
-        out_shape=[
-            jax.ShapeDtypeStruct((count, width, width), LOW),
-            jax.ShapeDtypeStruct((count * width, width), LOW),
-            jax.ShapeDtypeStruct((rows, width), f32),
-            jax.ShapeDtypeStruct((vec_rows, width), f32),
-        ],
-        scratch_shapes=[
-            pltpu.VMEM((rows, width), LOW),
-            pltpu.VMEM((rows, width), f32),
-            pltpu.VMEM((rows, width), LOW),
-            pltpu.VMEM((rows, width), f32),
-        ],
-        name="mlp_bwd",
-    )(grad, fnorm, fstat, normed, stat, up, square, down, vectors)
-
-
-def attn_bwd_kernel(
-    grad_ref, qkv_ref, stat_ref, mask_ref, w_ref, vec_in, dqkv_ref, grad_in_ref, low_ref, vec_ref, gctx
-):
+        name="mlp_bwd" if rider is None else "mlp_bwd_sums",
+        **carried(rider, in_specs, out_specs, out_shape, scratch),
+    )(grad, fnorm, fstat, normed, stat, up, square, down, vectors, *load)
+
+
+def attn_bwd_kernel(rider, *refs):
+    own, ride = aboard(refs, rider, 6, 4)
+    grad_ref, qkv_ref, stat_ref, mask_ref, w_ref, vec_in = own[:6]
+    dqkv_ref, grad_in_ref, low_ref, vec_ref, gctx = own[6:]
     rows, width = grad_ref.shape
+    bin_at = pl.program_id(0)
+    ride(lambda step: bin_at == step, 0)
 
     @pl.when(pl.program_id(0) == 0)
     def _():
@@ -834,6 +1010,8 @@
     lanes = lane_ids(rows)
 
     def pair_step(pair, carry):
+        for part in range(HEADS // 2):
+            ride(lambda step: (bin_at == step) & (pair == part), 1 + part)
         q = qkv_ref[:, pair_at(pair)]
         k = qkv_ref[:, pair_at(pair, width)]
         v = qkv_ref[:, pair_at(pair, 2 * width)]
@@ -865,35 +1043,37 @@
     for j in range(3):
         total = total + dot_back(dqkv_ref[:, j * width : (j + 1) * width], w_ref[0, j])
     grad_in_ref[...] = total
-
-
-def attn_bwd(grad_a, qkv, stat, mask, square, vec, layer_at):
+    ride(lambda step: bin_at == step, 1 + HEADS // 2)
+
+
+def attn_bwd(grad_a, qkv, stat, mask, square, vec, layer_at, rider=None, load=()):
     rows, width = grad_a.shape
     bins, block = mask.shape[:2]
     row = lambda n: pl.BlockSpec((block, n), lambda b: (b, 0))
     fixed = pl.BlockSpec(vec.shape, lambda b: (0, 0))
     f32 = jnp.float32
+    in_specs = [
+        row(width),
+        row(3 * width),
+        row(LANES),
+        pl.BlockSpec((1, block, block), lambda b: (b, 0, 0)),
+        pl.BlockSpec((1, 4, width, width), lambda b: (layer_at, 0, 0, 0)),
+        fixed,
+    ]
+    out_shape = [
+        jax.ShapeDtypeStruct((rows, 3 * width), LOW),
+        jax.ShapeDtypeStruct((rows, width), f32),
+        jax.ShapeDtypeStruct((rows, width), LOW),
+        jax.ShapeDtypeStruct(vec.shape, f32),
+    ]
+    out_specs = [row(3 * width), row(width), row(width), fixed]
+    scratch = [pltpu.VMEM((block, width), LOW)]
     return pl.pallas_call(
-        attn_bwd_kernel,
+        lambda *refs: attn_bwd_kernel(rider, *refs),
         grid=(bins,),
-        in_specs=[
-            row(width),
-            row(3 * width),
-            row(LANES),
-            pl.BlockSpec((1, block, block), lambda b: (b, 0, 0)),
-            pl.BlockSpec((1, 4, width, width), lambda b: (layer_at, 0, 0, 0)),
-            fixed,
-        ],
-        out_specs=[row(3 * width), row(width), row(width), fixed],
-        out_shape=[
-            jax.ShapeDtypeStruct((rows, 3 * width), LOW),
-            jax.ShapeDtypeStruct((rows, width), f32),
-            jax.ShapeDtypeStruct((rows, width), LOW),
-            jax.ShapeDtypeStruct(vec.shape, f32),
-        ],
-        scratch_shapes=[pltpu.VMEM((block, width), LOW)],
-        name="attn_bwd",
-    )(grad_a, qkv, stat, mask, square, vec)
+        name=f"attn_bwd_sums{rider.number}",
+        **carried(rider, in_specs, out_specs, out_shape, scratch),
+    )(grad_a, qkv, stat, mask, square, vec, *load)
 
 
 def attn_dw_kernel(act_ref, dqkv_ref, ctx_ref, low_ref, out_ref):
@@ -949,21 +1129,35 @@
     return out, out_low, (act_in, qkv, ctx, stat, normed, up, fnorm, fstat)
 
 
-def backward(grad, kept, w, mask, layer_at):
+def backward_layers(grad, back, kept, w, mask, sizes, rows):
     square, down, vectors = w
-    act_in, qkv, ctx, stat, normed, up, fnorm, fstat = kept
-    dwu, dwd, grad_a, vec = mlp_bwd(
-        grad, fnorm, fstat, normed, stat, up, square, down, vectors, layer_at
-    )
-    dqkv, grad_in, low_a, vec = attn_bwd(grad_a, qkv, stat, mask, square, vec, layer_at)
-    return grad_in, (attn_dw(act_in, dqkv, ctx, low_a), dwu, dwd, vec)
-
-
-def to_send(sizes, grads, rows):
-    dws, dwu, dwd = grads
-    width = dwd.shape[-1]
-    split = lambda t: t.reshape((4,) + sizes + (rows, width))
-    return split(dws), split(dwu), dwd.reshape(sizes + (4, rows, width))
+    width = square.shape[-1]
+
+    def of_mlp(grad, layer_at, *more):
+        act_in, qkv, ctx, stat, normed, up, fnorm, fstat = kept[layer_at]
+        return mlp_bwd(
+            grad, fnorm, fstat, normed, stat, up, square, down, vectors, layer_at, *more
+        )
+
+    def of_attn(grad_a, vec, layer_at, *more):
+        act_in, qkv, ctx, stat, *unused = kept[layer_at]
+        dqkv, grad_in, low_a, vec, *sums = attn_bwd(
+            grad_a, qkv, stat, mask, square, vec, layer_at, *more
+        )
+        return grad_in, attn_dw(act_in, dqkv, ctx, low_a), vec, sums
+
+    blocks_out = lambda t: t.reshape((4,) + sizes + (rows, width))
+    rows_out = lambda t: t.reshape(sizes + (4, rows, width))
+    dwu, dwd, grad_a, vec = of_mlp(grad, 1)
+    rider = Rider(sizes, rows, width, [("down", "early")], ATTN_STEPS, 2)
+    grad, dws, vec_late, halves = of_attn(grad_a, vec, 1, rider, [rows_out(dwd)])
+    grad, back = lax.optimization_barrier((grad, back))
+    rider = Rider(sizes, rows, width, [("down", "late"), ("up", "early")], MLP_STEPS, 3)
+    dwu, dwd, grad_a, vec, g_down, *halves = of_mlp(grad, 0, rider, [*halves, blocks_out(dwu)])
+    rider = Rider(sizes, rows, width, [("up", "late"), ("attn", "early")], ATTN_STEPS, 4)
+    grad, dws, vec, (g_up, *halves) = of_attn(grad_a, vec, 0, rider, [*halves, blocks_out(dws)])
+    left = (blocks_out(dws), blocks_out(dwu), rows_out(dwd))
+    return grad, back, (g_up, g_down), (halves, left, jnp.stack([vec, vec_late]))
 
 
 def shift_down(rows, amount):
@@ -1058,22 +1252,21 @@
         kept.append(stored)
     sent = to_slots(act_in)[:, None]
     back = lax.all_to_all(sent, "fsdp", split_axis=3, concat_axis=1, tiled=True)
-    output = in_order(back)
     arrived_grad, act_in = lax.optimization_barrier((arrived_grad, act_in))
     grad = packed(arrived_grad)
-    sums, vecs = [None] * LAYERS, [None] * LAYERS
-    for layer_at in reversed(range(LAYERS)):
-        grad, (*grads, vecs[layer_at]) = backward(grad, kept[layer_at], w, mask, layer_at)
-        sums[layer_at] = to_send(grid.sizes, grads, rows)
+    grad, back, (g_up, g_down_late), left = backward_layers(grad, back, kept, w, mask, grid.sizes, rows)
+    output = in_order(back)
     sent = to_slots(grad.astype(LOW)).reshape(batch_count, 2, members, rows_dev, width)
-    g_square, g_down, g_vec, back = take_home(grid.sizes, sums, jnp.stack(vecs), sent)
+    g_attn, g_square, g_down, g_vec, back = take_home(grid.sizes, *left, sent)
     input_grad = in_order(back)
-    beside = lambda blocks: blocks.transpose(0, 2, 1, 3).reshape(LAYERS, rows, -1)
+    beside = lambda *pairs: jnp.stack(
+        [blocks.transpose(1, 0, 2).reshape(rows, -1) for blocks in pairs]
+    )
     out = {
-        "wqkv": beside(g_square[:, :3]),
-        "wo": g_square[:, 3],
-        "wu": beside(g_square[:, 4:]),
-        "wd": g_down.reshape(LAYERS, -1, width),
+        "wqkv": beside(g_square[:3], g_attn[:3]),
+        "wo": jnp.stack([g_square[3], g_attn[3]]),
+        "wu": beside(g_square[4:], g_up),
+        "wd": jnp.stack([g_down.reshape(-1, width), g_down_late.reshape(-1, width)]),
     }
     place = group_at * members + member
     for at, name in enumerate(SMALL):

time: 674 us -> 669 us (level)
  Pallas kernels: 569 us -> 539 us
  local copies, waits for them, and re-layouts: 52.9 us -> 71.9 us
    pallas_call x5, Pallas kernels: 295 us -> 264 us  [the longest x1 116 us: take_home(): pl.pallas_call(lambda *refs: home_kernel(sizes, legs, *refs), out_shape=o...]
  transfers between devices with their start and end apart: 2 -> 2, of which waited for: 0 -> 0; matrix products, arithmetic and copies ran while one was open for 6% -> 3% of each run, Pallas kernels for 40% -> 23%
where the time goes in v3:
time: 669 us; the launch traced here: 663 us
  Pallas kernels  539 us (81%)
  local copies, waits for them, and re-layouts  71.9 us (11%)
  other arithmetic  29.4 us (4%)
  starting transfers between devices  14.9 us (2%)
  between operations  8.01 us (1%)
    pallas_call x1, Pallas kernels, bring(): pl.pallas_call(lambda *refs: bring_kernel(sizes, *refs), out_shape=outs,...  182 us
    pallas_call x1, Pallas kernels, take_home(): pl.pallas_call(lambda *refs: home_kernel(sizes, legs, *refs), out_shape=o...  116 us
    pallas_call x2, Pallas kernels, attn_bwd(): pl.pallas_call(lambda *refs: attn_bwd_kernel(rider, *refs), grid=(bins,),...  76.4 us
    pallas_call x2, Pallas kernels, mlp_bwd(): pl.pallas_call(lambda *refs: mlp_bwd_kernel(count, rider, *refs), grid=(c...  71.2 us
    pallas_call x2, Pallas kernels, attn_fwd(): pl.pallas_call(attn_fwd_kernel, grid=(bins,), in_specs=[row(width), pl.Bl...  42.1 us
    pallas_call x2, Pallas kernels, mlp_fwd(): pl.pallas_call(lambda *refs: mlp_fwd_kernel(count, *refs), grid=(count,),...  33.5 us
    pallas_call x2, Pallas kernels, attn_dw(): pl.pallas_call(attn_dw_kernel, grid=(4,), in_specs=[whole, pl.BlockSpec((...  17.5 us
  transfers between devices with their start and end apart: 2, of which 0 were waited for; matrix products, arithmetic and copies ran while one was open for 3% of the time, Pallas kernels for 23%

profile of v3, /device:TPU:0, one launch (start us, length us, event | category | flops | bytes accessed | tf_op | source)
XLA Modules:
  0.0 663.2 jit_solution(8897734018162328961)
XLA Ops:
  8.1 3.9 gather_fusion.2
  12.0 2.1 gather_fusion.1
  15.6 4.3 broadcast_select_fusion.2
  19.9 181.7 %bring.1 = (bf16[2,2,8,48,768]{4,3,2,1,0:T(8,128)(2,1)}, bf16[2,8,2,2,4,2,24,768]{7,6,5,4,3,2,1,0:T(8,128)(2,1)}, bf16[2,2,2,4,2,4,24,768]{7,6,5,4,3,2,1,0:T(8,128)(2,1)}, bf16[2,2,2,4,2,8,768]{6,5,4,3,2,1,0:T(8,128)(2,1)}) custom-call(bf16[2,8,2,48,768]{4,3,2,1,0:T(8,128)(2,1)} %bitcast.206, bf16[2,8,24,768]{3,2,1,0:T(8,128)(2,1)} %pad_maximum_fusion.2.refs_1_, ...), custom_call_target="tpu_custom_call" | custom-call | tf_op jit(solution)/shard_map/bring/pallas_call | solution.py:264
  203.1 8.6 %all-to-all-start = ((bf16[2,8,2,48,768]{4,3,2,0,1:T(8,128)(2,1)}), bf16[2,8,2,48,768]{4,3,2,0,1:T(8,128)(2,1)S(1)}, u32[]{:S(2)}, u32[]{:S(2)}) async-start(bf16[2,8,2,48,768]{4,3,2,0,1:T(8,128)(2,1)} %copy.142), calls=%async_computation | async-start | bytes 4718592 | tf_op jit(solution)/shard_map/all_to_all | solution.py:1218
  237.1 20.9 %attn_fwd.2 = (bf16[768,2304]{1,0:T(8,128)(2,1)}, bf16[768,768]{1,0:T(8,128)(2,1)}, f32[768,128]{1,0:T(8,128)}, f32[768,768]{1,0:T(8,128)}) custom-call(bf16[768,768]{1,0:T(8,128)(2,1)} %pad_maximum_fusion.x_ref.act_ref, bf16[2,8,768,768]{3,2,1,0:T(8,128)(2,1)} %bitcast.181, f32[2,12,768]{2,1,0:T(8,128)} %copy-done.2, f32[2,384,384]{2,1,0:T(8,128)} %copy.154.mask_ref.refs_3_), custom_call_target="tpu_custom_call" | custom-call | tf_op jit(solution)/shard_map/attn_fwd/pallas_call | solution.py:760
  258.0 16.8 %mlp_fwd.2 = (f32[768,3072]{1,0:T(8,128)}, f32[768,768]{1,0:T(8,128)}, bf16[768,768]{1,0:T(8,128)(2,1)}, f32[768,768]{1,0:T(8,128)}, f32[768,128]{1,0:T(8,128)}) custom-call(f32[768,768]{1,0:T(8,128)} %get-tuple-element.77.refs_0_.refs_3_, bf16[2,8,768,768]{3,2,1,0:T(8,128)(2,1)} %bitcast.182, bf16[2,3072,768]{2,1,0:T(8,128)(2,1)} %bitcast.189, ...), custom_call_target="tpu_custom_call" | custom-call | tf_op jit(solution)/shard_map/mlp_fwd/pallas_call | solution.py:821
  274.7 21.3 %attn_fwd.3 = (bf16[768,2304]{1,0:T(8,128)(2,1)}, bf16[768,768]{1,0:T(8,128)(2,1)}, f32[768,128]{1,0:T(8,128)}, f32[768,768]{1,0:T(8,128)}) custom-call(f32[768,768]{1,0:T(8,128)} %get-tuple-element.79.x_ref, bf16[2,8,768,768]{3,2,1,0:T(8,128)(2,1)} %bitcast.183, f32[2,12,768]{2,1,0:T(8,128)} %copy-done.2, f32[2,384,384]{2,1,0:T(8,128)} %copy.154.mask_ref.refs_3_), custom_call_target="tpu_custom_call" | custom-call | tf_op jit(solution)/shard_map/attn_fwd/pallas_call | solution.py:760
  296.0 16.8 %mlp_fwd.3 = (f32[768,3072]{1,0:T(8,128)}, f32[768,768]{1,0:T(8,128)}, bf16[768,768]{1,0:T(8,128)(2,1)}, f32[768,768]{1,0:T(8,128)}, f32[768,128]{1,0:T(8,128)}) custom-call(f32[768,768]{1,0:T(8,128)} %get-tuple-element.80.refs_0_.refs_3_, bf16[2,8,768,768]{3,2,1,0:T(8,128)(2,1)} %bitcast.184, bf16[2,3072,768]{2,1,0:T(8,128)(2,1)} %bitcast.190, ...), custom_call_target="tpu_custom_call" | custom-call | tf_op jit(solution)/shard_map/mlp_fwd/pallas_call | solution.py:821
  315.5 1.9 copy.143
  319.5 3.9 copy.157
  323.3 6.3 all-to-all-start.1
  331.6 30.0 %mlp_bwd.1 = (bf16[4,768,768]{2,1,0:T(8,128)(2,1)}, bf16[3072,768]{1,0:T(8,128)(2,1)}, f32[768,768]{1,0:T(8,128)}, f32[12,768]{1,0:T(8,128)}) custom-call(bf16[768,768]{1,0:T(8,128)(2,1)} %pad_maximum_fusion.1.refs_0_, f32[768,768]{1,0:T(8,128)} %get-tuple-element.83.refs_1_, f32[768,128]{1,0:T(8,128)} %get-tuple-element.84.refs_2_, ...), custom_call_target="tpu_custom_call" | custom-call | tf_op jit(solution)/shard_map/mlp_bwd/pallas_call | solution.py:987
  361.6 37.7 %attn_bwd_sums2.1 = (bf16[768,2304]{1,0:T(8,128)(2,1)}, f32[768,768]{1,0:T(8,128)}, bf16[768,768]{1,0:T(8,128)(2,1)}, f32[12,768]{1,0:T(8,128)}, bf16[2,4,2,24,7...) custom-call(f32[768,768]{1,0:T(8,128)} %get-tuple-element.87.refs_0_, ...), custom_call_target="tpu_custom_call" | custom-call | tf_op jit(solution)/shard_map/attn_bwd_sums2/pallas_call | solution.py:1071
  399.3 9.0 %attn_dw.2 = bf16[4,768,768]{2,1,0:T(8,128)(2,1)} custom-call(bf16[768,768]{1,0:T(8,128)(2,1)} %get-tuple-element.106.act_ref, bf16[768,2304]{1,0:T(8,128)(2,1)} %get-tuple-element.107.dqkv_ref, bf16[768,768]{1,0:T(8,128)(2,1)} %get-tuple-element.108.ctx_ref, bf16[768,768]{1,0:T(8,128)(2,1)} %get-tuple-element.109.low_ref), custom_call_target="tpu_custom_call" | custom-call | tf_op jit(solution)/shard_map/attn_dw/pallas_call | solution.py:1094
  408.3 3.4 copy.158
  411.7 41.2 %mlp_bwd_sums.1 = (bf16[4,768,768]{2,1,0:T(8,128)(2,1)}, bf16[3072,768]{1,0:T(8,128)(2,1)}, f32[768,768]{1,0:T(8,128)}, f32[12,768]{1,0:T(8,128)}, f32[4,24,768]...) custom-call(f32[768,768]{1,0:T(8,128)} %get-tuple-element.93.refs_0_, ...), custom_call_target="tpu_custom_call" | custom-call | tf_op jit(solution)/shard_map/mlp_bwd_sums/pallas_call | solution.py:987
  452.9 38.7 %attn_bwd_sums4.1 = (bf16[768,2304]{1,0:T(8,128)(2,1)}, f32[768,768]{1,0:T(8,128)}, bf16[768,768]{1,0:T(8,128)(2,1)}, f32[12,768]{1,0:T(8,128)}, f32[4,24,768]{2...) custom-call(f32[768,768]{1,0:T(8,128)} %get-tuple-element.101.refs_0_, ...), custom_call_target="tpu_custom_call" | custom-call | tf_op jit(solution)/shard_map/attn_bwd_sums4/pallas_call | solution.py:1071
  495.1 8.5 %attn_dw.3 = bf16[4,768,768]{2,1,0:T(8,128)(2,1)} custom-call(bf16[768,768]{1,0:T(8,128)(2,1)} %pad_maximum_fusion.x_ref.act_ref, bf16[768,2304]{1,0:T(8,128)(2,1)} %get-tuple-element.114.dqkv_ref, bf16[768,768]{1,0:T(8,128)(2,1)} %get-tuple-element.115.ctx_ref, bf16[768,768]{1,0:T(8,128)(2,1)} %get-tuple-element.116.low_ref), custom_call_target="tpu_custom_call" | custom-call | tf_op jit(solution)/shard_map/attn_dw/pallas_call | solution.py:1094
  505.2 116.5 %take_home.1 = (f32[4,24,768]{2,1,0:T(8,128)}, f32[8,24,768]{2,1,0:T(8,128)}, f32[4,24,768]{2,1,0:T(8,128)}, f32[2,12,768]{2,1,0:T(8,128)}, bf16[2,8,2,48,768]{4,3,2,1,0:T(8,128)(2,1)}) custom-call(bf16[2,2,4,24,768]{4,3,2,1,0:T(8,128)(2,1)} %get-tuple-element.110.refs_0_, bf16[2,4,2,24,768]{4,3,2,1,0:T(8,128)(2,1)} %get-tuple-element.111.refs_1_, ...), custom_call_target="tpu_custom_call" | custom-call | tf_op jit(solution)/shard_map/take_home/pallas_call | solution.py:627
  631.0 2.0 copy.159
  633.2 2.1 gather_fusion.5
  635.3 3.8 gather_fusion.6
  658.6 4.3 broadcast_select_fusion
  (174 shorter events, 69.7 us)
Async XLA Ops:
  8.1 3.9 copy-start.4
  12.0 2.7 copy-start.10
  203.1 8.8 %copy-start.25 = (s32[2,64]{1,0:T(2,128)S(1)}, s32[2,64]{1,0:T(2,128)}, u32[]{:S(2)}) copy-start(s32[2,64]{1,0:T(2,128)} %param.24) | copy-start | bytes 1540
  203.1 15.7 %copy-start.7 = (bf16[2,2,2,4,2,8,768]{6,5,4,3,2,1,0:T(8,128)(2,1)S(1)}, bf16[2,2,2,4,2,8,768]{6,5,4,3,2,1,0:T(8,128)(2,1)}, u32[]{:S(2)}) copy-start(bf16[2,2,2,4,2,8,768]{6,5,4,3,2,1,0:T(8,128)(2,1)} %get-tuple-element.76) | copy-start | bytes 2359300
  203.1 111.0 %all-to-all-start = ((bf16[2,8,2,48,768]{4,3,2,0,1:T(8,128)(2,1)}), bf16[2,8,2,48,768]{4,3,2,0,1:T(8,128)(2,1)S(1)}, u32[]{:S(2)}, u32[]{:S(2)}) async-start(bf16[2,8,2,48,768]{4,3,2,0,1:T(8,128)(2,1)} %copy.142), calls=%async_computation | async-start | bytes 4718592 | tf_op jit(solution)/shard_map/all_to_all | solution.py:1218
  211.7 11.7 %copy-start.11 = (s32[2,64,6,3]{1,0,3,2:T(2,128)S(1)}, s32[2,64,6,3]{1,0,3,2:T(2,128)}, u32[]{:S(2)}) copy-start(s32[2,64,6,3]{1,0,3,2:T(2,128)} %param.26) | copy-start | bytes 27652
  230.6 87.9 %copy-start.14 = (pred[384]{0:T(512)(128)(4,1)}, pred[384]{0:T(512)(128)(4,1)S(1)}, u32[]{:S(2)}) copy-start(pred[384]{0:T(512)(128)(4,1)S(1)} %iota_compare_fusion.4) | copy-start | bytes 1156
  231.3 98.9 %copy-start.16 = (pred[384]{0:T(512)(128)(4,1)}, pred[384]{0:T(512)(128)(4,1)S(1)}, u32[]{:S(2)}) copy-start(pred[384]{0:T(512)(128)(4,1)S(1)} %iota_compare_fusion.2) | copy-start | bytes 1156
  232.5 85.0 %copy-start.20 = (pred[384]{0:T(512)(128)(4,1)}, pred[384]{0:T(512)(128)(4,1)S(1)}, u32[]{:S(2)}) copy-start(pred[384]{0:T(512)(128)(4,1)S(1)} %iota_compare_fusion.3) | copy-start | bytes 1156
  233.2 85.3 %copy-start.18 = (pred[384]{0:T(512)(128)(4,1)}, pred[384]{0:T(512)(128)(4,1)S(1)}, u32[]{:S(2)}) copy-start(pred[384]{0:T(512)(128)(4,1)S(1)} %iota_compare_fusion.1) | copy-start | bytes 1156
  296.0 18.1 %copy-start.26 = (pred[768]{0:T(1024)(128)(4,1)S(1)}, pred[768]{0:T(1024)(128)(4,1)}, u32[]{:S(2)}) copy-start(pred[768]{0:T(1024)(128)(4,1)} %constant.114.clone.1) | copy-start | bytes 2308
  314.1 4.3 copy-start.23
  315.5 2.0 copy-start.3
  323.3 85.0 %all-to-all-start.1 = ((bf16[2,1,2,384,768]{4,2,0,1,3:T(2,128)(2,1)}), bf16[2,1,2,384,768]{4,2,0,1,3:T(2,128)(2,1)}, u32[]{:S(2)}, u32[]{:S(2)}) async-start(bf16[2,1,2,384,768]{4,2,0,1,3:T(2,128)(2,1)} %copy.157), calls=%async_computation.1 | async-start | bytes 4718592 | tf_op jit(solution)/shard_map/all_to_all | solution.py:1254
  491.6 1.9 copy-start.15
  491.6 1.9 copy-start.17
  491.6 1.8 copy-start.21
  491.6 1.8 copy-start.24
  630.9 2.0 copy-start.8
  631.0 2.3 copy-start.5
  635.3 3.8 copy-start.9
  650.1 8.6 %copy-start.1 = (bf16[32,48,768]{2,1,0:T(8,128)(2,1)S(1)}, bf16[32,48,768]{2,1,0:T(8,128)(2,1)}, u32[]{:S(2)}) copy-start(bf16[32,48,768]{2,1,0:T(8,128)(2,1)} %gather_fusion.5) | copy-start | bytes 7077892
  650.1 8.6 %copy-start.22 = (pred[2,16]{1,0:T(4,128)(4,1)S(1)}, pred[2,16]{1,0:T(4,128)(4,1)}, u32[]{:S(2)}) copy-start(pred[2,16]{1,0:T(4,128)(4,1)} %get-tuple-element.194) | copy-start | bytes 100
  652.1 5.7 copy-start.6
  (5 other events, 5.7 us)

commit v4 on v3

--- a/solution.py
+++ b/solution.py
@@ -14,6 +14,7 @@
 NEG = -1000000000.0
 HEAD_DIM = 64
 VMEM_BYTES = 67043328
+DEAL_TURNS = 8
 
 
 epsilon = 1e-06
@@ -112,11 +113,41 @@
 
     def begin(self):
         links = self.links
+        x, c, o, i = links.at
         spot = self.target(*links.at)
         self.own = links.start_here(self.source, spot)
-        self.column = [
-            links.start(self.source, spot, links.along(2, k)) for k in range(1, links.sizes[2])
-        ]
+        if links.sizes[2] != 4:
+            self.column = [
+                links.start(self.source, spot, links.along(2, k)) for k in range(1, links.sizes[2])
+            ]
+            return
+        self.inside = (o == 1) | (o == 2)
+        near = links.device((x, c, o + 1 - 2 * (o % 2), i))
+        across = links.device((x, c, 3 - o, i))
+        pair = lambda half: self.target(x, c, pl.ds(2 * half, 2), i)
+        ours, others = pair(o // 2), pair(1 - o // 2)
+        self.column = [links.start(self.source, spot, near)]
+        self.pairs = links.plan(ours, ours, across)
+        self.outwards = links.plan(others, others, near)
+
+    def cross(self):
+        if self.links.sizes[2] != 4:
+            return
+        self.own.wait()
+        self.column[0].wait_recv()
+
+        @pl.when(self.inside)
+        def _():
+            self.pairs.start()
+
+    def spread(self):
+        if self.links.sizes[2] != 4:
+            return
+
+        @pl.when(self.inside)
+        def _():
+            self.pairs.wait_recv()
+            self.outwards.start()
 
     def hand_over(self, spot):
         self.across.append(self.links.start(spot, spot, self.links.along(1, 1)))
@@ -124,9 +155,16 @@
     def first(self):
         links = self.links
         x, c, o, i = links.at
-        self.own.wait()
-        for copy in self.column:
-            copy.wait_recv()
+        if links.sizes[2] != 4:
+            self.own.wait()
+            for copy in self.column:
+                copy.wait_recv()
+        else:
+
+            @pl.when(~self.inside)
+            def _():
+                self.outwards.wait_recv()
+
         spot = self.target(x, c, ALL, i)
         axis = self.order[0]
         self.line = [
@@ -166,16 +204,23 @@
             copy.wait()
         for copy in self.column + self.line + self.sheet:
             copy.wait_send()
+        if self.links.sizes[2] == 4:
+
+            @pl.when(self.inside)
+            def _():
+                self.pairs.wait_send()
+                self.outwards.wait_send()
 
 
 def deal_out(links, source, target):
     count = links.sizes[2] * links.sizes[3]
     me = links.at[2] * links.sizes[3] + links.at[3]
     spot = target.at[:, :, me]
-    copies = [links.start_here(source.at[:, me], spot)]
-    for k in range(1, count):
-        copies.append(links.start(source.at[:, (me + k) % count], spot, links.member(k)))
-    return copies
+    starts = [
+        lambda k=k: links.start(source.at[:, (me + k) % count], spot, links.member(k))
+        for k in range(1, count)
+    ]
+    return starts + [lambda: links.start_here(source.at[:, me], spot)]
 
 
 def deal_back(links, source, target):
@@ -213,7 +258,7 @@
     return [
         [tiny, of_square(0, (0, 3)), of_square(2, (3, 0))],
         [of_square(4, (0, 3)), of_square(6, (3, 0))],
-        [of_down(0, (0, 3)), of_down(2, (3, 0))],
+        [of_down(0, (3, 0)), of_down(2, (3, 0))],
     ]
 
 
@@ -227,20 +272,29 @@
         groups += gathers_of(
             links, layer_at, square, down, small, all_square, all_down, all_small
         )
-    for group in groups:
-        for item in group:
-            item.begin()
-    moved = deal_out(links, sent_x, got_x)
+    starts = deal_out(links, sent_x, got_x)
+    share = -(-len(starts) // DEAL_TURNS)
+    moved = []
+
+    def run(step, at):
+        if 0 <= at < len(groups):
+            for item in groups[at]:
+                getattr(item, step)()
+
+    run("begin", 0)
+    run("begin", 1)
+    run("cross", 0)
+    run("spread", 0)
+    run("cross", 1)
+    run("begin", 2)
     for at in range(len(groups) + 2):
-        if at < len(groups):
-            for item in groups[at]:
-                item.first()
-        if 0 < at <= len(groups):
-            for item in groups[at - 1]:
-                item.second()
-        if at > 1:
-            for item in groups[at - 2]:
-                item.third()
+        run("first", at)
+        run("spread", at + 1)
+        run("cross", at + 2)
+        run("begin", at + 3)
+        moved += [start() for start in starts[at * share : (at + 1) * share]]
+        run("second", at - 1)
+        run("third", at - 2)
     for group in groups:
         for item in group:
             item.end()
@@ -259,7 +313,7 @@
         jax.ShapeDtypeStruct((LAYERS,) + sizes + (down.shape[1], r, width), low),
         jax.ShapeDtypeStruct((LAYERS,) + sizes + (8, width), low),
     ]
-    per_item = 1 + sum(n - 1 for n in sizes) + 4 + sizes[0] + sizes[3]
+    per_item = 3 + sum(n - 1 for n in sizes) + 4 + sizes[0] + sizes[3]
     count = 7 * LAYERS * per_item + members
     return pl.pallas_call(
         lambda *refs: bring_kernel(sizes, *refs),
@@ -345,6 +399,9 @@
         spot = axes.index(axis) + self.lead
 
         def add(at):
+            if size == 2 and into.dtype == LOW:
+                into[at] = ref[at[:spot] + (me,) + at[spot:]] + arrived[(0,) + at]
+                return
             total = wide(ref, at[:spot] + (me,) + at[spot:])
             for k in range(size - 1):
                 total = total + wide(arrived, (k,) + at)
@@ -361,7 +418,7 @@
         there.wait_recv()
 
         def add(at):
-            self.mine[at] = (wide(self.mine, at) + wide(self.theirs, at)).astype(LOW)
+            self.mine[at] = self.mine[at] + self.theirs[at]
 
         each(self.mine.shape[:-2], add)
         for copy in self.moving_first:

time: 669 us -> 653 us (0.976)
  Pallas kernels: 539 us -> 528 us
    pallas_call x1, Pallas kernels: 182 us -> 170 us  [bring(): pl.pallas_call(lambda *refs: bring_kernel(sizes, *refs), out_shape=outs,...]
  transfers between devices with their start and end apart: 2 -> 2, of which waited for: 0 -> 0; matrix products, arithmetic and copies ran while one was open for 3% -> 3% of each run, Pallas kernels for 23% -> 24%
where the time goes in v4:
time: 653 us; the launch traced here: 647 us
  Pallas kernels  528 us (81%)
  local copies, waits for them, and re-layouts  71.9 us (11%)
  other arithmetic  29.4 us (5%)
  starting transfers between devices  10.4 us (2%)
  between operations  8.01 us (1%)
    pallas_call x1, Pallas kernels, bring(): pl.pallas_call(lambda *refs: bring_kernel(sizes, *refs), out_shape=outs,...  170 us
    pallas_call x1, Pallas kernels, take_home(): pl.pallas_call(lambda *refs: home_kernel(sizes, legs, *refs), out_shape=o...  117 us
    pallas_call x2, Pallas kernels, attn_bwd(): pl.pallas_call(lambda *refs: attn_bwd_kernel(rider, *refs), grid=(bins,),...  77.4 us
    pallas_call x2, Pallas kernels, mlp_bwd(): pl.pallas_call(lambda *refs: mlp_bwd_kernel(count, rider, *refs), grid=(c...  69.5 us
    pallas_call x2, Pallas kernels, attn_fwd(): pl.pallas_call(attn_fwd_kernel, grid=(bins,), in_specs=[row(width), pl.Bl...  42.2 us
    pallas_call x2, Pallas kernels, mlp_fwd(): pl.pallas_call(lambda *refs: mlp_fwd_kernel(count, *refs), grid=(count,),...  33.5 us
    pallas_call x2, Pallas kernels, attn_dw(): pl.pallas_call(attn_dw_kernel, grid=(4,), in_specs=[whole, pl.BlockSpec((...  17.5 us
  transfers between devices with their start and end apart: 2, of which 0 were waited for; matrix products, arithmetic and copies ran while one was open for 3% of the time, Pallas kernels for 24%

profile of v4, /device:TPU:0, one launch (start us, length us, event | category | flops | bytes accessed | tf_op | source)
XLA Modules:
  0.0 647.4 jit_solution(12950483999329086573)
XLA Ops:
  8.1 3.9 gather_fusion.2
  12.0 2.1 gather_fusion.1
  15.6 4.3 broadcast_select_fusion.2
  19.9 170.3 %bring.1 = (bf16[2,2,8,48,768]{4,3,2,1,0:T(8,128)(2,1)}, bf16[2,8,2,2,4,2,24,768]{7,6,5,4,3,2,1,0:T(8,128)(2,1)}, bf16[2,2,2,4,2,4,24,768]{7,6,5,4,3,2,1,0:T(8,128)(2,1)}, bf16[2,2,2,4,2,8,768]{6,5,4,3,2,1,0:T(8,128)(2,1)}) custom-call(bf16[2,8,2,48,768]{4,3,2,1,0:T(8,128)(2,1)} %bitcast.206, bf16[2,8,24,768]{3,2,1,0:T(8,128)(2,1)} %pad_maximum_fusion.2.refs_1_, ...), custom_call_target="tpu_custom_call" | custom-call | tf_op jit(solution)/shard_map/bring/pallas_call | solution.py:318
  191.8 4.2 all-to-all-start
  221.3 20.9 %attn_fwd.2 = (bf16[768,2304]{1,0:T(8,128)(2,1)}, bf16[768,768]{1,0:T(8,128)(2,1)}, f32[768,128]{1,0:T(8,128)}, f32[768,768]{1,0:T(8,128)}) custom-call(bf16[768,768]{1,0:T(8,128)(2,1)} %pad_maximum_fusion.x_ref.act_ref, bf16[2,8,768,768]{3,2,1,0:T(8,128)(2,1)} %bitcast.181, f32[2,12,768]{2,1,0:T(8,128)} %copy-done.2, f32[2,384,384]{2,1,0:T(8,128)} %copy.154.mask_ref.refs_3_), custom_call_target="tpu_custom_call" | custom-call | tf_op jit(solution)/shard_map/attn_fwd/pallas_call | solution.py:817
  242.2 16.8 %mlp_fwd.2 = (f32[768,3072]{1,0:T(8,128)}, f32[768,768]{1,0:T(8,128)}, bf16[768,768]{1,0:T(8,128)(2,1)}, f32[768,768]{1,0:T(8,128)}, f32[768,128]{1,0:T(8,128)}) custom-call(f32[768,768]{1,0:T(8,128)} %get-tuple-element.77.refs_0_.refs_3_, bf16[2,8,768,768]{3,2,1,0:T(8,128)(2,1)} %bitcast.182, bf16[2,3072,768]{2,1,0:T(8,128)(2,1)} %bitcast.189, ...), custom_call_target="tpu_custom_call" | custom-call | tf_op jit(solution)/shard_map/mlp_fwd/pallas_call | solution.py:878
  259.0 21.3 %attn_fwd.3 = (bf16[768,2304]{1,0:T(8,128)(2,1)}, bf16[768,768]{1,0:T(8,128)(2,1)}, f32[768,128]{1,0:T(8,128)}, f32[768,768]{1,0:T(8,128)}) custom-call(f32[768,768]{1,0:T(8,128)} %get-tuple-element.79.x_ref, bf16[2,8,768,768]{3,2,1,0:T(8,128)(2,1)} %bitcast.183, f32[2,12,768]{2,1,0:T(8,128)} %copy-done.2, f32[2,384,384]{2,1,0:T(8,128)} %copy.154.mask_ref.refs_3_), custom_call_target="tpu_custom_call" | custom-call | tf_op jit(solution)/shard_map/attn_fwd/pallas_call | solution.py:817
  280.2 16.8 %mlp_fwd.3 = (f32[768,3072]{1,0:T(8,128)}, f32[768,768]{1,0:T(8,128)}, bf16[768,768]{1,0:T(8,128)(2,1)}, f32[768,768]{1,0:T(8,128)}, f32[768,128]{1,0:T(8,128)}) custom-call(f32[768,768]{1,0:T(8,128)} %get-tuple-element.80.refs_0_.refs_3_, bf16[2,8,768,768]{3,2,1,0:T(8,128)(2,1)} %bitcast.184, bf16[2,3072,768]{2,1,0:T(8,128)(2,1)} %bitcast.190, ...), custom_call_target="tpu_custom_call" | custom-call | tf_op jit(solution)/shard_map/mlp_fwd/pallas_call | solution.py:878
  299.8 1.9 copy.143
  303.7 3.9 copy.157
  307.6 6.2 all-to-all-start.1
  315.8 30.0 %mlp_bwd.1 = (bf16[4,768,768]{2,1,0:T(8,128)(2,1)}, bf16[3072,768]{1,0:T(8,128)(2,1)}, f32[768,768]{1,0:T(8,128)}, f32[12,768]{1,0:T(8,128)}) custom-call(bf16[768,768]{1,0:T(8,128)(2,1)} %pad_maximum_fusion.1.refs_0_, f32[768,768]{1,0:T(8,128)} %get-tuple-element.83.refs_1_, f32[768,128]{1,0:T(8,128)} %get-tuple-element.84.refs_2_, ...), custom_call_target="tpu_custom_call" | custom-call | tf_op jit(solution)/shard_map/mlp_bwd/pallas_call | solution.py:1044
  345.9 38.6 %attn_bwd_sums2.1 = (bf16[768,2304]{1,0:T(8,128)(2,1)}, f32[768,768]{1,0:T(8,128)}, bf16[768,768]{1,0:T(8,128)(2,1)}, f32[12,768]{1,0:T(8,128)}, bf16[2,4,2,24,7...) custom-call(f32[768,768]{1,0:T(8,128)} %get-tuple-element.87.refs_0_, ...), custom_call_target="tpu_custom_call" | custom-call | tf_op jit(solution)/shard_map/attn_bwd_sums2/pallas_call | solution.py:1128
  384.5 9.0 %attn_dw.2 = bf16[4,768,768]{2,1,0:T(8,128)(2,1)} custom-call(bf16[768,768]{1,0:T(8,128)(2,1)} %get-tuple-element.106.act_ref, bf16[768,2304]{1,0:T(8,128)(2,1)} %get-tuple-element.107.dqkv_ref, bf16[768,768]{1,0:T(8,128)(2,1)} %get-tuple-element.108.ctx_ref, bf16[768,768]{1,0:T(8,128)(2,1)} %get-tuple-element.109.low_ref), custom_call_target="tpu_custom_call" | custom-call | tf_op jit(solution)/shard_map/attn_dw/pallas_call | solution.py:1151
  393.5 3.4 copy.158
  396.8 39.5 %mlp_bwd_sums.1 = (bf16[4,768,768]{2,1,0:T(8,128)(2,1)}, bf16[3072,768]{1,0:T(8,128)(2,1)}, f32[768,768]{1,0:T(8,128)}, f32[12,768]{1,0:T(8,128)}, f32[4,24,768]...) custom-call(f32[768,768]{1,0:T(8,128)} %get-tuple-element.93.refs_0_, ...), custom_call_target="tpu_custom_call" | custom-call | tf_op jit(solution)/shard_map/mlp_bwd_sums/pallas_call | solution.py:1044
  436.3 38.8 %attn_bwd_sums4.1 = (bf16[768,2304]{1,0:T(8,128)(2,1)}, f32[768,768]{1,0:T(8,128)}, bf16[768,768]{1,0:T(8,128)(2,1)}, f32[12,768]{1,0:T(8,128)}, f32[4,24,768]{2...) custom-call(f32[768,768]{1,0:T(8,128)} %get-tuple-element.101.refs_0_, ...), custom_call_target="tpu_custom_call" | custom-call | tf_op jit(solution)/shard_map/attn_bwd_sums4/pallas_call | solution.py:1128
  478.6 8.5 %attn_dw.3 = bf16[4,768,768]{2,1,0:T(8,128)(2,1)} custom-call(bf16[768,768]{1,0:T(8,128)(2,1)} %pad_maximum_fusion.x_ref.act_ref, bf16[768,2304]{1,0:T(8,128)(2,1)} %get-tuple-element.114.dqkv_ref, bf16[768,768]{1,0:T(8,128)(2,1)} %get-tuple-element.115.ctx_ref, bf16[768,768]{1,0:T(8,128)(2,1)} %get-tuple-element.116.low_ref), custom_call_target="tpu_custom_call" | custom-call | tf_op jit(solution)/shard_map/attn_dw/pallas_call | solution.py:1151
  488.7 117.2 %take_home.1 = (f32[4,24,768]{2,1,0:T(8,128)}, f32[8,24,768]{2,1,0:T(8,128)}, f32[4,24,768]{2,1,0:T(8,128)}, f32[2,12,768]{2,1,0:T(8,128)}, bf16[2,8,2,48,768]{4,3,2,1,0:T(8,128)(2,1)}) custom-call(bf16[2,2,4,24,768]{4,3,2,1,0:T(8,128)(2,1)} %get-tuple-element.110.refs_0_, bf16[2,4,2,24,768]{4,3,2,1,0:T(8,128)(2,1)} %get-tuple-element.111.refs_1_, ...), custom_call_target="tpu_custom_call" | custom-call | tf_op jit(solution)/shard_map/take_home/pallas_call | solution.py:684
  615.2 2.0 copy.159
  617.5 2.1 gather_fusion.5
  619.6 3.8 gather_fusion.6
  642.9 4.3 broadcast_select_fusion
  (174 shorter events, 69.7 us)
Async XLA Ops:
  8.1 3.9 copy-start.4
  12.0 2.7 copy-start.10
  191.8 4.3 copy-start.25
  191.8 11.3 %copy-start.7 = (bf16[2,2,2,4,2,8,768]{6,5,4,3,2,1,0:T(8,128)(2,1)S(1)}, bf16[2,2,2,4,2,8,768]{6,5,4,3,2,1,0:T(8,128)(2,1)}, u32[]{:S(2)}) copy-start(bf16[2,2,2,4,2,8,768]{6,5,4,3,2,1,0:T(8,128)(2,1)} %get-tuple-element.76) | copy-start | bytes 2359300
  191.8 106.6 %all-to-all-start = ((bf16[2,8,2,48,768]{4,3,2,0,1:T(8,128)(2,1)}), bf16[2,8,2,48,768]{4,3,2,0,1:T(8,128)(2,1)S(1)}, u32[]{:S(2)}, u32[]{:S(2)}) async-start(bf16[2,8,2,48,768]{4,3,2,0,1:T(8,128)(2,1)} %copy.142), calls=%async_computation | async-start | bytes 4718592 | tf_op jit(solution)/shard_map/all_to_all | solution.py:1275
  196.0 11.7 %copy-start.11 = (s32[2,64,6,3]{1,0,3,2:T(2,128)S(1)}, s32[2,64,6,3]{1,0,3,2:T(2,128)}, u32[]{:S(2)}) copy-start(s32[2,64,6,3]{1,0,3,2:T(2,128)} %param.26) | copy-start | bytes 27652
  214.9 87.9 %copy-start.14 = (pred[384]{0:T(512)(128)(4,1)}, pred[384]{0:T(512)(128)(4,1)S(1)}, u32[]{:S(2)}) copy-start(pred[384]{0:T(512)(128)(4,1)S(1)} %iota_compare_fusion.4) | copy-start | bytes 1156
  215.5 98.9 %copy-start.16 = (pred[384]{0:T(512)(128)(4,1)}, pred[384]{0:T(512)(128)(4,1)S(1)}, u32[]{:S(2)}) copy-start(pred[384]{0:T(512)(128)(4,1)S(1)} %iota_compare_fusion.2) | copy-start | bytes 1156
  216.8 85.0 %copy-start.20 = (pred[384]{0:T(512)(128)(4,1)}, pred[384]{0:T(512)(128)(4,1)S(1)}, u32[]{:S(2)}) copy-start(pred[384]{0:T(512)(128)(4,1)S(1)} %iota_compare_fusion.3) | copy-start | bytes 1156
  217.5 85.3 %copy-start.18 = (pred[384]{0:T(512)(128)(4,1)}, pred[384]{0:T(512)(128)(4,1)S(1)}, u32[]{:S(2)}) copy-start(pred[384]{0:T(512)(128)(4,1)S(1)} %iota_compare_fusion.1) | copy-start | bytes 1156
  280.2 18.1 %copy-start.26 = (pred[768]{0:T(1024)(128)(4,1)S(1)}, pred[768]{0:T(1024)(128)(4,1)}, u32[]{:S(2)}) copy-start(pred[768]{0:T(1024)(128)(4,1)} %constant.114.clone.1) | copy-start | bytes 2308
  298.4 4.3 copy-start.23
  299.8 2.0 copy-start.3
  307.6 85.9 %all-to-all-start.1 = ((bf16[2,1,2,384,768]{4,2,0,1,3:T(2,128)(2,1)}), bf16[2,1,2,384,768]{4,2,0,1,3:T(2,128)(2,1)}, u32[]{:S(2)}, u32[]{:S(2)}) async-start(bf16[2,1,2,384,768]{4,2,0,1,3:T(2,128)(2,1)} %copy.157), calls=%async_computation.1 | async-start | bytes 4718592 | tf_op jit(solution)/shard_map/all_to_all | solution.py:1311
  475.1 1.9 copy-start.15
  475.2 1.9 copy-start.17
  475.2 1.8 copy-start.21
  475.2 1.8 copy-start.24
  615.2 2.0 copy-start.8
  615.2 2.3 copy-start.5
  619.6 3.8 copy-start.9
  634.3 8.6 %copy-start.1 = (bf16[32,48,768]{2,1,0:T(8,128)(2,1)S(1)}, bf16[32,48,768]{2,1,0:T(8,128)(2,1)}, u32[]{:S(2)}) copy-start(bf16[32,48,768]{2,1,0:T(8,128)(2,1)} %gather_fusion.5) | copy-start | bytes 7077892
  634.3 8.6 %copy-start.22 = (pred[2,16]{1,0:T(4,128)(4,1)S(1)}, pred[2,16]{1,0:T(4,128)(4,1)}, u32[]{:S(2)}) copy-start(pred[2,16]{1,0:T(4,128)(4,1)} %get-tuple-element.194) | copy-start | bytes 100
  636.4 5.7 copy-start.6
  (5 other events, 5.7 us)

commit v5 on v4

--- a/solution.py
+++ b/solution.py
@@ -371,7 +371,10 @@
             self.stages = [self.take_up, self.add_second, self.add_last, self.nothing]
             if leg == "both":
                 self.stages = [self.add_core, self.add_first, self.add_second, self.add_last]
-        self.result = links.plan_here(self.out, out_ref)
+        if isinstance(out_ref, list):
+            self.results = [links.plan_here(self.out.at[j], ref) for j, ref in enumerate(out_ref)]
+        else:
+            self.results = [links.plan_here(self.out, out_ref)]
 
     def send(self, source, target, axis, offset):
         copy = self.links.plan(source, target, self.links.along(axis, offset))
@@ -428,7 +431,7 @@
         for copy in self.moving_first:
             copy.wait_recv()
         self.fold(self.mine, (0, 2, 3), self.order[0], self.first, self.half)
-        for copy in [self.result] if self.leg == "early" else self.moving_second:
+        for copy in self.results if self.leg == "early" else self.moving_second:
             copy.start()
 
     def take_up(self):
@@ -447,10 +450,12 @@
         for copy in self.moving_last:
             copy.wait_recv()
         self.fold(self.quarter, (2,), 2, self.last, self.out)
-        self.result.start()
+        for copy in self.results:
+            copy.start()
 
     def end(self):
-        self.result.wait()
+        for copy in self.results:
+            copy.wait()
         for copy in self.sent:
             copy.wait_send()
 
@@ -538,7 +543,7 @@
 
 
 def sum_count(sizes):
-    return 3 + sum(n - 1 for n in sizes)
+    return 4 + sum(n - 1 for n in sizes)
 
 
 def source_of_core(kind, array, start):
@@ -619,10 +624,19 @@
 
 def home_kernel(sizes, legs, *refs):
     inputs, refs = refs[: len(legs) + 1], refs[len(legs) + 1 :]
-    vec, sent, late_sum, g_square, g_down, g_vec, back = refs[:7]
-    links = Links(sizes, *refs[7:9])
-    whole = Whole(links, vec, refs[9:18], g_vec)
-    refs = list(refs[18:])
+    vec, sent, late_up, late_down, g_qkv, g_out, g_up, g_down, g_vec, back = refs[:10]
+    links = Links(sizes, *refs[10:12])
+    whole = Whole(links, vec, refs[12:21], g_vec)
+    refs = list(refs[21:])
+    width = vec.shape[-1]
+
+    def place(layer_at, kind, j):
+        if kind == "down":
+            return g_down.at[layer_at, j]
+        if kind == "attn" and j == 3:
+            return g_out.at[layer_at]
+        return (g_qkv if kind == "attn" else g_up).at[layer_at, :, j * width : (j + 1) * width]
+
     links.greet(links.partners())
     inputs = list(inputs)
     groups = []
@@ -634,14 +648,8 @@
             count = 5 if leg == "late" else 8
             bufs = refs[:count]
             del refs[:count]
-            blocks = slice(start, start + 2)
-            if leg == "late":
-                source, out = inputs.pop(0), late_sum.at[blocks]
-            else:
-                source = source_of_core(kind, array, start)
-                out = g_down.at[blocks] if kind == "down" else None
-                if out is None:
-                    out = g_square.at[blocks if kind == "attn" else slice(start + 4, start + 6)]
+            source = inputs.pop(0) if leg == "late" else source_of_core(kind, array, start)
+            out = [place(int(leg == "late"), kind, j) for j in (start, start + 1)]
             group.append(Sum(links, source, order, len(lead), bufs, out, leg))
         groups.append(group)
     groups[0].append(whole)
@@ -649,6 +657,9 @@
     for item in sums:
         item.begin()
     moved = deal_back(links, sent, back)
+    for j in range(4):
+        moved.append(links.start_here(late_up.at[j], place(1, "up", j)))
+        moved.append(links.start_here(late_down.at[j], place(1, "down", j)))
     for turn in range(len(groups) + 3):
         for depth in range(4):
             if 0 <= turn - depth < len(groups):
@@ -660,7 +671,7 @@
         copy.wait()
 
 
-def take_home(sizes, halves, grads, vec, sent):
+def take_home(sizes, halves, grads, vec, sent, late):
     dws, dwu, dwd = grads
     r, width = dws.shape[-2:]
     legs = [("attn", "late"), ("down", "both"), ("up", "both"), ("attn", "both")]
@@ -668,18 +679,19 @@
     f32 = jnp.float32
     batch, two, count, rows = sent.shape[:4]
     outs = [
-        jax.ShapeDtypeStruct((4, r, width), f32),
-        jax.ShapeDtypeStruct((8, r, width), f32),
-        jax.ShapeDtypeStruct((4, r, width), f32),
+        jax.ShapeDtypeStruct((LAYERS, r, 3 * width), f32),
+        jax.ShapeDtypeStruct((LAYERS, r, width), f32),
+        jax.ShapeDtypeStruct((LAYERS, r, 4 * width), f32),
+        jax.ShapeDtypeStruct((LAYERS, 4, r, width), f32),
         jax.ShapeDtypeStruct(vec.shape, f32),
         jax.ShapeDtypeStruct((batch, count, two, rows, width), LOW),
     ]
-    args = [*halves, dwd, dwu, dws, vec, sent]
+    args = [*halves, dwd, dwu, dws, vec, sent, *late]
     scratch = whole_buffers(sizes, vec.shape)
     for kind, leg in legs:
         for order, start, lead, tail in pair_of(kind, r, width):
             scratch += sum_buffers(sizes, order, lead, tail, leg)
-    count = (2 * len(legs) + 1) * sum_count(sizes) + members
+    count = (2 * len(legs) + 1) * sum_count(sizes) + members + 8
     sems = [pltpu.SemaphoreType.DMA((count,)), pltpu.SemaphoreType.DMA((count,))]
     return pl.pallas_call(
         lambda *refs: home_kernel(sizes, legs, *refs),
@@ -1314,16 +1326,15 @@
     grad, back, (g_up, g_down_late), left = backward_layers(grad, back, kept, w, mask, grid.sizes, rows)
     output = in_order(back)
     sent = to_slots(grad.astype(LOW)).reshape(batch_count, 2, members, rows_dev, width)
-    g_attn, g_square, g_down, g_vec, back = take_home(grid.sizes, *left, sent)
+    g_qkv, g_out, g_up, g_down, g_vec, back = take_home(
+        grid.sizes, *left, sent, (g_up, g_down_late)
+    )
     input_grad = in_order(back)
-    beside = lambda *pairs: jnp.stack(
-        [blocks.transpose(1, 0, 2).reshape(rows, -1) for blocks in pairs]
-    )
     out = {
-        "wqkv": beside(g_square[:3], g_attn[:3]),
-        "wo": jnp.stack([g_square[3], g_attn[3]]),
-        "wu": beside(g_square[4:], g_up),
-        "wd": jnp.stack([g_down.reshape(-1, width), g_down_late.reshape(-1, width)]),
+        "wqkv": g_qkv,
+        "wo": g_out,
+        "wu": g_up,
+        "wd": g_down.reshape(LAYERS, -1, width),
     }
     place = group_at * members + member
     for at, name in enumerate(SMALL):

time: 653 us -> 636 us (0.974)
  local copies, waits for them, and re-layouts: 71.9 us -> 59.4 us
where the time goes in v5:
time: 636 us; the launch traced here: 630 us
  Pallas kernels  528 us (83%)
  local copies, waits for them, and re-layouts  59.4 us (9%)
  other arithmetic  24.4 us (4%)
  starting transfers between devices  10.2 us (2%)
  between operations  8.02 us (1%)
    pallas_call x1, Pallas kernels, bring(): pl.pallas_call(lambda *refs: bring_kernel(sizes, *refs), out_shape=outs,...  170 us
    pallas_call x1, Pallas kernels, take_home(): pl.pallas_call(lambda *refs: home_kernel(sizes, legs, *refs), out_shape=o...  117 us
    pallas_call x2, Pallas kernels, attn_bwd(): pl.pallas_call(lambda *refs: attn_bwd_kernel(rider, *refs), grid=(bins,),...  77.6 us
    pallas_call x2, Pallas kernels, mlp_bwd(): pl.pallas_call(lambda *refs: mlp_bwd_kernel(count, rider, *refs), grid=(c...  69.6 us
    pallas_call x2, Pallas kernels, attn_fwd(): pl.pallas_call(attn_fwd_kernel, grid=(bins,), in_specs=[row(width), pl.Bl...  42.5 us
    pallas_call x2, Pallas kernels, mlp_fwd(): pl.pallas_call(lambda *refs: mlp_fwd_kernel(count, *refs), grid=(count,),...  33.5 us
    pallas_call x2, Pallas kernels, attn_dw(): pl.pallas_call(attn_dw_kernel, grid=(4,), in_specs=[whole, pl.BlockSpec((...  17.3 us
  transfers between devices with their start and end apart: 2, of which 0 were waited for; matrix products, arithmetic and copies ran while one was open for 3% of the time, Pallas kernels for 24%

profile of v5, /device:TPU:0, one launch (start us, length us, event | category | flops | bytes accessed | tf_op | source)
XLA Modules:
  0.0 630.3 jit_solution(11369033587599318740)
XLA Ops:
  8.1 3.9 gather_fusion.2
  12.0 2.1 gather_fusion.1
  15.6 4.3 broadcast_select_fusion.2
  19.9 170.3 %bring.1 = (bf16[2,2,8,48,768]{4,3,2,1,0:T(8,128)(2,1)}, bf16[2,8,2,2,4,2,24,768]{7,6,5,4,3,2,1,0:T(8,128)(2,1)}, bf16[2,2,2,4,2,4,24,768]{7,6,5,4,3,2,1,0:T(8,128)(2,1)}, bf16[2,2,2,4,2,8,768]{6,5,4,3,2,1,0:T(8,128)(2,1)}) custom-call(bf16[2,8,2,48,768]{4,3,2,1,0:T(8,128)(2,1)} %bitcast.198, bf16[2,8,24,768]{3,2,1,0:T(8,128)(2,1)} %pad_maximum_fusion.2.refs_1_, ...), custom_call_target="tpu_custom_call" | custom-call | tf_op jit(solution)/shard_map/bring/pallas_call | solution.py:318
  191.8 4.0 all-to-all-start
  221.2 20.9 %attn_fwd.2 = (bf16[768,2304]{1,0:T(8,128)(2,1)}, bf16[768,768]{1,0:T(8,128)(2,1)}, f32[768,128]{1,0:T(8,128)}, f32[768,768]{1,0:T(8,128)}) custom-call(bf16[768,768]{1,0:T(8,128)(2,1)} %pad_maximum_fusion.x_ref.act_ref, bf16[2,8,768,768]{3,2,1,0:T(8,128)(2,1)} %bitcast.173, f32[2,12,768]{2,1,0:T(8,128)} %copy-done.2, f32[2,384,384]{2,1,0:T(8,128)} %copy.138.mask_ref.refs_3_), custom_call_target="tpu_custom_call" | custom-call | tf_op jit(solution)/shard_map/attn_fwd/pallas_call | solution.py:829
  242.1 16.8 %mlp_fwd.2 = (f32[768,3072]{1,0:T(8,128)}, f32[768,768]{1,0:T(8,128)}, bf16[768,768]{1,0:T(8,128)(2,1)}, f32[768,768]{1,0:T(8,128)}, f32[768,128]{1,0:T(8,128)}) custom-call(f32[768,768]{1,0:T(8,128)} %get-tuple-element.78.refs_0_.refs_3_, bf16[2,8,768,768]{3,2,1,0:T(8,128)(2,1)} %bitcast.174, bf16[2,3072,768]{2,1,0:T(8,128)(2,1)} %bitcast.181, ...), custom_call_target="tpu_custom_call" | custom-call | tf_op jit(solution)/shard_map/mlp_fwd/pallas_call | solution.py:890
  258.8 21.6 %attn_fwd.3 = (bf16[768,2304]{1,0:T(8,128)(2,1)}, bf16[768,768]{1,0:T(8,128)(2,1)}, f32[768,128]{1,0:T(8,128)}, f32[768,768]{1,0:T(8,128)}) custom-call(f32[768,768]{1,0:T(8,128)} %get-tuple-element.80.x_ref, bf16[2,8,768,768]{3,2,1,0:T(8,128)(2,1)} %bitcast.175, f32[2,12,768]{2,1,0:T(8,128)} %copy-done.2, f32[2,384,384]{2,1,0:T(8,128)} %copy.138.mask_ref.refs_3_), custom_call_target="tpu_custom_call" | custom-call | tf_op jit(solution)/shard_map/attn_fwd/pallas_call | solution.py:829
  280.4 16.8 %mlp_fwd.3 = (f32[768,3072]{1,0:T(8,128)}, f32[768,768]{1,0:T(8,128)}, bf16[768,768]{1,0:T(8,128)(2,1)}, f32[768,768]{1,0:T(8,128)}, f32[768,128]{1,0:T(8,128)}) custom-call(f32[768,768]{1,0:T(8,128)} %get-tuple-element.81.refs_0_.refs_3_, bf16[2,8,768,768]{3,2,1,0:T(8,128)(2,1)} %bitcast.176, bf16[2,3072,768]{2,1,0:T(8,128)(2,1)} %bitcast.182, ...), custom_call_target="tpu_custom_call" | custom-call | tf_op jit(solution)/shard_map/mlp_fwd/pallas_call | solution.py:890
  300.0 1.9 copy.127
  303.9 3.9 copy.141
  307.8 6.2 all-to-all-start.1
  316.0 30.0 %mlp_bwd.1 = (bf16[4,768,768]{2,1,0:T(8,128)(2,1)}, bf16[3072,768]{1,0:T(8,128)(2,1)}, f32[768,768]{1,0:T(8,128)}, f32[12,768]{1,0:T(8,128)}) custom-call(bf16[768,768]{1,0:T(8,128)(2,1)} %pad_maximum_fusion.1.refs_0_, f32[768,768]{1,0:T(8,128)} %get-tuple-element.84.refs_1_, f32[768,128]{1,0:T(8,128)} %get-tuple-element.85.refs_2_, ...), custom_call_target="tpu_custom_call" | custom-call | tf_op jit(solution)/shard_map/mlp_bwd/pallas_call | solution.py:1056
  346.0 38.7 %attn_bwd_sums2.1 = (bf16[768,2304]{1,0:T(8,128)(2,1)}, f32[768,768]{1,0:T(8,128)}, bf16[768,768]{1,0:T(8,128)(2,1)}, f32[12,768]{1,0:T(8,128)}, bf16[2,4,2,24,7...) custom-call(f32[768,768]{1,0:T(8,128)} %get-tuple-element.88.refs_0_, ...), custom_call_target="tpu_custom_call" | custom-call | tf_op jit(solution)/shard_map/attn_bwd_sums2/pallas_call | solution.py:1140
  384.7 8.8 %attn_dw.2 = bf16[4,768,768]{2,1,0:T(8,128)(2,1)} custom-call(bf16[768,768]{1,0:T(8,128)(2,1)} %get-tuple-element.107.act_ref, bf16[768,2304]{1,0:T(8,128)(2,1)} %get-tuple-element.108.dqkv_ref, bf16[768,768]{1,0:T(8,128)(2,1)} %get-tuple-element.109.ctx_ref, bf16[768,768]{1,0:T(8,128)(2,1)} %get-tuple-element.110.low_ref), custom_call_target="tpu_custom_call" | custom-call | tf_op jit(solution)/shard_map/attn_dw/pallas_call | solution.py:1163
  393.5 3.4 copy.142
  396.8 39.6 %mlp_bwd_sums.1 = (bf16[4,768,768]{2,1,0:T(8,128)(2,1)}, bf16[3072,768]{1,0:T(8,128)(2,1)}, f32[768,768]{1,0:T(8,128)}, f32[12,768]{1,0:T(8,128)}, f32[4,24,768]...) custom-call(f32[768,768]{1,0:T(8,128)} %get-tuple-element.94.refs_0_, ...), custom_call_target="tpu_custom_call" | custom-call | tf_op jit(solution)/shard_map/mlp_bwd_sums/pallas_call | solution.py:1056
  436.4 39.0 %attn_bwd_sums4.1 = (bf16[768,2304]{1,0:T(8,128)(2,1)}, f32[768,768]{1,0:T(8,128)}, bf16[768,768]{1,0:T(8,128)(2,1)}, f32[12,768]{1,0:T(8,128)}, f32[4,24,768]{2...) custom-call(f32[768,768]{1,0:T(8,128)} %get-tuple-element.102.refs_0_, ...), custom_call_target="tpu_custom_call" | custom-call | tf_op jit(solution)/shard_map/attn_bwd_sums4/pallas_call | solution.py:1140
  478.8 8.5 %attn_dw.3 = bf16[4,768,768]{2,1,0:T(8,128)(2,1)} custom-call(bf16[768,768]{1,0:T(8,128)(2,1)} %pad_maximum_fusion.x_ref.act_ref, bf16[768,2304]{1,0:T(8,128)(2,1)} %get-tuple-element.115.dqkv_ref, bf16[768,768]{1,0:T(8,128)(2,1)} %get-tuple-element.116.ctx_ref, bf16[768,768]{1,0:T(8,128)(2,1)} %get-tuple-element.117.low_ref), custom_call_target="tpu_custom_call" | custom-call | tf_op jit(solution)/shard_map/attn_dw/pallas_call | solution.py:1163
  489.0 117.5 %take_home.1 = (f32[2,24,2304]{2,1,0:T(8,128)}, f32[2,24,768]{2,1,0:T(8,128)}, f32[2,24,3072]{2,1,0:T(8,128)}, f32[2,4,24,768]{3,2,1,0:T(8,128)}, f32[2,12,768]{...) custom-call(bf16[2,2,4,24,768]{4,3,2,1,0:T(8,128)(2,1)} %get-tuple-element.111.refs_0_, ...), custom_call_target="tpu_custom_call" | custom-call | tf_op jit(solution)/shard_map/take_home/pallas_call | solution.py:696
  608.8 1.9 copy.143
  610.8 2.1 gather_fusion.5
  612.9 3.9 gather_fusion.6
  622.6 4.4 broadcast_select_fusion
  (163 shorter events, 51.9 us)
Async XLA Ops:
  8.1 3.9 copy-start.4
  12.0 2.7 copy-start.11
  191.8 4.2 copy-start.26
  191.8 11.1 %copy-start.6 = (bf16[2,2,2,4,2,8,768]{6,5,4,3,2,1,0:T(8,128)(2,1)S(1)}, bf16[2,2,2,4,2,8,768]{6,5,4,3,2,1,0:T(8,128)(2,1)}, u32[]{:S(2)}) copy-start(bf16[2,2,2,4,2,8,768]{6,5,4,3,2,1,0:T(8,128)(2,1)} %get-tuple-element.77) | copy-start | bytes 2359300
  191.8 106.8 %all-to-all-start = ((bf16[2,8,2,48,768]{4,3,2,0,1:T(8,128)(2,1)}), bf16[2,8,2,48,768]{4,3,2,0,1:T(8,128)(2,1)S(1)}, u32[]{:S(2)}, u32[]{:S(2)}) async-start(bf16[2,8,2,48,768]{4,3,2,0,1:T(8,128)(2,1)} %copy.126), calls=%async_computation | async-start | bytes 4718592 | tf_op jit(solution)/shard_map/all_to_all | solution.py:1287
  195.8 11.7 %copy-start.12 = (s32[2,64,6,3]{1,0,3,2:T(2,128)S(1)}, s32[2,64,6,3]{1,0,3,2:T(2,128)}, u32[]{:S(2)}) copy-start(s32[2,64,6,3]{1,0,3,2:T(2,128)} %param.26) | copy-start | bytes 27652
  214.7 88.2 %copy-start.15 = (pred[384]{0:T(512)(128)(4,1)}, pred[384]{0:T(512)(128)(4,1)S(1)}, u32[]{:S(2)}) copy-start(pred[384]{0:T(512)(128)(4,1)S(1)} %iota_compare_fusion.4) | copy-start | bytes 1156
  215.4 99.2 %copy-start.17 = (pred[384]{0:T(512)(128)(4,1)}, pred[384]{0:T(512)(128)(4,1)S(1)}, u32[]{:S(2)}) copy-start(pred[384]{0:T(512)(128)(4,1)S(1)} %iota_compare_fusion.2) | copy-start | bytes 1156
  216.7 85.3 %copy-start.21 = (pred[384]{0:T(512)(128)(4,1)}, pred[384]{0:T(512)(128)(4,1)S(1)}, u32[]{:S(2)}) copy-start(pred[384]{0:T(512)(128)(4,1)S(1)} %iota_compare_fusion.3) | copy-start | bytes 1156
  217.3 85.6 %copy-start.19 = (pred[384]{0:T(512)(128)(4,1)}, pred[384]{0:T(512)(128)(4,1)S(1)}, u32[]{:S(2)}) copy-start(pred[384]{0:T(512)(128)(4,1)S(1)} %iota_compare_fusion.1) | copy-start | bytes 1156
  280.4 18.1 %copy-start.27 = (pred[768]{0:T(1024)(128)(4,1)S(1)}, pred[768]{0:T(1024)(128)(4,1)}, u32[]{:S(2)}) copy-start(pred[768]{0:T(1024)(128)(4,1)} %constant.114.clone.1) | copy-start | bytes 2308
  298.6 4.3 copy-start.24
  300.0 2.0 copy-start.3
  307.8 85.7 %all-to-all-start.1 = ((bf16[2,1,2,384,768]{4,2,0,1,3:T(2,128)(2,1)}), bf16[2,1,2,384,768]{4,2,0,1,3:T(2,128)(2,1)}, u32[]{:S(2)}, u32[]{:S(2)}) async-start(bf16[2,1,2,384,768]{4,2,0,1,3:T(2,128)(2,1)} %copy.141), calls=%async_computation.1 | async-start | bytes 4718592 | tf_op jit(solution)/shard_map/all_to_all | solution.py:1323
  475.4 1.9 copy-start.16
  475.4 1.9 copy-start.18
  475.4 1.8 copy-start.22
  608.8 1.9 copy-start.5
  612.9 9.7 %copy-start.1 = (bf16[32,48,768]{2,1,0:T(8,128)(2,1)S(1)}, bf16[32,48,768]{2,1,0:T(8,128)(2,1)}, u32[]{:S(2)}) copy-start(bf16[32,48,768]{2,1,0:T(8,128)(2,1)} %gather_fusion.5) | copy-start | bytes 7077892
  612.9 9.7 %copy-start.23 = (pred[2,16]{1,0:T(4,128)(4,1)S(1)}, pred[2,16]{1,0:T(4,128)(4,1)}, u32[]{:S(2)}) copy-start(pred[2,16]{1,0:T(4,128)(4,1)} %get-tuple-element.196) | copy-start | bytes 100
  622.5 4.5 copy-start.9
  622.5 5.2 copy-start.10
  622.5 5.9 copy-start.8
  627.0 2.3 copy-start.7
  (6 other events, 7.5 us)

commit v6 on v5

--- a/solution.py
+++ b/solution.py
@@ -1337,10 +1337,12 @@
         "wd": g_down.reshape(LAYERS, -1, width),
     }
     place = group_at * members + member
-    for at, name in enumerate(SMALL):
-        values = g_vec[:, at:].reshape(LAYERS, -1) if name == "bu" else g_vec[:, at]
-        count = rows * (values.shape[1] // width)
-        out[name] = lax.dynamic_slice_in_dim(values, place * count, count, 1)
+    even = lax.dynamic_slice(g_vec, (0, 0, place * rows), (LAYERS, BU, rows))
+    for at, name in enumerate(SMALL[:BU]):
+        out[name] = even[:, at]
+    parts = g_vec[:, BU:].reshape(LAYERS, -1)
+    count = parts.shape[1] // grid.count
+    out["bu"] = lax.dynamic_slice_in_dim(parts, place * count, count, 1)
     return (output, input_grad) + tuple(out[name] for name in names)
 
 

time: 636 us -> 627 us (0.986)
  local copies, waits for them, and re-layouts: 59.4 us -> 49.7 us
  transfers between devices with their start and end apart: 2 -> 2, of which waited for: 0 -> 0; matrix products, arithmetic and copies ran while one was open for 3% -> 4% of each run, Pallas kernels for 24% -> 25%
where the time goes in v6:
time: 627 us; the launch traced here: 622 us
  Pallas kernels  528 us (84%)
  local copies, waits for them, and re-layouts  49.7 us (8%)
  other arithmetic  25.1 us (4%)
  starting transfers between devices  10.2 us (2%)
  between operations  8.24 us (1%)
    pallas_call x1, Pallas kernels, bring(): pl.pallas_call(lambda *refs: bring_kernel(sizes, *refs), out_shape=outs,...  170 us
    pallas_call x1, Pallas kernels, take_home(): pl.pallas_call(lambda *refs: home_kernel(sizes, legs, *refs), out_shape=o...  117 us
    pallas_call x2, Pallas kernels, attn_bwd(): pl.pallas_call(lambda *refs: attn_bwd_kernel(rider, *refs), grid=(bins,),...  77.6 us
    pallas_call x2, Pallas kernels, mlp_bwd(): pl.pallas_call(lambda *refs: mlp_bwd_kernel(count, rider, *refs), grid=(c...  69.6 us
    pallas_call x2, Pallas kernels, attn_fwd(): pl.pallas_call(attn_fwd_kernel, grid=(bins,), in_specs=[row(width), pl.Bl...  42.5 us
    pallas_call x2, Pallas kernels, mlp_fwd(): pl.pallas_call(lambda *refs: mlp_fwd_kernel(count, *refs), grid=(count,),...  33.6 us
    pallas_call x2, Pallas kernels, attn_dw(): pl.pallas_call(attn_dw_kernel, grid=(4,), in_specs=[whole, pl.BlockSpec((...  17.3 us
  transfers between devices with their start and end apart: 2, of which 0 were waited for; matrix products, arithmetic and copies ran while one was open for 4% of the time, Pallas kernels for 25%

profile of v6, /device:TPU:0, one launch (start us, length us, event | category | flops | bytes accessed | tf_op | source)
XLA Modules:
  0.0 621.7 jit_solution(15618080397947142050)
XLA Ops:
  2.0 2.4 gather_fusion.2
  4.6 3.8 gather_fusion.1
  9.5 4.4 broadcast_select_fusion.2
  14.8 170.3 %bring.1 = (bf16[2,2,8,48,768]{4,3,2,1,0:T(8,128)(2,1)}, bf16[2,8,2,2,4,2,24,768]{7,6,5,4,3,2,1,0:T(8,128)(2,1)}, bf16[2,2,2,4,2,4,24,768]{7,6,5,4,3,2,1,0:T(8,128)(2,1)}, bf16[2,2,2,4,2,8,768]{6,5,4,3,2,1,0:T(8,128)(2,1)}) custom-call(bf16[2,8,2,48,768]{4,3,2,1,0:T(8,128)(2,1)} %bitcast.198, bf16[2,8,24,768]{3,2,1,0:T(8,128)(2,1)} %pad_maximum_fusion.2.refs_1_, ...), custom_call_target="tpu_custom_call" | custom-call | tf_op jit(solution)/shard_map/bring/pallas_call | solution.py:318
  186.7 4.0 all-to-all-start
  216.1 20.9 %attn_fwd.2 = (bf16[768,2304]{1,0:T(8,128)(2,1)}, bf16[768,768]{1,0:T(8,128)(2,1)}, f32[768,128]{1,0:T(8,128)}, f32[768,768]{1,0:T(8,128)}) custom-call(bf16[768,768]{1,0:T(8,128)(2,1)} %pad_maximum_fusion.x_ref.act_ref, bf16[2,8,768,768]{3,2,1,0:T(8,128)(2,1)} %bitcast.173, f32[2,12,768]{2,1,0:T(8,128)} %copy-done.4, f32[2,384,384]{2,1,0:T(8,128)} %copy.138.mask_ref.refs_3_), custom_call_target="tpu_custom_call" | custom-call | tf_op jit(solution)/shard_map/attn_fwd/pallas_call | solution.py:829
  237.0 16.8 %mlp_fwd.2 = (f32[768,3072]{1,0:T(8,128)}, f32[768,768]{1,0:T(8,128)}, bf16[768,768]{1,0:T(8,128)(2,1)}, f32[768,768]{1,0:T(8,128)}, f32[768,128]{1,0:T(8,128)}) custom-call(f32[768,768]{1,0:T(8,128)} %get-tuple-element.78.refs_0_.refs_3_, bf16[2,8,768,768]{3,2,1,0:T(8,128)(2,1)} %bitcast.174, bf16[2,3072,768]{2,1,0:T(8,128)(2,1)} %bitcast.181, ...), custom_call_target="tpu_custom_call" | custom-call | tf_op jit(solution)/shard_map/mlp_fwd/pallas_call | solution.py:890
  253.7 21.6 %attn_fwd.3 = (bf16[768,2304]{1,0:T(8,128)(2,1)}, bf16[768,768]{1,0:T(8,128)(2,1)}, f32[768,128]{1,0:T(8,128)}, f32[768,768]{1,0:T(8,128)}) custom-call(f32[768,768]{1,0:T(8,128)} %get-tuple-element.80.x_ref, bf16[2,8,768,768]{3,2,1,0:T(8,128)(2,1)} %bitcast.175, f32[2,12,768]{2,1,0:T(8,128)} %copy-done.4, f32[2,384,384]{2,1,0:T(8,128)} %copy.138.mask_ref.refs_3_), custom_call_target="tpu_custom_call" | custom-call | tf_op jit(solution)/shard_map/attn_fwd/pallas_call | solution.py:829
  275.3 16.8 %mlp_fwd.3 = (f32[768,3072]{1,0:T(8,128)}, f32[768,768]{1,0:T(8,128)}, bf16[768,768]{1,0:T(8,128)(2,1)}, f32[768,768]{1,0:T(8,128)}, f32[768,128]{1,0:T(8,128)}) custom-call(f32[768,768]{1,0:T(8,128)} %get-tuple-element.81.refs_0_.refs_3_, bf16[2,8,768,768]{3,2,1,0:T(8,128)(2,1)} %bitcast.176, bf16[2,3072,768]{2,1,0:T(8,128)(2,1)} %bitcast.182, ...), custom_call_target="tpu_custom_call" | custom-call | tf_op jit(solution)/shard_map/mlp_fwd/pallas_call | solution.py:890
  295.0 1.9 copy.127
  298.9 3.9 copy.141
  302.8 6.2 all-to-all-start.1
  311.0 30.0 %mlp_bwd.1 = (bf16[4,768,768]{2,1,0:T(8,128)(2,1)}, bf16[3072,768]{1,0:T(8,128)(2,1)}, f32[768,768]{1,0:T(8,128)}, f32[12,768]{1,0:T(8,128)}) custom-call(bf16[768,768]{1,0:T(8,128)(2,1)} %pad_maximum_fusion.1.refs_0_, f32[768,768]{1,0:T(8,128)} %get-tuple-element.84.refs_1_, f32[768,128]{1,0:T(8,128)} %get-tuple-element.85.refs_2_, ...), custom_call_target="tpu_custom_call" | custom-call | tf_op jit(solution)/shard_map/mlp_bwd/pallas_call | solution.py:1056
  341.0 38.6 %attn_bwd_sums2.1 = (bf16[768,2304]{1,0:T(8,128)(2,1)}, f32[768,768]{1,0:T(8,128)}, bf16[768,768]{1,0:T(8,128)(2,1)}, f32[12,768]{1,0:T(8,128)}, bf16[2,4,2,24,7...) custom-call(f32[768,768]{1,0:T(8,128)} %get-tuple-element.88.refs_0_, ...), custom_call_target="tpu_custom_call" | custom-call | tf_op jit(solution)/shard_map/attn_bwd_sums2/pallas_call | solution.py:1140
  379.7 8.8 %attn_dw.2 = bf16[4,768,768]{2,1,0:T(8,128)(2,1)} custom-call(bf16[768,768]{1,0:T(8,128)(2,1)} %get-tuple-element.107.act_ref, bf16[768,2304]{1,0:T(8,128)(2,1)} %get-tuple-element.108.dqkv_ref, bf16[768,768]{1,0:T(8,128)(2,1)} %get-tuple-element.109.ctx_ref, bf16[768,768]{1,0:T(8,128)(2,1)} %get-tuple-element.110.low_ref), custom_call_target="tpu_custom_call" | custom-call | tf_op jit(solution)/shard_map/attn_dw/pallas_call | solution.py:1163
  388.5 3.4 copy.142
  391.8 39.6 %mlp_bwd_sums.1 = (bf16[4,768,768]{2,1,0:T(8,128)(2,1)}, bf16[3072,768]{1,0:T(8,128)(2,1)}, f32[768,768]{1,0:T(8,128)}, f32[12,768]{1,0:T(8,128)}, f32[4,24,768]...) custom-call(f32[768,768]{1,0:T(8,128)} %get-tuple-element.94.refs_0_, ...), custom_call_target="tpu_custom_call" | custom-call | tf_op jit(solution)/shard_map/mlp_bwd_sums/pallas_call | solution.py:1056
  431.4 39.0 %attn_bwd_sums4.1 = (bf16[768,2304]{1,0:T(8,128)(2,1)}, f32[768,768]{1,0:T(8,128)}, bf16[768,768]{1,0:T(8,128)(2,1)}, f32[12,768]{1,0:T(8,128)}, f32[4,24,768]{2...) custom-call(f32[768,768]{1,0:T(8,128)} %get-tuple-element.102.refs_0_, ...), custom_call_target="tpu_custom_call" | custom-call | tf_op jit(solution)/shard_map/attn_bwd_sums4/pallas_call | solution.py:1140
  470.4 1.8 convert_element_type.38
  476.3 8.5 %attn_dw.3 = bf16[4,768,768]{2,1,0:T(8,128)(2,1)} custom-call(bf16[768,768]{1,0:T(8,128)(2,1)} %pad_maximum_fusion.x_ref.act_ref, bf16[768,2304]{1,0:T(8,128)(2,1)} %get-tuple-element.115.dqkv_ref, bf16[768,768]{1,0:T(8,128)(2,1)} %get-tuple-element.116.ctx_ref, bf16[768,768]{1,0:T(8,128)(2,1)} %get-tuple-element.117.low_ref), custom_call_target="tpu_custom_call" | custom-call | tf_op jit(solution)/shard_map/attn_dw/pallas_call | solution.py:1163
  486.4 117.4 %take_home.1 = (f32[2,24,2304]{2,1,0:T(8,128)}, f32[2,24,768]{2,1,0:T(8,128)}, f32[2,24,3072]{2,1,0:T(8,128)}, f32[2,4,24,768]{3,2,1,0:T(8,128)}, f32[2,12,768]{...) custom-call(bf16[2,2,4,24,768]{4,3,2,1,0:T(8,128)(2,1)} %get-tuple-element.111.refs_0_, ...), custom_call_target="tpu_custom_call" | custom-call | tf_op jit(solution)/shard_map/take_home/pallas_call | solution.py:696
  603.9 4.0 gather_fusion.6
  608.0 2.1 gather_fusion.5
  611.5 5.1 broadcast_select_fusion
  (179 shorter events, 42.0 us)
Async XLA Ops:
  4.5 4.0 copy-start.32
  4.5 4.0 copy-start.33
  4.5 4.0 copy-start.34
  4.5 4.0 copy-start.35
  4.5 4.3 copy-start.11
  4.5 4.3 copy-start.12
  9.5 4.4 copy-start.14
  13.9 171.2 %copy-start.3 = (bf16[2,16,48,768]{3,2,1,0:T(8,128)(2,1)S(1)}, bf16[2,16,48,768]{3,2,1,0:T(8,128)(2,1)}, u32[]{:S(2)}) copy-start(bf16[2,16,48,768]{3,2,1,0:T(8,128)(2,1)} %get-tuple-element.176) | copy-start | bytes 7077892
  186.7 4.2 copy-start.38
  186.7 8.6 %copy-start.7 = (bf16[2,2,2,4,2,8,768]{6,5,4,3,2,1,0:T(8,128)(2,1)S(1)}, bf16[2,2,2,4,2,8,768]{6,5,4,3,2,1,0:T(8,128)(2,1)}, u32[]{:S(2)}) copy-start(bf16[2,2,2,4,2,8,768]{6,5,4,3,2,1,0:T(8,128)(2,1)} %get-tuple-element.77) | copy-start | bytes 2359300
  186.7 106.9 %all-to-all-start = ((bf16[2,8,2,48,768]{4,3,2,0,1:T(8,128)(2,1)}), bf16[2,8,2,48,768]{4,3,2,0,1:T(8,128)(2,1)S(1)}, u32[]{:S(2)}, u32[]{:S(2)}) async-start(bf16[2,8,2,48,768]{4,3,2,0,1:T(8,128)(2,1)} %copy.126), calls=%async_computation | async-start | bytes 4718592 | tf_op jit(solution)/shard_map/all_to_all | solution.py:1287
  190.7 11.7 %copy-start.15 = (s32[2,64,6,3]{1,0,3,2:T(2,128)S(1)}, s32[2,64,6,3]{1,0,3,2:T(2,128)}, u32[]{:S(2)}) copy-start(s32[2,64,6,3]{1,0,3,2:T(2,128)} %param.26) | copy-start | bytes 27652
  209.6 88.3 %copy-start.18 = (pred[384]{0:T(512)(128)(4,1)}, pred[384]{0:T(512)(128)(4,1)S(1)}, u32[]{:S(2)}) copy-start(pred[384]{0:T(512)(128)(4,1)S(1)} %iota_compare_fusion.4) | copy-start | bytes 1156
  210.3 99.3 %copy-start.20 = (pred[384]{0:T(512)(128)(4,1)}, pred[384]{0:T(512)(128)(4,1)S(1)}, u32[]{:S(2)}) copy-start(pred[384]{0:T(512)(128)(4,1)S(1)} %iota_compare_fusion.2) | copy-start | bytes 1156
  211.6 85.4 %copy-start.24 = (pred[384]{0:T(512)(128)(4,1)}, pred[384]{0:T(512)(128)(4,1)S(1)}, u32[]{:S(2)}) copy-start(pred[384]{0:T(512)(128)(4,1)S(1)} %iota_compare_fusion.3) | copy-start | bytes 1156
  212.3 85.7 %copy-start.22 = (pred[384]{0:T(512)(128)(4,1)}, pred[384]{0:T(512)(128)(4,1)S(1)}, u32[]{:S(2)}) copy-start(pred[384]{0:T(512)(128)(4,1)S(1)} %iota_compare_fusion.1) | copy-start | bytes 1156
  275.3 17.5 %copy-start.39 = (pred[768]{0:T(1024)(128)(4,1)S(1)}, pred[768]{0:T(1024)(128)(4,1)}, u32[]{:S(2)}) copy-start(pred[768]{0:T(1024)(128)(4,1)} %constant.106.clone.1) | copy-start | bytes 2308
  292.9 4.0 copy-start.36
  302.8 85.7 %all-to-all-start.1 = ((bf16[2,1,2,384,768]{4,2,0,1,3:T(2,128)(2,1)}), bf16[2,1,2,384,768]{4,2,0,1,3:T(2,128)(2,1)}, u32[]{:S(2)}, u32[]{:S(2)}) async-start(bf16[2,1,2,384,768]{4,2,0,1,3:T(2,128)(2,1)} %copy.141), calls=%async_computation.1 | async-start | bytes 4718592 | tf_op jit(solution)/shard_map/all_to_all | solution.py:1323
  603.9 4.1 copy-start.2
  603.9 4.1 copy-start.6
  611.5 6.8 %copy-start.10 = (f32[2,24,2304]{2,1,0:T(8,128)S(1)}, f32[2,24,2304]{2,1,0:T(8,128)}, u32[]{:S(2)}) copy-start(f32[2,24,2304]{2,1,0:T(8,128)} %get-tuple-element.224) | copy-start | bytes 1327108
  611.5 7.6 %copy-start.13 = (f32[2,24,768]{2,1,0:T(8,128)S(1)}, f32[2,24,768]{2,1,0:T(8,128)}, u32[]{:S(2)}) copy-start(f32[2,24,768]{2,1,0:T(8,128)} %get-tuple-element.227) | copy-start | bytes 442372
  611.5 8.3 %copy-start.9 = (f32[2,24,3072]{2,1,0:T(8,128)S(1)}, f32[2,24,3072]{2,1,0:T(8,128)}, u32[]{:S(2)}) copy-start(f32[2,24,3072]{2,1,0:T(8,128)} %get-tuple-element.231) | copy-start | bytes 1769476
  (18 other events, 45.6 us)
